TPU v7x, 512 devices: a whole 4x4x16 slice. The times are simulated.
512 devices in a mesh: blk: 32 (over z, core), shard: 16 (over x, y).
Axes of the slice: x: 4, y: 4, z: 16, core: 2. Of those that a mesh axis runs over, the one named last changes fastest.
Arguments:
- seed_field: float32 [32, 2, 32, 32, 1024], P('blk', None, 'shard'), may hold values from -5 to 5
- segment_order: int32 [32], P('blk'), may hold values from 0 to 31, each once
- seg_disp: float32 [32], replicated, may hold values from -1 to 1
- seg_kerr: float32 [32], replicated, may hold values from 0.5 to 2
- seg_gain: float32 [32], replicated, may hold values from 1 to 4
- seg_sat: float32 [32], replicated, may hold values from 1 to 4
Outputs:
- out_field: float32 [32, 2, 32, 32, 1024], P('blk', None, 'shard')
Inputs may be any that keep to these rules, and one draw needn't show every extreme that they name: segment_order[b] is the kind of the segment at cycle position b; each of the 32 kinds appears once.
All inputs are finite; a program needn't handle non-finite values.
Results may differ from a plain program's by a relative error of at most 0.0006.
Values sent between devices are 32-bit elements; how exact they have to be, the bound alone decides.
No kernel may reach another device: no remote copies, remote signals or barrier semaphores. Data moves between devices by JAX's collectives and lax.ppermute only.
A program may use at most 64 MiB of HBM per device.

v0:
```python
import math

import jax
import jax.numpy as jnp
from jax import lax
from jax.sharding import PartitionSpec as P

KRYLOV = 8


epsilon = 1e-06
step_length = 2.5
grin_depth = 1.5
squarings = 8
taylor_terms = 10
gain_width = 0.25
loss_rate = 0.5
disp_scale = 60.0
raman_share = 0.18
raman_freq = 0.05
raman_damp = 0.035


def shifted(block, axis, distance):
    devices = range(lax.axis_size(axis))
    route = [((i - distance) % len(devices), i) for i in devices]
    return lax.ppermute(block, axis, route)


def potential_table(x_count, x_total, y_count):
    x_cells = jnp.arange(x_count, dtype=jnp.int32).astype(jnp.float32)
    y_cells = jnp.arange(y_count, dtype=jnp.int32).astype(jnp.float32)
    x_norm = (x_cells - (x_total - 1) / 2.0) / (x_total / 2.0)
    y_norm = (y_cells - (y_count - 1) / 2.0) / (y_count / 2.0)
    return grin_depth * (x_norm[:, None] * x_norm[:, None] + y_norm[None, :] * y_norm[None, :])


def krylov_exp(diagonals, couplings):
    basis_count = len(diagonals)
    coupled = jnp.stack(couplings)
    tridiag = jnp.diag(jnp.stack(diagonals)) + jnp.diag(coupled, 1) + jnp.diag(coupled, -1)
    scaled = tridiag * (step_length / 2.0**squarings)
    zero_block = jnp.zeros_like(scaled)
    generator = jnp.concatenate(
        [
            jnp.concatenate([zero_block, -scaled], axis=1),
            jnp.concatenate([scaled, zero_block], axis=1),
        ],
        axis=0,
    )
    unit_matrix = jnp.eye(2 * basis_count, dtype=jnp.float32)
    power_term = unit_matrix
    running = unit_matrix
    for order_k in range(1, taylor_terms + 1):
        power_term = jnp.dot(power_term, generator, precision=lax.Precision.HIGHEST) / order_k
        running = running + power_term
    for repeat in range(squarings):
        running = jnp.dot(running, running, precision=lax.Precision.HIGHEST)
    return (running[:basis_count, 0], running[basis_count:, 0])


def assemble(vectors, real_coef, imag_coef):
    real_part = real_coef[0] * vectors[0][0] - imag_coef[0] * vectors[0][1]
    imag_part = real_coef[0] * vectors[0][1] + imag_coef[0] * vectors[0][0]
    for position in range(1, len(vectors)):
        real_part = (
            real_part
            + real_coef[position] * vectors[position][0]
            - imag_coef[position] * vectors[position][1]
        )
        imag_part = (
            imag_part
            + real_coef[position] * vectors[position][1]
            + imag_coef[position] * vectors[position][0]
        )
    return jnp.stack([real_part, imag_part])


def frequency_tables(freq_index, n_time, gain_now, dispersion):
    signed = jnp.where(freq_index >= n_time // 2, freq_index - n_time, freq_index)
    freq_norm = signed.astype(jnp.float32) / (n_time / 2.0)
    relative = freq_norm / gain_width
    amplitude = jnp.exp(0.5 * gain_now / (1.0 + relative * relative) - loss_rate)
    angle_k = disp_scale * dispersion * freq_norm * freq_norm
    resonance = raman_freq * raman_freq
    real_den = resonance - freq_norm * freq_norm
    imag_den = raman_damp * freq_norm
    magnitude = real_den * real_den + imag_den * imag_den
    return (
        amplitude * jnp.cos(angle_k),
        amplitude * jnp.sin(angle_k),
        resonance * real_den / magnitude,
        resonance * imag_den / magnitude,
    )


def field_sum(value):
    return lax.psum(value, "shard")


def pass_on(values):
    return shifted(values, "blk", 1)


def lanczos(incoming, energy, operate):
    scale_zero = jnp.sqrt(energy + epsilon)
    vectors = [incoming / scale_zero]
    diagonals = []
    couplings = []
    for lanczos_step in range(KRYLOV):
        current = vectors[lanczos_step]
        image = operate(current)
        if lanczos_step > 0:
            image = image - couplings[lanczos_step - 1] * vectors[lanczos_step - 1]
        if lanczos_step + 1 < KRYLOV:
            diagonal_now = field_sum(jnp.sum(current * image))
            image = image - diagonal_now * current
            coupling = jnp.sqrt(field_sum(jnp.sum(image * image)) + epsilon)
            couplings.append(coupling)
            vectors.append(image / coupling)
        else:
            diagonal_now = field_sum(jnp.sum(current * image))
        diagonals.append(diagonal_now)
    real_coef, imag_coef = krylov_exp(diagonals, couplings)
    return scale_zero * assemble(vectors, real_coef, imag_coef)


def circle(length):
    positions = jnp.arange(length, dtype=jnp.int32)
    angle_t = (positions[:, None] * positions[None, :] % length).astype(jnp.float32) * (
        2.0 * math.pi / length
    )
    return (jnp.cos(angle_t), jnp.sin(angle_t))


def twist(outer_len, inner_len, n_time):
    outer_idx = jnp.arange(outer_len, dtype=jnp.int32)[:, None]
    inner_idx = jnp.arange(inner_len, dtype=jnp.int32)[None, :]
    angle_t = (outer_idx * inner_idx % n_time).astype(jnp.float32) * (2.0 * math.pi / n_time)
    return (jnp.cos(angle_t), jnp.sin(angle_t))


def contract(pattern, values, table):
    return jnp.einsum(pattern, values, table, precision=lax.Precision.HIGHEST)


def spin(real_in, imag_in, cosine_table, sine_table, pattern, orientation):
    first_term = contract(pattern, real_in, cosine_table)
    cross_term = orientation * contract(pattern, real_in, sine_table)
    if imag_in is None:
        return (first_term, cross_term)
    return (
        first_term - orientation * contract(pattern, imag_in, sine_table),
        cross_term + contract(pattern, imag_in, cosine_table),
    )


def rotate(real_in, imag_in, cosine_r, sine_r):
    return (real_in * cosine_r - imag_in * sine_r, real_in * sine_r + imag_in * cosine_r)


def transform(real_in, imag_in):
    row_count = real_in.shape[0]
    n_time = real_in.shape[1]
    outer_len = n_time // 128
    inner_len = 128
    cos_outer, sin_outer = circle(outer_len)
    cos_inner, sin_inner = circle(inner_len)
    cos_twist, sin_twist = twist(outer_len, inner_len, n_time)
    real_blocks = real_in.reshape(row_count, outer_len, inner_len)
    imag_blocks = None if imag_in is None else imag_in.reshape(row_count, outer_len, inner_len)
    section_real, section_imag = spin(
        real_blocks, imag_blocks, cos_outer, sin_outer, "pab,ak->pkb", -1.0
    )
    section_real, section_imag = rotate(section_real, section_imag, cos_twist, -sin_twist)
    return spin(section_real, section_imag, cos_inner, sin_inner, "pkb,bm->pkm", -1.0)


def untransform(spec_real, spec_imag, real_only):
    row_count, outer_len, inner_len = spec_real.shape
    n_time = outer_len * inner_len
    cos_outer, sin_outer = circle(outer_len)
    cos_inner, sin_inner = circle(inner_len)
    cos_twist, sin_twist = twist(outer_len, inner_len, n_time)
    section_real, section_imag = spin(
        spec_real, spec_imag, cos_inner, sin_inner, "pkm,mb->pkb", 1.0
    )
    section_real, section_imag = rotate(section_real, section_imag, cos_twist, sin_twist)
    if real_only:
        time_real = contract("pkb,ka->pab", section_real, cos_outer) - contract(
            "pkb,ka->pab", section_imag, sin_outer
        )
        return time_real.reshape(row_count, n_time) / n_time
    time_real, time_imag = spin(
        section_real, section_imag, cos_outer, sin_outer, "pkb,ka->pab", 1.0
    )
    return (
        time_real.reshape(row_count, n_time) / n_time,
        time_imag.reshape(row_count, n_time) / n_time,
    )


def finish(columns, gain_now, dispersion, kerr_coef):
    shape_cols = columns.shape
    n_time = shape_cols[3]
    outer_len = n_time // 128
    real_in = columns[0].reshape(-1, n_time)
    imag_in = columns[1].reshape(-1, n_time)
    spec_real, spec_imag = transform(real_in, imag_in)
    freq_index = (
        jnp.arange(outer_len, dtype=jnp.int32)[:, None]
        + outer_len * jnp.arange(128, dtype=jnp.int32)[None, :]
    )
    gain_real, gain_imag, raman_real, raman_imag = frequency_tables(
        freq_index, n_time, gain_now, dispersion
    )
    spec_real, spec_imag = rotate(spec_real, spec_imag, gain_real, gain_imag)
    disp_real, disp_imag = untransform(spec_real, spec_imag, False)
    intensity = disp_real * disp_real + disp_imag * disp_imag
    ram_real, ram_imag = transform(intensity, None)
    ram_real, ram_imag = rotate(ram_real, ram_imag, raman_real, raman_imag)
    delayed = untransform(ram_real, ram_imag, True)
    rotation = kerr_coef * ((1.0 - raman_share) * intensity + raman_share * delayed)
    out_real, out_imag = rotate(disp_real, disp_imag, jnp.cos(rotation), jnp.sin(rotation))
    result = jnp.stack([out_real, out_imag]).reshape(shape_cols)
    return result


def per_device(seed_field, segment_order, seg_disp, seg_kerr, seg_gain, seg_sat):
    incoming = seed_field[0]
    rows_here = incoming.shape[1]
    width_y = incoming.shape[2]
    n_time = incoming.shape[3]
    total_x = rows_here * lax.axis_size("shard")
    energy = field_sum(jnp.sum(incoming * incoming))
    selected = jnp.arange(seg_disp.shape[0], dtype=jnp.int32) == segment_order[0]
    dispersion = jnp.sum(jnp.where(selected, seg_disp, 0.0))
    kerr_coef = jnp.sum(jnp.where(selected, seg_kerr, 0.0))
    gain_peak = jnp.sum(jnp.where(selected, seg_gain, 0.0))
    saturation = jnp.sum(jnp.where(selected, seg_sat, 0.0))
    gain_now = gain_peak / (1.0 + energy / (total_x * width_y * n_time) / saturation)
    regrouped = lax.all_to_all(incoming, "shard", split_axis=3, concat_axis=1, tiled=True)
    time_here = regrouped.shape[3]
    merged = regrouped.reshape(2, total_x, width_y * time_here)
    potential = jnp.repeat(potential_table(total_x, total_x, width_y), time_here, axis=1)

    def operate(vector):
        padded = jnp.pad(vector, ((0, 0), (1, 1), (time_here, time_here)))
        beside = padded[:, 2:, time_here:-time_here] + padded[:, :-2, time_here:-time_here]
        beside = beside + padded[:, 1:-1, 2 * time_here :] + padded[:, 1:-1, : -2 * time_here]
        return 0.5 * beside - potential * vector

    linear = lanczos(merged, energy, operate).reshape(2, total_x, width_y, time_here)
    result = finish(
        lax.all_to_all(linear, "shard", split_axis=1, concat_axis=3, tiled=True),
        gain_now,
        dispersion,
        kerr_coef,
    )
    result = pass_on(result)
    return result[None]


def solution(mesh):
    in_specs = (P("blk", None, "shard", None, None), P("blk"), P(), P(), P(), P())
    out_specs = P("blk", None, "shard", None, None)
    return jax.shard_map(
        per_device, mesh=mesh, in_specs=in_specs, out_specs=out_specs, check_vma=False
    )
```

profile of v0, /device:TPU:8, one launch (start us, length us, event | category | flops | bytes accessed | tf_op | source)
XLA Modules:
  0.0 749.3 jit_solution(11067476767364682421)
XLA Ops:
  0.0 2.8 copy.10
  2.8 2.1 bitcast_bitcast_fusion
  4.9 4.3 reshape.336
  9.2 9.2 %all-to-all-start = ((f32[16,1,8192]{2,1,0:T(1,128)}), f32[16,1,8192]{2,1,0:T(1,128)S(1)}, u32[]{:S(2)}, u32[]{:S(2)}) async-start(f32[16,1,8192]{2,1,0:T(1,128)} %reshape.336), calls=%async_computation | async-start | bytes 1048576 | tf_op jit(solution)/shard_map/all_to_all | solution.py:242
  18.4 2.7 multiply_reduce_fusion
  21.1 37.0 %psum.112 = f32[]{:T(128)} all-reduce(f32[]{:T(128)} %multiply_reduce_fusion), channel_id=1, replica_groups=mesh['blk'=32,'shard'=16] {'shard'}, use_global_device_ids=true, to_apply=%region_1.0 | all-reduce | flops 1 | bytes 8 | tf_op jit(solution)/shard_map/psum | solution.py:98
  59.7 1.9 reduce
  61.6 1.8 reshape.337
  63.4 2.1 broadcast_divide_fusion
  65.4 2.7 copy.11
  68.5 0.9 multiply_reduce_fusion.14
  69.4 40.6 %psum.113 = f32[]{:T(128)} all-reduce(f32[]{:T(128)} %get-tuple-element.19), channel_id=1, replica_groups=mesh['blk'=32,'shard'=16] {'shard'}, use_global_device_ids=true, to_apply=%region_3.4 | all-reduce | flops 1 | bytes 8 | tf_op jit(solution)/shard_map/psum | solution.py:98
  110.0 1.3 multiply_reduce_fusion.13
  112.0 36.1 %psum.114 = f32[]{:T(128)} all-reduce(f32[]{:T(128)} %multiply_reduce_fusion.13), channel_id=1, replica_groups=mesh['blk'=32,'shard'=16] {'shard'}, use_global_device_ids=true, to_apply=%region_5.6 | all-reduce | flops 1 | bytes 8 | tf_op jit(solution)/shard_map/psum | solution.py:98
  149.6 0.9 multiply_reduce_fusion.12
  150.5 38.1 %psum.115 = f32[]{:T(128)} all-reduce(f32[]{:T(128)} %get-tuple-element.17), channel_id=1, replica_groups=mesh['blk'=32,'shard'=16] {'shard'}, use_global_device_ids=true, to_apply=%region_7.8 | all-reduce | flops 1 | bytes 8 | tf_op jit(solution)/shard_map/psum | solution.py:98
  188.6 1.4 multiply_reduce_fusion.11
  190.6 36.6 %psum.116 = f32[]{:T(128)} all-reduce(f32[]{:T(128)} %multiply_reduce_fusion.11), channel_id=1, replica_groups=mesh['blk'=32,'shard'=16] {'shard'}, use_global_device_ids=true, to_apply=%region_9.10 | all-reduce | flops 1 | bytes 8 | tf_op jit(solution)/shard_map/psum | solution.py:98
  227.9 0.7 broadcast_divide_fusion.6
  228.6 0.9 multiply_reduce_fusion.10
  229.6 38.1 %psum.117 = f32[]{:T(128)} all-reduce(f32[]{:T(128)} %get-tuple-element.15), channel_id=1, replica_groups=mesh['blk'=32,'shard'=16] {'shard'}, use_global_device_ids=true, to_apply=%region_11.12 | all-reduce | flops 1 | bytes 8 | tf_op jit(solution)/shard_map/psum | solution.py:98
  267.6 1.4 multiply_reduce_fusion.9
  269.6 36.1 %psum.118 = f32[]{:T(128)} all-reduce(f32[]{:T(128)} %multiply_reduce_fusion.9), channel_id=1, replica_groups=mesh['blk'=32,'shard'=16] {'shard'}, use_global_device_ids=true, to_apply=%region_13.14 | all-reduce | flops 1 | bytes 8 | tf_op jit(solution)/shard_map/psum | solution.py:98
  306.4 0.7 broadcast_divide_fusion.5
  307.1 0.9 multiply_reduce_fusion.8
  308.1 38.1 %psum.119 = f32[]{:T(128)} all-reduce(f32[]{:T(128)} %get-tuple-element.13), channel_id=1, replica_groups=mesh['blk'=32,'shard'=16] {'shard'}, use_global_device_ids=true, to_apply=%region_15.16 | all-reduce | flops 1 | bytes 8 | tf_op jit(solution)/shard_map/psum | solution.py:98
  346.1 1.4 multiply_reduce_fusion.7
  348.2 36.2 %psum.120 = f32[]{:T(128)} all-reduce(f32[]{:T(128)} %multiply_reduce_fusion.7), channel_id=1, replica_groups=mesh['blk'=32,'shard'=16] {'shard'}, use_global_device_ids=true, to_apply=%region_17.18 | all-reduce | flops 1 | bytes 8 | tf_op jit(solution)/shard_map/psum | solution.py:98
  385.0 0.7 broadcast_divide_fusion.4
  385.7 0.9 multiply_reduce_fusion.6
  386.7 38.1 %psum.121 = f32[]{:T(128)} all-reduce(f32[]{:T(128)} %get-tuple-element.11), channel_id=1, replica_groups=mesh['blk'=32,'shard'=16] {'shard'}, use_global_device_ids=true, to_apply=%region_19.20 | all-reduce | flops 1 | bytes 8 | tf_op jit(solution)/shard_map/psum | solution.py:98
  424.7 1.4 multiply_reduce_fusion.5
  426.2 36.2 %psum.122 = f32[]{:T(128)} all-reduce(f32[]{:T(128)} %multiply_reduce_fusion.5), channel_id=1, replica_groups=mesh['blk'=32,'shard'=16] {'shard'}, use_global_device_ids=true, to_apply=%region_21.22 | all-reduce | flops 1 | bytes 8 | tf_op jit(solution)/shard_map/psum | solution.py:98
  463.1 0.8 broadcast_divide_fusion.3
  463.9 0.9 multiply_reduce_fusion.4
  464.8 38.0 %psum.123 = f32[]{:T(128)} all-reduce(f32[]{:T(128)} %get-tuple-element.9), channel_id=1, replica_groups=mesh['blk'=32,'shard'=16] {'shard'}, use_global_device_ids=true, to_apply=%region_23.24 | all-reduce | flops 1 | bytes 8 | tf_op jit(solution)/shard_map/psum | solution.py:98
  502.8 1.4 multiply_reduce_fusion.3
  504.2 36.1 %psum.124 = f32[]{:T(128)} all-reduce(f32[]{:T(128)} %multiply_reduce_fusion.3), channel_id=1, replica_groups=mesh['blk'=32,'shard'=16] {'shard'}, use_global_device_ids=true, to_apply=%region_25.26 | all-reduce | flops 1 | bytes 8 | tf_op jit(solution)/shard_map/psum | solution.py:98
  541.0 1.7 broadcast_divide_fusion.2
  542.8 1.8 multiply_reduce_fusion.2
  544.5 37.9 %psum.125 = f32[]{:T(128)} all-reduce(f32[]{:T(128)} %get-tuple-element.7), channel_id=1, replica_groups=mesh['blk'=32,'shard'=16] {'shard'}, use_global_device_ids=true, to_apply=%region_27.28 | all-reduce | flops 1 | bytes 8 | tf_op jit(solution)/shard_map/psum | solution.py:98
  582.5 2.3 multiply_reduce_fusion.1
  584.8 36.3 %psum.126 = f32[]{:T(128)} all-reduce(f32[]{:T(128)} %multiply_reduce_fusion.1), channel_id=1, replica_groups=mesh['blk'=32,'shard'=16] {'shard'}, use_global_device_ids=true, to_apply=%region_29.30 | all-reduce | flops 1 | bytes 8 | tf_op jit(solution)/shard_map/psum | solution.py:98
  621.8 1.7 broadcast_divide_fusion.1
  623.5 1.0 fusion.56
  624.5 37.8 %psum.127 = f32[1]{0:T(128)} all-reduce(f32[1]{0:T(128)} %bitcast.11), channel_id=1, replica_groups=mesh['blk'=32,'shard'=16] {'shard'}, use_global_device_ids=true, to_apply=%region_31.32 | all-reduce | flops 1 | bytes 8 | tf_op jit(solution)/shard_map/psum | solution.py:98
  662.4 5.1 stack.73
  671.5 3.6 multiply_subtract_fusion
  675.1 1.2 sub.238
  676.3 10.8 %multiply_subtract_fusion.14 = f32[1,32,2048]{2,1,0:T(8,128)} fusion(f32[1,32,2048]{2,1,0:T(8,128)S(1)} %sub.238, f32[2,32,2048]{2,1,0:T(8,128)} %copy-done.1, f32[2,32,2048]{2,1,0:T(8,128)S(1)} %broadcast_divide_fusion.2, f32[2,32,2048]{2,1,0:T(8,128)S(1)} %broadcast_divide_fusion.3, f32[2,32,2048]{2,1,0:T(8,128)S(1)} %broadcast_divide_fusion.4, ...), kind=kLoop, calls=%fused_computation.177 | loop fusion | flops 1835008 | bytes 4194360 | tf_op jit(solution)/shard_map/sub | solution.py:67
  687.1 1.9 stack.82
  689.0 1.2 add.744
  690.3 10.8 %multiply_add_fusion.8 = f32[1,32,2048]{2,1,0:T(8,128)} fusion(f32[1,32,2048]{2,1,0:T(8,128)S(1)} %add.744, f32[2,32,2048]{2,1,0:T(8,128)} %copy-done.1, f32[2,32,2048]{2,1,0:T(8,128)S(1)} %broadcast_divide_fusion.2, f32[2,32,2048]{2,1,0:T(8,128)S(1)} %broadcast_divide_fusion.3, f32[2,32,2048]{2,1,0:T(8,128)S(1)} %broadcast_divide_fusion.4, ...), kind=kLoop, calls=%fused_computation.176 | loop fusion | flops 1835008 | bytes 4194360 | tf_op jit(solution)/shard_map/add | solution.py:72
  701.1 1.1 stack.83
  702.2 1.2 fusion.297
  703.4 1.4 reshape.338
  704.9 3.8 all-to-all-start.1
  711.2 6.1 all-to-all-done.1
  717.3 1.9 reduce.1
  730.5 0.8 convolution_multiply_fusion
  736.0 1.5 fusion.286
  737.5 0.9 multiply_subtract_fusion.8
  738.5 9.8 %collective-permute-done = f32[2,2,32,1024]{3,2,1,0:T(8,128)S(1)} collective-permute-done((f32[2,2,32,1024]{3,2,1,0:T(8,128)S(1)}, f32[2,2,32,1024]{3,2,1,0:T(8,128)S(1)}, u32[]{:S(2)}, u32[]{:S(2)}) %collective-permute-start) | collective-permute-done | bytes 524320 | tf_op jit(solution)/shard_map/ppermute | solution.py:27
  748.3 0.8 copy.19
  (93 shorter events, 24.0 us)
Async XLA Ops:
  9.2 50.0 %all-to-all-start = ((f32[16,1,8192]{2,1,0:T(1,128)}), f32[16,1,8192]{2,1,0:T(1,128)S(1)}, u32[]{:S(2)}, u32[]{:S(2)}) async-start(f32[16,1,8192]{2,1,0:T(1,128)} %reshape.336), calls=%async_computation | async-start | bytes 1048576 | tf_op jit(solution)/shard_map/all_to_all | solution.py:242
  68.1 81.4 %copy-start = (f32[2,2,32,16,64]{4,2,1,3,0:T(8,128)}, f32[2,2,32,16,64]{4,2,1,3,0:T(8,128)S(1)}, u32[]{:S(2)}) copy-start(f32[2,2,32,16,64]{4,2,1,3,0:T(8,128)S(1)} %copy.11) | copy-start | bytes 1572868
  148.9 41.1 %copy-start.3 = (f32[32]{0:T(128)S(1)}, f32[32]{0:T(128)}, u32[]{:S(2)}) copy-start(f32[32]{0:T(128)} %param.9) | copy-start | bytes 388
  148.9 41.1 %copy-start.4 = (f32[32]{0:T(128)S(1)}, f32[32]{0:T(128)}, u32[]{:S(2)}) copy-start(f32[32]{0:T(128)} %param.8) | copy-start | bytes 388
  227.9 41.1 %copy-start.5 = (f32[32]{0:T(128)S(1)}, f32[32]{0:T(128)}, u32[]{:S(2)}) copy-start(f32[32]{0:T(128)} %param.11) | copy-start | bytes 388
  306.4 41.1 %copy-start.6 = (f32[32]{0:T(128)S(1)}, f32[32]{0:T(128)}, u32[]{:S(2)}) copy-start(f32[32]{0:T(128)} %param.10) | copy-start | bytes 388
  464.8 76.2 %copy-start.2 = (f32[2,32,2048]{2,1,0:T(8,128)}, f32[2,32,2048]{2,1,0:T(8,128)S(1)}, u32[]{:S(2)}) copy-start(f32[2,32,2048]{2,1,0:T(8,128)S(1)} %get-tuple-element.10) | copy-start | bytes 1572868
  623.5 1.0 copy-start.1
  704.9 12.5 %all-to-all-start.1 = ((f32[16,1,8192]{2,1,0:T(1,128)}), f32[16,1,8192]{2,1,0:T(1,128)S(1)}, u32[]{:S(2)}, u32[]{:S(2)}) async-start(f32[16,1,8192]{2,1,0:T(1,128)} %reshape.338), calls=%async_computation.1 | async-start | bytes 1048576 | tf_op jit(solution)/shard_map/all_to_all | solution.py:255
  738.5 9.8 %collective-permute-start = (f32[2,2,32,1024]{3,2,1,0:T(8,128)S(1)}, f32[2,2,32,1024]{3,2,1,0:T(8,128)S(1)}, u32[]{:S(2)}, u32[]{:S(2)}) collective-permute-start(f32[2,2,32,1024]{3,2,1,0:T(8,128)S(1)} %pad_maximum_fusion), channel_id=1, source_target_pairs={{496,0},{0,16},{16,32},{32,48},{48,64},{64,80},{80,96},{96,112},{1... | collective-permute-start | bytes 1572872 | tf_op jit(solution)/shard_map/ppermute | solution.py:27
where the time goes:
time: 759 us; the launch traced here: 749 us
  blocking collectives  597 us (79%)
  other arithmetic  65.5 us (9%)
  local copies, waits for them, and re-layouts  30.2 us (4%)
  matrix products  18.1 us (2%)
  waiting for transfers between devices  15.9 us (2%)
  starting transfers between devices  13 us (2%)
  between operations  9.26 us (1%)
    psum x16, blocking collectives, field_sum(): return lax.psum(value, 'shard')  597 us
  transfers between devices with their start and end apart: 3, of which 2 were waited for; matrix products, arithmetic and copies ran while one was open for 0% of the time, Pallas kernels for 0%

commit v1 on v0

v1 whole, which is shorter than its diff:
```python
import functools

import jax
import jax.numpy as jnp
import numpy as np
from jax import lax
from jax.experimental import pallas as pl
from jax.experimental.pallas import tpu as pltpu
from jax.sharding import PartitionSpec as P

KRYLOV = 8
NS = 16
NG = 32
NT = 1024
NK = 8
NB = 128

epsilon = 1e-06
step_length = 2.5
grin_depth = 1.5
squarings = 8
taylor_terms = 10
gain_width = 0.25
loss_rate = 0.5
disp_scale = 60.0
raman_share = 0.18
raman_freq = 0.05
raman_damp = 0.035

F32 = jnp.float32
HIGHEST = lax.Precision.HIGHEST


@functools.cache
def tables():
    cell = (np.arange(NG) - (NG - 1) / 2.0) / (NG / 2.0)
    line = np.diag(-grin_depth * cell * cell)
    line = line + 0.5 * (np.eye(NG, k=1) + np.eye(NG, k=-1))
    values, q = np.linalg.eigh(line)

    to_ymode = np.zeros((NS, 2, 2, 2, 2, 2, NG))
    to_xmode = np.zeros((2, 2, NG, NS, 2, 2, 2))
    for part in range(2):
        for side in range(2):
            for jj in range(2):
                to_ymode[:, part, jj, side, part, side, :] = q[:, jj::2].T
                to_xmode[part, jj, :, :, part, jj, side] = q[side::2, :].T
    to_ymode = to_ymode.reshape(128, 128)
    to_xmode = to_xmode.reshape(128, 128)

    pair = values.reshape(NS, 2)
    lam = pair[:, None, :, None] + values[None, None, None, :] + np.zeros((1, 2, 1, 1))
    lam_all = lam.reshape(NS, 128)
    lam_own = np.broadcast_to(lam_all[:, :64, None], (NS, 64, 128))

    inner = np.arange(NB)
    angle = 2.0 * np.pi * ((inner[:, None] * inner[None, :]) % NB) / NB
    c, s = np.cos(angle), np.sin(angle)
    forward = np.block([[c, -s], [s, c]])
    backward = np.block([[c, s], [-s, c]])
    turn = 2.0 * np.pi * (np.arange(NK)[:, None] * inner[None, :]) / NT
    tw_cos, tw_sin = np.cos(turn), np.sin(turn)

    freq = np.arange(NK)[:, None] + NK * inner[None, :]
    signed = np.where(freq >= NT // 2, freq - NT, freq)
    w = signed / (NT / 2.0)
    resonance = raman_freq * raman_freq
    raman = resonance / (resonance - w * w - 1j * raman_damp * w)
    ram_re = raman.real / NT
    ram_im = np.where(signed == -(NT // 2), 0.0, raman.imag) / NT

    f32 = lambda a: np.ascontiguousarray(a, dtype=np.float32)
    return dict(
        to_ymode=f32(to_ymode),
        from_ymode=f32(to_ymode.T),
        to_xmode=f32(to_xmode),
        from_xmode=f32(to_xmode.T),
        lam_all=f32(lam_all),
        lam_own=f32(lam_own),
        forward=f32(forward),
        backward=f32(backward),
        twiddle=f32(np.stack([tw_cos, tw_sin])),
        w=f32(w),
        raman=f32(np.stack([ram_re, ram_im])),
    )


def mm(a, b):
    return jnp.dot(a, b, precision=HIGHEST, preferred_element_type=F32)


def fourier8(re, im, sign):
    def four(r, i):
        pr, pi = r[0] + r[2], i[0] + i[2]
        mr, mi = r[0] - r[2], i[0] - i[2]
        qr, qi = r[1] + r[3], i[1] + i[3]
        nr, ni = r[1] - r[3], i[1] - i[3]
        tr, ti = (-ni, nr) if sign > 0 else (ni, -nr)
        return (
            [pr + qr, mr + tr, pr - qr, mr - tr],
            [pi + qi, mi + ti, pi - qi, mi - ti],
        )

    er, ei = four(re[0::2], im[0::2])
    orr, oi = four(re[1::2], im[1::2])
    h = np.float32(np.sqrt(0.5))
    if sign > 0:
        w1 = ((orr[1] - oi[1]) * h, (orr[1] + oi[1]) * h)
        w2 = (-oi[2], orr[2])
        w3 = (-(orr[3] + oi[3]) * h, (orr[3] - oi[3]) * h)
    else:
        w1 = ((orr[1] + oi[1]) * h, (oi[1] - orr[1]) * h)
        w2 = (oi[2], -orr[2])
        w3 = ((oi[3] - orr[3]) * h, -(orr[3] + oi[3]) * h)
    tr = [orr[0], w1[0], w2[0], w3[0]]
    ti = [oi[0], w1[1], w2[1], w3[1]]
    out_r = [er[k] + tr[k] for k in range(4)] + [er[k] - tr[k] for k in range(4)]
    out_i = [ei[k] + ti[k] for k in range(4)] + [ei[k] - ti[k] for k in range(4)]
    return out_r, out_i


def outer_forward(load, rows, tw_ref, dest):
    for r0 in range(0, rows, 8):
        re = [load(0, r0, a) for a in range(NK)]
        im = [load(1, r0, a) for a in range(NK)]
        re, im = fourier8(re, im, -1)
        for k in range(NK):
            if k:
                c, s = tw_ref[0, k : k + 1, :], tw_ref[1, k : k + 1, :]
                re[k], im[k] = re[k] * c + im[k] * s, im[k] * c - re[k] * s
            dest[k * rows + r0 : k * rows + r0 + 8, 0:NB] = re[k]
            dest[k * rows + r0 : k * rows + r0 + 8, NB : 2 * NB] = im[k]


def outer_backward(src, rows, tw_ref, store):
    for r0 in range(0, rows, 8):
        re, im = [], []
        for k in range(NK):
            a = src[k * rows + r0 : k * rows + r0 + 8, 0:NB]
            b = src[k * rows + r0 : k * rows + r0 + 8, NB : 2 * NB]
            if k:
                c, s = tw_ref[0, k : k + 1, :], tw_ref[1, k : k + 1, :]
                a, b = a * c - b * s, a * s + b * c
            re.append(a)
            im.append(b)
        re, im = fourier8(re, im, 1)
        for a in range(NK):
            store(r0, a, re[a], im[a])


def filter_spectrum(spec, rows, factor_re, factor_im):
    for k in range(NK):
        fr, fi = factor_re[k : k + 1, :], factor_im[k : k + 1, :]
        lo, hi = k * rows, (k + 1) * rows
        a, b = spec[lo:hi, 0:NB], spec[lo:hi, NB : 2 * NB]
        spec[lo:hi, 0:NB] = a * fr - b * fi
        spec[lo:hi, NB : 2 * NB] = a * fi + b * fr


def ymode_kernel(seed_ref, mat_ref, out_ref):
    total = jnp.zeros((8, 128), F32)
    for c in range(NK):
        block = seed_ref[:, c * 128 : (c + 1) * 128]
        square = block * block
        for r in range(16):
            total = total + square[8 * r : 8 * r + 8, :]
        modes = mm(mat_ref[...], block)
        out_ref[:, 8 * c : 8 * c + 8, :] = modes.reshape(NS, 8, 128)
    for d in range(NS):
        out_ref[d, 64:72, :] = total


def xmode_kernel(in_ref, mat_ref, modes_ref, weight_ref, energy_ref):
    square = jnp.zeros((128, 128), F32)
    for c in range(NK):
        block = in_ref[:, 8 * c : 8 * c + 8, :].reshape(128, 128)
        modes = mm(mat_ref[...], block)
        modes_ref[:, c * 128 : (c + 1) * 128] = modes
        square = square + modes * modes
    weight = lax.dot_general(
        jnp.ones((8, 128), F32),
        square,
        (((1,), (1,)), ((), ())),
        precision=HIGHEST,
        preferred_element_type=F32,
    )
    for d in range(NS):
        weight_ref[d] = weight
    total = in_ref[0, 64:72, :]
    for d in range(1, NS):
        total = total + in_ref[d, 64:72, :]
    energy_ref[...] = total


def whole_sum(value):
    return jnp.sum(jnp.sum(value, axis=0, keepdims=True), axis=1, keepdims=True)


def disperse_kernel(
    kind_ref, disp_ref, gain_ref, sat_ref, modes_ref, energy_ref, w_ref, tw_ref, fwd_ref, bwd_ref,
    out_ref, one, two
):
    kind = kind_ref[0]

    def load(part, r0, a):
        return modes_ref[64 * part + r0 : 64 * part + r0 + 8, a * NB : (a + 1) * NB]

    outer_forward(load, 64, tw_ref, one)
    two[...] = mm(one[...], fwd_ref[...])

    energy = whole_sum(energy_ref[...])
    gain = gain_ref[kind] / (1.0 + energy / (NG * NG * NT) / sat_ref[kind])
    w = w_ref[...]
    relative = w / gain_width
    amplitude = jnp.exp(0.5 * gain / (1.0 + relative * relative) - loss_rate) * (1.0 / NT)
    angle = disp_scale * disp_ref[kind] * w * w
    filter_spectrum(two, 64, amplitude * jnp.cos(angle), amplitude * jnp.sin(angle))

    one[...] = mm(two[...], bwd_ref[...])

    def store(r0, a, re, im):
        out_ref[r0 : r0 + 8, a * NB : (a + 1) * NB] = re
        out_ref[64 + r0 : 64 + r0 + 8, a * NB : (a + 1) * NB] = im

    outer_backward(one, 64, tw_ref, store)


def small_product(a, b):
    total = a[:, 0:1] * b[0:1, :]
    for k in range(1, KRYLOV):
        total = total + a[:, k : k + 1] * b[k : k + 1, :]
    return total


def krylov_exp(diagonals, couplings):
    row = lax.broadcasted_iota(jnp.int32, (8, 128), 0)
    lane = lax.broadcasted_iota(jnp.int32, (8, 128), 1)
    zero = jnp.zeros((8, 128), F32)
    scale = step_length / 2.0**squarings
    mid, low, high = zero, zero, zero
    for j in range(KRYLOV):
        mid = jnp.where(row == j, diagonals[j] * scale, mid)
        if j + 1 < KRYLOV:
            high = jnp.where(row == j, couplings[j] * scale, high)
            low = jnp.where(row == j + 1, couplings[j] * scale, low)
    term = jnp.where(row == lane, 1.0, 0.0).astype(F32)
    real, imag = term, zero
    for order in range(1, taylor_terms + 1):
        term = mid * term + low * pltpu.roll(term, 1, 0) + high * pltpu.roll(term, 7, 0)
        term = term * (1.0 / order)
        signed = -term if order % 4 in (2, 3) else term
        if order % 2:
            imag = imag + signed
        else:
            real = real + signed
    for _ in range(squarings):
        real, imag = (
            small_product(real, real) - small_product(imag, imag),
            2.0 * small_product(real, imag),
        )
    return real, imag


def propagate_kernel(
    shard_ref, weight_ref, lam_ref, own_ref, modes_ref, mat_ref, out_ref, scaled
):
    weight = weight_ref[:, 0, :]
    lam = lam_ref[...]
    own = own_ref[0]
    scale_zero = jnp.sqrt(whole_sum(weight) + epsilon)
    vector = jnp.sqrt(weight) / scale_zero
    poly = jnp.ones((64, 128), F32) / scale_zero
    before_vector, before_poly, coupling = None, None, None
    diagonals, couplings, polys = [], [], [poly]
    for step in range(KRYLOV):
        image = lam * vector
        if step:
            image = image - coupling * before_vector
        diagonal = whole_sum(vector * image)
        diagonals.append(diagonal)
        if step + 1 < KRYLOV:
            image = image - diagonal * vector
            grown = own * poly
            if step:
                grown = grown - coupling * before_poly
            grown = grown - diagonal * poly
            coupling = jnp.sqrt(whole_sum(image * image) + epsilon)
            couplings.append(coupling)
            before_vector, vector = vector, image / coupling
            before_poly, poly = poly, grown / coupling
            polys.append(poly)
    real, imag = krylov_exp(diagonals, couplings)
    gain_re = real[0:1, 0:1] * polys[0]
    gain_im = imag[0:1, 0:1] * polys[0]
    for j in range(1, KRYLOV):
        gain_re = gain_re + real[j : j + 1, 0:1] * polys[j]
        gain_im = gain_im + imag[j : j + 1, 0:1] * polys[j]
    gain_re = gain_re * scale_zero
    gain_im = gain_im * scale_zero
    for c in range(NK):
        a = modes_ref[0:64, c * 128 : (c + 1) * 128]
        b = modes_ref[64:128, c * 128 : (c + 1) * 128]
        scaled[0:64, :] = gain_re * a - gain_im * b
        scaled[64:128, :] = gain_im * a + gain_re * b
        back = mm(mat_ref[...], scaled[...])
        out_ref[:, :, c * 128 : (c + 1) * 128] = back.reshape(NS, 8, 128)


def kerr_kernel(
    kind_ref, kerr_ref, in_ref, mat_ref, tw_ref, fwd_ref, bwd_ref, raman_ref,
    out_ref, field, delayed, one, two
):
    kerr = kerr_ref[kind_ref[0]]
    field[...] = mm(mat_ref[...], in_ref[...].reshape(128, NT))

    def load(side, r0, a):
        lanes = slice(a * NB, (a + 1) * NB)
        re = field[32 * side + r0 : 32 * side + r0 + 8, lanes]
        im = field[64 + 32 * side + r0 : 64 + 32 * side + r0 + 8, lanes]
        return re * re + im * im

    outer_forward(load, 32, tw_ref, one)
    two[...] = mm(one[...], fwd_ref[...])
    filter_spectrum(two, 32, raman_ref[0], raman_ref[1])
    one[...] = mm(two[...], bwd_ref[...])

    def store(r0, a, re, im):
        lanes = slice(a * NB, (a + 1) * NB)
        delayed[r0 : r0 + 8, lanes] = re
        delayed[32 + r0 : 32 + r0 + 8, lanes] = im

    outer_backward(one, 32, tw_ref, store)

    for r0 in range(0, 64, 8):
        re, im = field[r0 : r0 + 8, :], field[64 + r0 : 64 + r0 + 8, :]
        late = delayed[r0 : r0 + 8, :]
        rotation = kerr * ((1.0 - raman_share) * (re * re + im * im) + raman_share * late)
        c, s = jnp.cos(rotation), jnp.sin(rotation)
        out_ref[r0 : r0 + 8, :] = re * c - im * s
        out_ref[64 + r0 : 64 + r0 + 8, :] = re * s + im * c


def sds(*shape):
    return jax.ShapeDtypeStruct(shape, F32)


SMEM = pl.BlockSpec(memory_space=pltpu.SMEM)
VMEM = pl.BlockSpec(memory_space=pltpu.VMEM)


def cost(flops, moved):
    return pl.CostEstimate(flops=flops, bytes_accessed=moved, transcendentals=0)


def exchange(value):
    return lax.all_to_all(value, "shard", split_axis=0, concat_axis=0, tiled=True)


def per_device(seed_field, segment_order, seg_disp, seg_kerr, seg_gain, seg_sat):
    t = tables()
    shard = lax.axis_index("shard").astype(jnp.int32).reshape(1)
    seed = seed_field.reshape(128, NT)

    ymodes = pl.pallas_call(
        ymode_kernel, out_shape=sds(NS, 72, 128), in_specs=[VMEM] * 2, out_specs=VMEM,
        name="ymode",
    )(seed, t["to_ymode"])
    gathered = exchange(ymodes)
    modes, weight, energy = pl.pallas_call(
        xmode_kernel,
        out_shape=(sds(128, NT), sds(NS, 8, 128), sds(8, 128)),
        in_specs=[VMEM] * 2,
        out_specs=(VMEM,) * 3,
        name="xmode",
    )(gathered, t["to_xmode"])
    weights = exchange(weight)
    modes = pl.pallas_call(
        disperse_kernel,
        out_shape=sds(128, NT),
        in_specs=[SMEM] * 4 + [VMEM] * 6,
        out_specs=VMEM,
        scratch_shapes=[pltpu.VMEM((512, 256), F32)] * 2,
        cost_estimate=cost(6 * 4 * 512 * 256 * 256, 2**20),
        name="disperse",
    )(
        segment_order, seg_disp, seg_gain, seg_sat, modes, energy, t["w"], t["twiddle"],
        t["forward"], t["backward"],
    )
    xback = pl.pallas_call(
        propagate_kernel,
        out_shape=sds(NS, 8, NT),
        grid_spec=pltpu.PrefetchScalarGridSpec(
            num_scalar_prefetch=1,
            grid=(1,),
            in_specs=[
                pl.BlockSpec((NS, 8, 128), lambda i, s: (0, 0, 0)),
                pl.BlockSpec((NS, 128), lambda i, s: (0, 0)),
                pl.BlockSpec((1, 64, 128), lambda i, s: (s[0], 0, 0)),
                pl.BlockSpec((128, NT), lambda i, s: (0, 0)),
                pl.BlockSpec((128, 128), lambda i, s: (0, 0)),
            ],
            out_specs=pl.BlockSpec((NS, 8, NT), lambda i, s: (0, 0, 0)),
            scratch_shapes=[pltpu.VMEM((128, 128), F32)],
        ),
        name="propagate",
    )(shard, weights, t["lam_all"], t["lam_own"], modes, t["from_xmode"])
    rows = exchange(xback)
    result = pl.pallas_call(
        kerr_kernel,
        out_shape=sds(128, NT),
        in_specs=[SMEM] * 2 + [VMEM] * 6,
        out_specs=VMEM,
        scratch_shapes=[pltpu.VMEM((128, NT), F32), pltpu.VMEM((64, NT), F32)]
        + [pltpu.VMEM((256, 256), F32)] * 2,
        name="kerr",
    )(
        segment_order, seg_kerr, rows, t["from_ymode"], t["twiddle"], t["forward"],
        t["backward"], t["raman"],
    )
    count = lax.axis_size("blk")
    result = lax.ppermute(result, "blk", [(b, (b + 1) % count) for b in range(count)])
    return result.reshape(seed_field.shape)


def solution(mesh):
    in_specs = (P("blk", None, "shard", None, None), P("blk"), P(), P(), P(), P())
    out_specs = P("blk", None, "shard", None, None)
    return jax.shard_map(
        per_device, mesh=mesh, in_specs=in_specs, out_specs=out_specs, check_vma=False
    )
```

time: 759 us -> 73.1 us (0.10); the launches traced: 749 us -> 72.7 us
  blocking collectives: 597 us -> 14.3 us
  other arithmetic: 65.5 us -> 0 us
  local copies, waits for them, and re-layouts: 30.2 us -> 2.22 us
  Pallas kernels: 0 us -> 18.4 us
  matrix products: 18.1 us -> 0 us
  between operations: 9.26 us -> 0.66 us
    psum x16 -> x0, blocking collectives: 597 us -> none  [field_sum(): return lax.psum(value, 'shard')]
    reduce_sum x19 -> x0, other arithmetic: 23.6 us -> none  [the longest x7 10.6 us: lanczos(): coupling = jnp.sqrt(field_sum(jnp.sum(image * image)) + epsilon)]
    pallas_call x0 -> x5, Pallas kernels: none -> 18.4 us  [the longest x1 4.86 us: per_device(): pl.pallas_call(propagate_kernel, out_shape=sds(NS, 8, NT), grid_spec=pltp...]
    dot_general x46 -> x0, matrix products: 18.1 us -> none  [the longest x28 14.9 us: contract(): return jnp.einsum(pattern, values, table, precision=lax.Precision.HIGHEST)]
    sub x3 -> x0, other arithmetic: 15.3 us -> none  [the longest x1 10.8 us: assemble(): real_part + real_coef[position] * vectors[position][0]]
    all_to_all x0 -> x1, blocking collectives: none -> 14.3 us  [exchange(): lax.all_to_all(value, 'shard', split_axis=0, concat_axis=0, tiled=True)]
    unnamed x21 -> x5, local copies, waits for them, and re-layouts: 13.6 us -> 2.22 us
    add x2 -> x0, other arithmetic: 10.8 us -> none  [the longest x1 10.8 us: assemble(): imag_part + real_coef[position] * vectors[position][1]]
  transfers between devices with their start and end apart: 3 -> 3, of which waited for: 2 -> 3; matrix products, arithmetic and copies ran while one was open for 0% -> 0% of each run, Pallas kernels for 0% -> 5%
where the time goes in v1:
time: 73.1 us; the launch traced here: 72.7 us
  waiting for transfers between devices  23 us (31%)
  Pallas kernels  18.4 us (25%)
  blocking collectives  14.3 us (20%)
  starting transfers between devices  14 us (19%)
  local copies, waits for them, and re-layouts  2.22 us (3%)
    all_to_all x1, blocking collectives, exchange(): lax.all_to_all(value, 'shard', split_axis=0, concat_axis=0, tiled=True)  14.3 us
    all_to_all x2, starting transfers between devices, exchange(): lax.all_to_all(value, 'shard', split_axis=0, concat_axis=0, tiled=True)  14 us
    ppermute x1, waiting for transfers between devices, per_device(): lax.ppermute(result, 'blk', [(b, (b + 1) % count) for b in range(count)])  12.1 us
    all_to_all x2, waiting for transfers between devices, exchange(): lax.all_to_all(value, 'shard', split_axis=0, concat_axis=0, tiled=True)  10.9 us
    pallas_call x1, Pallas kernels, per_device(): pl.pallas_call(propagate_kernel, out_shape=sds(NS, 8, NT), grid_spec=pltp...  4.86 us
    pallas_call x1, Pallas kernels, per_device(): pl.pallas_call(kerr_kernel, out_shape=sds(128, NT), in_specs=[SMEM] * 2 +...  4.7 us
    pallas_call x1, Pallas kernels, per_device(): pl.pallas_call(disperse_kernel, out_shape=sds(128, NT), in_specs=[SMEM] *...  3.93 us
    pallas_call x1, Pallas kernels, per_device(): pl.pallas_call(xmode_kernel, out_shape=(sds(128, NT), sds(NS, 8, 128), sd...  2.49 us
  transfers between devices with their start and end apart: 3, of which 3 were waited for; matrix products, arithmetic and copies ran while one was open for 0% of the time, Pallas kernels for 5%

profile of v1, /device:TPU:8, one launch (start us, length us, event | category | flops | bytes accessed | tf_op | source)
XLA Modules:
  0.0 72.7 jit_solution(15600986046057332554)
XLA Ops:
  0.0 2.4 %ymode.1 = f32[16,72,128]{2,1,0:T(8,128)} custom-call(f32[128,1024]{1,0:T(8,128)} %bitcast.3, f32[128,128]{1,0:T(8,128)} %constant.26.clone.mat_ref), custom_call_target="tpu_custom_call" | custom-call | tf_op jit(solution)/shard_map/ymode/pallas_call | solution.py:364
  2.4 9.2 %all-to-all-start = ((f32[16,72,128]{2,1,0:T(8,128)}), f32[16,72,128]{2,1,0:T(8,128)S(1)}, u32[]{:S(2)}, u32[]{:S(2)}) async-start(f32[16,72,128]{2,1,0:T(8,128)} %ymode.1), calls=%async_computation | async-start | bytes 1179648 | tf_op jit(solution)/shard_map/all_to_all | solution.py:356
  12.3 8.5 %all-to-all-done.in_ref = f32[16,72,128]{2,1,0:T(8,128)S(1)} async-done(((f32[16,72,128]{2,1,0:T(8,128)}), f32[16,72,128]{2,1,0:T(8,128)S(1)}, u32[]{:S(2)}, u32[]{:S(2)}) %all-to-all-start) | async-done | bytes 589856 | tf_op jit(solution)/shard_map/all_to_all | solution.py:356
  20.8 0.0 copy-start
  20.8 0.8 %copy-done = f32[16,72,128]{2,1,0:T(8,128)} copy-done((f32[16,72,128]{2,1,0:T(8,128)}, f32[16,72,128]{2,1,0:T(8,128)S(1)}, u32[]{:S(2)}) %copy-start) | copy-done | bytes 589848
  21.6 2.5 %xmode.1 = (f32[128,1024]{1,0:T(8,128)}, f32[16,8,128]{2,1,0:T(8,128)}, f32[8,128]{1,0:T(8,128)}) custom-call(f32[16,72,128]{2,1,0:T(8,128)} %copy-done, f32[128,128]{1,0:T(8,128)} %constant.27.clone.mat_ref), custom_call_target="tpu_custom_call" | custom-call | tf_op jit(solution)/shard_map/xmode/pallas_call | solution.py:369
  24.1 4.8 %all-to-all-start.1 = ((f32[16,8,128]{2,1,0:T(8,128)}), f32[16,8,128]{2,1,0:T(8,128)S(1)}, u32[]{:S(2)}, u32[]{:S(2)}) async-start(f32[16,8,128]{2,1,0:T(8,128)} %get-tuple-element.8), calls=%async_computation.1 | async-start | bytes 131072 | tf_op jit(solution)/shard_map/all_to_all | solution.py:356
  28.9 3.9 %disperse.1.modes_ref = f32[128,1024]{1,0:T(8,128)} custom-call(s32[1]{0:T(128)S(6)} %copy.19.kind_ref, f32[32]{0:T(128)} %disp_ref.1, f32[32]{0:T(128)} %gain_ref.1, f32[32]{0:T(128)} %sat_ref.1, f32[128,1024]{1,0:T(8,128)} %get-tuple-element.9.modes_ref, f32[8,128]{1,0:T(8,128)} %get-tuple-element.10.energy_ref, f32[8,128]{1,0:T(8,128)} %constant.28.clone.w_ref, ...), custom_call_target="tpu_custom_call" | custom-call | flops 805306368 | bytes 1048576 | tf_op jit(solution)/shard_map/disperse/pallas_call | solution.py:377
  32.8 2.4 %all-to-all-done.1.weight_ref = f32[16,8,128]{2,1,0:T(8,128)S(1)} async-done(((f32[16,8,128]{2,1,0:T(8,128)}), f32[16,8,128]{2,1,0:T(8,128)S(1)}, u32[]{:S(2)}, u32[]{:S(2)}) %all-to-all-start.1) | async-done | bytes 65568 | tf_op jit(solution)/shard_map/all_to_all | solution.py:356
  35.2 0.0 copy-start.1
  35.2 0.6 copy-done.1
  35.8 4.9 %propagate.1 = f32[16,8,1024]{2,1,0:T(8,128)} custom-call(s32[1]{0:T(128)} %bitcast.shard_ref, f32[16,8,128]{2,1,0:T(8,128)} %copy-done.1, f32[16,128]{1,0:T(8,128)} %constant.32.clone.lam_ref, f32[16,64,128]{2,1,0:T(8,128)} %constant.33.clone.own_ref, f32[128,1024]{1,0:T(8,128)} %disperse.1.modes_ref, f32[128,128]{1,0:T(8,128)} %constant.34.clone.mat_ref), custom_call_target="tpu_custom_call" | custom-call | tf_op jit(solution)/shard_map/propagate/pallas_call | solution.py:389
  40.7 14.3 %all_to_all.15.in_ref = f32[16,8,1024]{2,1,0:T(8,128)} all-to-all(f32[16,8,1024]{2,1,0:T(8,128)} %propagate.1), channel_id=1, replica_groups=mesh['blk'=32,'shard'=16] {'shard'}, dimensions={0} | all-to-all | bytes 1048576 | tf_op jit(solution)/shard_map/all_to_all | solution.py:356
  55.0 4.7 %kerr.1 = f32[128,1024]{1,0:T(8,128)} custom-call(s32[1]{0:T(128)S(6)} %copy.19.kind_ref, f32[32]{0:T(128)} %kerr_ref.1, f32[16,8,1024]{2,1,0:T(8,128)} %all_to_all.15.in_ref, f32[128,128]{1,0:T(8,128)} %constant.35.clone.mat_ref, f32[2,8,128]{2,1,0:T(8,128)} %constant.29.clone.tw_ref, f32[256,256]{1,0:T(8,128)} %constant.30.clone.fwd_ref, ...), custom_call_target="tpu_custom_call" | custom-call | tf_op jit(solution)/shard_map/kerr/pallas_call | solution.py:408
  59.7 0.0 collective-permute-start
  59.7 12.1 %collective-permute-done = f32[128,1024]{1,0:T(8,128)S(1)} collective-permute-done((f32[128,1024]{1,0:T(8,128)}, f32[128,1024]{1,0:T(8,128)S(1)}, u32[]{:S(2)}, u32[]{:S(2)}) %collective-permute-start) | collective-permute-done | bytes 524320 | tf_op jit(solution)/shard_map/ppermute | solution.py:421
  71.9 0.8 %copy.20 = f32[1,2,2,32,1024]{4,3,2,1,0:T(8,128)} copy(f32[1,2,2,32,1024]{4,3,2,1,0:T(8,128)S(1)} %bitcast.4) | data formatting | bytes 1048576
Async XLA Ops:
  2.4 18.4 %all-to-all-start = ((f32[16,72,128]{2,1,0:T(8,128)}), f32[16,72,128]{2,1,0:T(8,128)S(1)}, u32[]{:S(2)}, u32[]{:S(2)}) async-start(f32[16,72,128]{2,1,0:T(8,128)} %ymode.1), calls=%async_computation | async-start | bytes 1179648 | tf_op jit(solution)/shard_map/all_to_all | solution.py:356
  20.8 0.8 %copy-start = (f32[16,72,128]{2,1,0:T(8,128)}, f32[16,72,128]{2,1,0:T(8,128)S(1)}, u32[]{:S(2)}) copy-start(f32[16,72,128]{2,1,0:T(8,128)S(1)} %all-to-all-done.in_ref) | copy-start | bytes 1769476
  24.1 11.1 %all-to-all-start.1 = ((f32[16,8,128]{2,1,0:T(8,128)}), f32[16,8,128]{2,1,0:T(8,128)S(1)}, u32[]{:S(2)}, u32[]{:S(2)}) async-start(f32[16,8,128]{2,1,0:T(8,128)} %get-tuple-element.8), calls=%async_computation.1 | async-start | bytes 131072 | tf_op jit(solution)/shard_map/all_to_all | solution.py:356
  35.2 0.6 copy-start.1
  59.7 12.1 %collective-permute-start = (f32[128,1024]{1,0:T(8,128)}, f32[128,1024]{1,0:T(8,128)S(1)}, u32[]{:S(2)}, u32[]{:S(2)}) collective-permute-start(f32[128,1024]{1,0:T(8,128)} %kerr.1), channel_id=1, source_target_pairs={{0,16},{16,32},{32,48},{48,64},{64,80},{80,96},{96,112},{112,128},... | collective-permute-start | bytes 1572872 | tf_op jit(solution)/shard_map/ppermute | solution.py:421

commit v2 on v1

--- a/solution.py
+++ b/solution.py
@@ -170,7 +170,9 @@
         out_ref[d, 64:72, :] = total
 
 
-def xmode_kernel(in_ref, mat_ref, modes_ref, weight_ref, energy_ref):
+def xmode_kernel(
+    kind_ref, disp_ref, gain_ref, sat_ref, kerr_ref, in_ref, mat_ref, modes_ref, tile_ref
+):
     square = jnp.zeros((128, 128), F32)
     for c in range(NK):
         block = in_ref[:, 8 * c : 8 * c + 8, :].reshape(128, 128)
@@ -184,12 +186,17 @@
         precision=HIGHEST,
         preferred_element_type=F32,
     )
-    for d in range(NS):
-        weight_ref[d] = weight
     total = in_ref[0, 64:72, :]
     for d in range(1, NS):
         total = total + in_ref[d, 64:72, :]
-    energy_ref[...] = total
+    total = jnp.sum(total, axis=0, keepdims=True)
+    kind = kind_ref[0]
+    row = lax.broadcasted_iota(jnp.int32, (8, 128), 0)
+    tile = jnp.where(row == 1, total, weight)
+    for place, ref in ((2, disp_ref), (3, gain_ref), (4, sat_ref), (5, kerr_ref)):
+        tile = jnp.where(row == place, ref[kind], tile)
+    for d in range(NS):
+        tile_ref[d] = tile
 
 
 def whole_sum(value):
@@ -197,10 +204,8 @@
 
 
 def disperse_kernel(
-    kind_ref, disp_ref, gain_ref, sat_ref, modes_ref, energy_ref, w_ref, tw_ref, fwd_ref, bwd_ref,
-    out_ref, one, two
+    modes_ref, tile_ref, w_ref, tw_ref, fwd_ref, bwd_ref, out_ref, one, two
 ):
-    kind = kind_ref[0]
 
     def load(part, r0, a):
         return modes_ref[64 * part + r0 : 64 * part + r0 + 8, a * NB : (a + 1) * NB]
@@ -208,12 +213,13 @@
     outer_forward(load, 64, tw_ref, one)
     two[...] = mm(one[...], fwd_ref[...])
 
-    energy = whole_sum(energy_ref[...])
-    gain = gain_ref[kind] / (1.0 + energy / (NG * NG * NT) / sat_ref[kind])
+    energy = whole_sum(tile_ref[0, 1:2, :])
+    dispersion, gain_peak = tile_ref[0, 2:3, :], tile_ref[0, 3:4, :]
+    gain = gain_peak / (1.0 + energy / (NG * NG * NT) / tile_ref[0, 4:5, :])
     w = w_ref[...]
     relative = w / gain_width
     amplitude = jnp.exp(0.5 * gain / (1.0 + relative * relative) - loss_rate) * (1.0 / NT)
-    angle = disp_scale * disp_ref[kind] * w * w
+    angle = disp_scale * dispersion * w * w
     filter_spectrum(two, 64, amplitude * jnp.cos(angle), amplitude * jnp.sin(angle))
 
     one[...] = mm(two[...], bwd_ref[...])
@@ -307,10 +313,10 @@
 
 
 def kerr_kernel(
-    kind_ref, kerr_ref, in_ref, mat_ref, tw_ref, fwd_ref, bwd_ref, raman_ref,
+    tile_ref, in_ref, mat_ref, tw_ref, fwd_ref, bwd_ref, raman_ref,
     out_ref, field, delayed, one, two
 ):
-    kerr = kerr_ref[kind_ref[0]]
+    kerr = tile_ref[0, 5:6, 0:1]
     field[...] = mm(mat_ref[...], in_ref[...].reshape(128, NT))
 
     def load(side, r0, a):
@@ -340,20 +346,29 @@
         out_ref[64 + r0 : 64 + r0 + 8, :] = re * s + im * c
 
 
-def sds(*shape):
-    return jax.ShapeDtypeStruct(shape, F32)
-
-
 SMEM = pl.BlockSpec(memory_space=pltpu.SMEM)
 VMEM = pl.BlockSpec(memory_space=pltpu.VMEM)
 
 
+def near(*shape):
+    return pltpu.VMEM(shape, F32)
+
+
+def hold(value):
+    return pltpu.with_memory_space_constraint(value, pltpu.VMEM)
+
+
 def cost(flops, moved):
     return pl.CostEstimate(flops=flops, bytes_accessed=moved, transcendentals=0)
 
 
 def exchange(value):
     return lax.all_to_all(value, "shard", split_axis=0, concat_axis=0, tiled=True)
+
+
+def pass_on(value):
+    count = lax.axis_size("blk")
+    return lax.ppermute(value, "blk", [(b, (b + 1) % count) for b in range(count)])
 
 
 def per_device(seed_field, segment_order, seg_disp, seg_kerr, seg_gain, seg_sat):
@@ -362,63 +377,60 @@
     seed = seed_field.reshape(128, NT)
 
     ymodes = pl.pallas_call(
-        ymode_kernel, out_shape=sds(NS, 72, 128), in_specs=[VMEM] * 2, out_specs=VMEM,
+        ymode_kernel, out_shape=near(NS, 72, 128), in_specs=[VMEM] * 2, out_specs=VMEM,
         name="ymode",
     )(seed, t["to_ymode"])
     gathered = exchange(ymodes)
-    modes, weight, energy = pl.pallas_call(
+    modes, tile = pl.pallas_call(
         xmode_kernel,
-        out_shape=(sds(128, NT), sds(NS, 8, 128), sds(8, 128)),
-        in_specs=[VMEM] * 2,
-        out_specs=(VMEM,) * 3,
+        out_shape=(near(128, NT), near(NS, 8, 128)),
+        in_specs=[SMEM] * 5 + [VMEM] * 2,
+        out_specs=(VMEM,) * 2,
         name="xmode",
-    )(gathered, t["to_xmode"])
-    weights = exchange(weight)
+    )(segment_order, seg_disp, seg_gain, seg_sat, seg_kerr, hold(gathered), t["to_xmode"])
+    modes = pass_on(modes)
+    tile = pass_on(tile)
+    weights = exchange(tile)
     modes = pl.pallas_call(
         disperse_kernel,
-        out_shape=sds(128, NT),
-        in_specs=[SMEM] * 4 + [VMEM] * 6,
+        out_shape=near(128, NT),
+        in_specs=[VMEM] * 6,
         out_specs=VMEM,
         scratch_shapes=[pltpu.VMEM((512, 256), F32)] * 2,
         cost_estimate=cost(6 * 4 * 512 * 256 * 256, 2**20),
         name="disperse",
-    )(
-        segment_order, seg_disp, seg_gain, seg_sat, modes, energy, t["w"], t["twiddle"],
-        t["forward"], t["backward"],
-    )
+    )(hold(modes), hold(tile), t["w"], t["twiddle"], t["forward"], t["backward"])
     xback = pl.pallas_call(
         propagate_kernel,
-        out_shape=sds(NS, 8, NT),
+        out_shape=near(NS, 8, NT),
         grid_spec=pltpu.PrefetchScalarGridSpec(
             num_scalar_prefetch=1,
             grid=(1,),
             in_specs=[
-                pl.BlockSpec((NS, 8, 128), lambda i, s: (0, 0, 0)),
-                pl.BlockSpec((NS, 128), lambda i, s: (0, 0)),
+                VMEM,
+                VMEM,
                 pl.BlockSpec((1, 64, 128), lambda i, s: (s[0], 0, 0)),
-                pl.BlockSpec((128, NT), lambda i, s: (0, 0)),
-                pl.BlockSpec((128, 128), lambda i, s: (0, 0)),
+                VMEM,
+                VMEM,
             ],
-            out_specs=pl.BlockSpec((NS, 8, NT), lambda i, s: (0, 0, 0)),
+            out_specs=VMEM,
             scratch_shapes=[pltpu.VMEM((128, 128), F32)],
         ),
         name="propagate",
-    )(shard, weights, t["lam_all"], t["lam_own"], modes, t["from_xmode"])
+    )(shard, hold(weights), t["lam_all"], t["lam_own"], hold(modes), t["from_xmode"])
     rows = exchange(xback)
     result = pl.pallas_call(
         kerr_kernel,
-        out_shape=sds(128, NT),
-        in_specs=[SMEM] * 2 + [VMEM] * 6,
+        out_shape=jax.ShapeDtypeStruct((128, NT), F32),
+        in_specs=[VMEM] * 7,
         out_specs=VMEM,
         scratch_shapes=[pltpu.VMEM((128, NT), F32), pltpu.VMEM((64, NT), F32)]
         + [pltpu.VMEM((256, 256), F32)] * 2,
         name="kerr",
     )(
-        segment_order, seg_kerr, rows, t["from_ymode"], t["twiddle"], t["forward"],
-        t["backward"], t["raman"],
+        hold(tile), hold(rows), t["from_ymode"], t["twiddle"], t["forward"], t["backward"],
+        t["raman"],
     )
-    count = lax.axis_size("blk")
-    result = lax.ppermute(result, "blk", [(b, (b + 1) % count) for b in range(count)])
     return result.reshape(seed_field.shape)
 
 

time: 73.1 us -> 71.2 us (0.974)
  Pallas kernels: 18.4 us -> 15.6 us
  waiting for transfers between devices: 23 us -> 25.5 us
  local copies, waits for them, and re-layouts: 2.22 us -> 0 us
  starting transfers between devices: 14 us -> 15.7 us
  blocking collectives: 14.3 us -> 13.3 us
    pallas_call x5, Pallas kernels: 18.4 us -> 15.6 us  [the longest x1 4.57 us: per_device(): pl.pallas_call(kerr_kernel, out_shape=jax.ShapeDtypeStruct((128, NT), F32...]
    unnamed x5 -> x0, local copies, waits for them, and re-layouts: 2.22 us -> none
    ppermute x1 -> x2, waiting for transfers between devices: 12.1 us -> 13.6 us  [pass_on(): lax.ppermute(value, 'blk', [(b, (b + 1) % count) for b in range(count)])]
    ppermute x1 -> x2, starting transfers between devices: 0.01 us -> 1.47 us  [pass_on(): lax.ppermute(value, 'blk', [(b, (b + 1) % count) for b in range(count)])]
    all_to_all x1, blocking collectives: 14.3 us -> 13.3 us  [exchange(): lax.all_to_all(value, 'shard', split_axis=0, concat_axis=0, tiled=True)]
    all_to_all x2, waiting for transfers between devices: 10.9 us -> 11.8 us  [exchange(): lax.all_to_all(value, 'shard', split_axis=0, concat_axis=0, tiled=True)]
  transfers between devices with their start and end apart: 3 -> 4, of which waited for: 3 -> 3; matrix products, arithmetic and copies ran while one was open for 0% -> 0% of each run, Pallas kernels for 5% -> 4%
where the time goes in v2:
time: 71.2 us; the launch traced here: 70.7 us
  waiting for transfers between devices  25.5 us (36%)
  starting transfers between devices  15.7 us (22%)
  Pallas kernels  15.6 us (22%)
  blocking collectives  13.3 us (19%)
    all_to_all x2, starting transfers between devices, exchange(): lax.all_to_all(value, 'shard', split_axis=0, concat_axis=0, tiled=True)  14.2 us
    ppermute x2, waiting for transfers between devices, pass_on(): lax.ppermute(value, 'blk', [(b, (b + 1) % count) for b in range(count)])  13.6 us
    all_to_all x1, blocking collectives, exchange(): lax.all_to_all(value, 'shard', split_axis=0, concat_axis=0, tiled=True)  13.3 us
    all_to_all x2, waiting for transfers between devices, exchange(): lax.all_to_all(value, 'shard', split_axis=0, concat_axis=0, tiled=True)  11.8 us
    pallas_call x1, Pallas kernels, per_device(): pl.pallas_call(kerr_kernel, out_shape=jax.ShapeDtypeStruct((128, NT), F32...  4.57 us
    pallas_call x1, Pallas kernels, per_device(): pl.pallas_call(propagate_kernel, out_shape=near(NS, 8, NT), grid_spec=plt...  3.88 us
    pallas_call x1, Pallas kernels, per_device(): pl.pallas_call(disperse_kernel, out_shape=near(128, NT), in_specs=[VMEM]...  3.01 us
    pallas_call x1, Pallas kernels, per_device(): pl.pallas_call(ymode_kernel, out_shape=near(NS, 72, 128), in_specs=[VMEM]...  2.45 us
  transfers between devices with their start and end apart: 4, of which 3 were waited for; matrix products, arithmetic and copies ran while one was open for 0% of the time, Pallas kernels for 4%

profile of v2, /device:TPU:8, one launch (start us, length us, event | category | flops | bytes accessed | tf_op | source)
XLA Modules:
  0.0 70.7 jit_solution(1213666068855285742)
XLA Ops:
  0.0 2.4 %ymode.1 = f32[16,72,128]{2,1,0:T(8,128)} custom-call(f32[128,1024]{1,0:T(8,128)} %bitcast.3, f32[128,128]{1,0:T(8,128)} %constant.26.clone.mat_ref), custom_call_target="tpu_custom_call" | custom-call | tf_op jit(solution)/shard_map/ymode/pallas_call | solution.py:379
  2.4 9.2 %all-to-all-start = ((f32[16,72,128]{2,1,0:T(8,128)}), f32[16,72,128]{2,1,0:T(8,128)S(1)}, u32[]{:S(2)}, u32[]{:S(2)}) async-start(f32[16,72,128]{2,1,0:T(8,128)} %ymode.1), calls=%async_computation | async-start | bytes 1179648 | tf_op jit(solution)/shard_map/all_to_all | solution.py:366
  12.3 8.5 %all-to-all-done.in_ref = f32[16,72,128]{2,1,0:T(8,128)S(1)} async-done(((f32[16,72,128]{2,1,0:T(8,128)}), f32[16,72,128]{2,1,0:T(8,128)S(1)}, u32[]{:S(2)}, u32[]{:S(2)}) %all-to-all-start) | async-done | bytes 589856 | tf_op jit(solution)/shard_map/all_to_all | solution.py:366
  20.8 1.6 %xmode.1 = (f32[128,1024]{1,0:T(8,128)S(1)}, f32[16,8,128]{2,1,0:T(8,128)S(1)}) custom-call(s32[1]{0:T(128)S(6)} %copy.18.kind_ref, f32[32]{0:T(128)} %disp_ref.1, f32[32]{0:T(128)} %gain_ref.1, f32[32]{0:T(128)} %sat_ref.1, f32[32]{0:T(128)} %kerr_ref.1, f32[16,72,128]{2,1,0:T(8,128)S(1)} %all-to-all-done.in_ref, f32[128,128]{1,0:T(8,128)} %constant.27.clone.mat_ref), custom_call_target="tpu_custom_call" | custom-call | tf_op jit(solution)/shard_map/xmode/pallas_call | solution.py:384
  22.5 0.0 collective-permute-start.1
  22.5 1.4 %collective-permute-start = (f32[16,8,128]{2,1,0:T(8,128)S(1)}, f32[16,8,128]{2,1,0:T(8,128)}, u32[]{:S(2)}, u32[]{:S(2)}) collective-permute-start(f32[16,8,128]{2,1,0:T(8,128)S(1)} %get-tuple-element.7), channel_id=1, source_target_pairs={{0,16},{16,32},{32,48},{48,64},{64,80},{80,96},{96,112},{112,128},... | collective-permute-start | bytes 196616 | tf_op jit(solution)/shard_map/ppermute | solution.py:371
  23.9 13.6 %collective-permute-done.tile_ref = f32[16,8,128]{2,1,0:T(8,128)} collective-permute-done((f32[16,8,128]{2,1,0:T(8,128)S(1)}, f32[16,8,128]{2,1,0:T(8,128)}, u32[]{:S(2)}, u32[]{:S(2)}) %collective-permute-start) | collective-permute-done | bytes 65568 | tf_op jit(solution)/shard_map/ppermute | solution.py:371
  37.6 5.0 %all-to-all-start.1 = ((f32[16,8,128]{2,1,0:T(8,128)}), f32[16,8,128]{2,1,0:T(8,128)S(1)}, u32[]{:S(2)}, u32[]{:S(2)}) async-start(f32[16,8,128]{2,1,0:T(8,128)} %collective-permute-done.tile_ref), calls=%async_computation.1 | async-start | bytes 131072 | tf_op jit(solution)/shard_map/all_to_all | solution.py:366
  42.6 0.0 collective-permute-done.1.modes_ref
  42.6 3.0 %disperse.1.modes_ref = f32[128,1024]{1,0:T(8,128)S(1)} custom-call(f32[128,1024]{1,0:T(8,128)S(1)} %collective-permute-done.1.modes_ref, f32[16,8,128]{2,1,0:T(8,128)} %collective-permute-done.tile_ref, f32[8,128]{1,0:T(8,128)} %constant.28.clone.w_ref, f32[2,8,128]{2,1,0:T(8,128)} %constant.29.clone.tw_ref, f32[256,256]{1,0:T(8,128)} %constant.30.clone.fwd_ref, ...), custom_call_target="tpu_custom_call" | custom-call | flops 805306368 | bytes 1048576 | tf_op jit(solution)/shard_map/disperse/pallas_call | solution.py:394
  45.6 3.3 %all-to-all-done.1.weight_ref = f32[16,8,128]{2,1,0:T(8,128)S(1)} async-done(((f32[16,8,128]{2,1,0:T(8,128)}), f32[16,8,128]{2,1,0:T(8,128)S(1)}, u32[]{:S(2)}, u32[]{:S(2)}) %all-to-all-start.1) | async-done | bytes 65568 | tf_op jit(solution)/shard_map/all_to_all | solution.py:366
  48.9 3.9 %propagate.1 = f32[16,8,1024]{2,1,0:T(8,128)S(1)} custom-call(s32[1]{0:T(128)} %bitcast.1.shard_ref, f32[16,8,128]{2,1,0:T(8,128)S(1)} %all-to-all-done.1.weight_ref, f32[16,128]{1,0:T(8,128)} %constant.32.clone.lam_ref, f32[16,64,128]{2,1,0:T(8,128)} %constant.33.clone.own_ref, f32[128,1024]{1,0:T(8,128)S(1)} %disperse.1.modes_ref, ...), custom_call_target="tpu_custom_call" | custom-call | tf_op jit(solution)/shard_map/propagate/pallas_call | solution.py:403
  52.8 13.3 %all_to_all.15.in_ref = f32[16,8,1024]{2,1,0:T(8,128)S(1)} all-to-all(f32[16,8,1024]{2,1,0:T(8,128)S(1)} %propagate.1), channel_id=1, replica_groups=mesh['blk'=32,'shard'=16] {'shard'}, dimensions={0} | all-to-all | bytes 1048576 | tf_op jit(solution)/shard_map/all_to_all | solution.py:366
  66.1 4.6 %kerr.1 = f32[128,1024]{1,0:T(8,128)} custom-call(f32[16,8,128]{2,1,0:T(8,128)} %collective-permute-done.tile_ref, f32[16,8,1024]{2,1,0:T(8,128)S(1)} %all_to_all.15.in_ref, f32[128,128]{1,0:T(8,128)} %constant.35.clone.mat_ref, f32[2,8,128]{2,1,0:T(8,128)} %constant.29.clone.tw_ref, f32[256,256]{1,0:T(8,128)} %constant.30.clone.fwd_ref, ...), custom_call_target="tpu_custom_call" | custom-call | tf_op jit(solution)/shard_map/kerr/pallas_call | solution.py:422
Async XLA Ops:
  2.4 18.4 %all-to-all-start = ((f32[16,72,128]{2,1,0:T(8,128)}), f32[16,72,128]{2,1,0:T(8,128)S(1)}, u32[]{:S(2)}, u32[]{:S(2)}) async-start(f32[16,72,128]{2,1,0:T(8,128)} %ymode.1), calls=%async_computation | async-start | bytes 1179648 | tf_op jit(solution)/shard_map/all_to_all | solution.py:366
  22.5 20.2 %collective-permute-start.1 = (f32[128,1024]{1,0:T(8,128)S(1)}, f32[128,1024]{1,0:T(8,128)S(1)}, u32[]{:S(2)}, u32[]{:S(2)}) collective-permute-start(f32[128,1024]{1,0:T(8,128)S(1)} %get-tuple-element.8), channel_id=1, source_target_pairs={{0,16},{16,32},{32,48},{48,64},{64,80},{80,96},{96,112},{112,128},... | collective-permute-start | bytes 1572872 | tf_op jit(solution)/shard_map/ppermute | solution.py:371
  22.5 15.1 %collective-permute-start = (f32[16,8,128]{2,1,0:T(8,128)S(1)}, f32[16,8,128]{2,1,0:T(8,128)}, u32[]{:S(2)}, u32[]{:S(2)}) collective-permute-start(f32[16,8,128]{2,1,0:T(8,128)S(1)} %get-tuple-element.7), channel_id=1, source_target_pairs={{0,16},{16,32},{32,48},{48,64},{64,80},{80,96},{96,112},{112,128},... | collective-permute-start | bytes 196616 | tf_op jit(solution)/shard_map/ppermute | solution.py:371
  37.6 11.3 %all-to-all-start.1 = ((f32[16,8,128]{2,1,0:T(8,128)}), f32[16,8,128]{2,1,0:T(8,128)S(1)}, u32[]{:S(2)}, u32[]{:S(2)}) async-start(f32[16,8,128]{2,1,0:T(8,128)} %collective-permute-done.tile_ref), calls=%async_computation.1 | async-start | bytes 131072 | tf_op jit(solution)/shard_map/all_to_all | solution.py:366

commit v3 on v2

--- a/solution.py
+++ b/solution.py
@@ -267,9 +267,7 @@
     return real, imag
 
 
-def propagate_kernel(
-    shard_ref, weight_ref, lam_ref, own_ref, modes_ref, mat_ref, out_ref, scaled
-):
+def lanczos_kernel(shard_ref, weight_ref, lam_ref, own_ref, factor_ref):
     weight = weight_ref[:, 0, :]
     lam = lam_ref[...]
     own = own_ref[0]
@@ -301,8 +299,12 @@
     for j in range(1, KRYLOV):
         gain_re = gain_re + real[j : j + 1, 0:1] * polys[j]
         gain_im = gain_im + imag[j : j + 1, 0:1] * polys[j]
-    gain_re = gain_re * scale_zero
-    gain_im = gain_im * scale_zero
+    factor_ref[0] = gain_re * scale_zero
+    factor_ref[1] = gain_im * scale_zero
+
+
+def propagate_kernel(factor_ref, modes_ref, mat_ref, out_ref, scaled):
+    gain_re, gain_im = factor_ref[0], factor_ref[1]
     for c in range(NK):
         a = modes_ref[0:64, c * 128 : (c + 1) * 128]
         b = modes_ref[64:128, c * 128 : (c + 1) * 128]
@@ -388,9 +390,7 @@
         out_specs=(VMEM,) * 2,
         name="xmode",
     )(segment_order, seg_disp, seg_gain, seg_sat, seg_kerr, hold(gathered), t["to_xmode"])
-    modes = pass_on(modes)
-    tile = pass_on(tile)
-    weights = exchange(tile)
+    shifted = pass_on(tile)
     modes = pl.pallas_call(
         disperse_kernel,
         out_shape=near(128, NT),
@@ -400,24 +400,29 @@
         cost_estimate=cost(6 * 4 * 512 * 256 * 256, 2**20),
         name="disperse",
     )(hold(modes), hold(tile), t["w"], t["twiddle"], t["forward"], t["backward"])
+    modes, shifted = lax.optimization_barrier((modes, shifted))
+    modes = pass_on(modes)
+    weights = exchange(shifted)
+    factor = pl.pallas_call(
+        lanczos_kernel,
+        out_shape=near(2, 64, 128),
+        grid_spec=pltpu.PrefetchScalarGridSpec(
+            num_scalar_prefetch=1,
+            grid=(1,),
+            in_specs=[VMEM, VMEM, pl.BlockSpec((1, 64, 128), lambda i, s: (s[0], 0, 0))],
+            out_specs=VMEM,
+        ),
+        cost_estimate=cost(6 * 2 * 512 * 256 * 256, 2**20),
+        name="lanczos",
+    )(shard, hold(weights), t["lam_all"], t["lam_own"])
     xback = pl.pallas_call(
         propagate_kernel,
         out_shape=near(NS, 8, NT),
-        grid_spec=pltpu.PrefetchScalarGridSpec(
-            num_scalar_prefetch=1,
-            grid=(1,),
-            in_specs=[
-                VMEM,
-                VMEM,
-                pl.BlockSpec((1, 64, 128), lambda i, s: (s[0], 0, 0)),
-                VMEM,
-                VMEM,
-            ],
-            out_specs=VMEM,
-            scratch_shapes=[pltpu.VMEM((128, 128), F32)],
-        ),
+        in_specs=[VMEM] * 3,
+        out_specs=VMEM,
+        scratch_shapes=[pltpu.VMEM((128, 128), F32)],
         name="propagate",
-    )(shard, hold(weights), t["lam_all"], t["lam_own"], hold(modes), t["from_xmode"])
+    )(hold(factor), hold(modes), t["from_xmode"])
     rows = exchange(xback)
     result = pl.pallas_call(
         kerr_kernel,
@@ -428,7 +433,7 @@
         + [pltpu.VMEM((256, 256), F32)] * 2,
         name="kerr",
     )(
-        hold(tile), hold(rows), t["from_ymode"], t["twiddle"], t["forward"], t["backward"],
+        hold(shifted), hold(rows), t["from_ymode"], t["twiddle"], t["forward"], t["backward"],
         t["raman"],
     )
     return result.reshape(seed_field.shape)

time: 71.2 us -> 66.3 us (0.931)
  waiting for transfers between devices: 25.5 us -> 21.3 us
  starting transfers between devices: 15.7 us -> 14.2 us
    ppermute x2, waiting for transfers between devices: 13.6 us -> 6.5 us  [pass_on(): lax.ppermute(value, 'blk', [(b, (b + 1) % count) for b in range(count)])]
    all_to_all x2, waiting for transfers between devices: 11.8 us -> 14.8 us  [exchange(): lax.all_to_all(value, 'shard', split_axis=0, concat_axis=0, tiled=True)]
    ppermute x2, starting transfers between devices: 1.47 us -> 0.02 us  [pass_on(): lax.ppermute(value, 'blk', [(b, (b + 1) % count) for b in range(count)])]
    pallas_call x1 -> x2, Pallas kernels: 3.88 us -> 4.6 us  [the longest x1 3.17 us: per_device(): pl.pallas_call(lanczos_kernel, out_shape=near(2, 64, 128), grid_spec=pltp...]
  transfers between devices with their start and end apart: 4 -> 4, of which waited for: 3 -> 3; matrix products, arithmetic and copies ran while one was open for 0% -> 0% of each run, Pallas kernels for 4% -> 9%
where the time goes in v3:
time: 66.3 us; the launch traced here: 65.8 us
  waiting for transfers between devices  21.3 us (32%)
  Pallas kernels  16.2 us (24%)
  starting transfers between devices  14.2 us (21%)
  blocking collectives  13.3 us (20%)
  between operations  0.7 us (1%)
    all_to_all x2, waiting for transfers between devices, exchange(): lax.all_to_all(value, 'shard', split_axis=0, concat_axis=0, tiled=True)  14.8 us
    all_to_all x2, starting transfers between devices, exchange(): lax.all_to_all(value, 'shard', split_axis=0, concat_axis=0, tiled=True)  14.2 us
    all_to_all x1, blocking collectives, exchange(): lax.all_to_all(value, 'shard', split_axis=0, concat_axis=0, tiled=True)  13.3 us
    ppermute x2, waiting for transfers between devices, pass_on(): lax.ppermute(value, 'blk', [(b, (b + 1) % count) for b in range(count)])  6.5 us
    pallas_call x1, Pallas kernels, per_device(): pl.pallas_call(kerr_kernel, out_shape=jax.ShapeDtypeStruct((128, NT), F32...  4.57 us
    pallas_call x1, Pallas kernels, per_device(): pl.pallas_call(lanczos_kernel, out_shape=near(2, 64, 128), grid_spec=pltp...  3.17 us
    pallas_call x1, Pallas kernels, per_device(): pl.pallas_call(disperse_kernel, out_shape=near(128, NT), in_specs=[VMEM]...  2.97 us
    pallas_call x1, Pallas kernels, per_device(): pl.pallas_call(ymode_kernel, out_shape=near(NS, 72, 128), in_specs=[VMEM]...  2.45 us
  transfers between devices with their start and end apart: 4, of which 3 were waited for; matrix products, arithmetic and copies ran while one was open for 0% of the time, Pallas kernels for 9%

profile of v3, /device:TPU:8, one launch (start us, length us, event | category | flops | bytes accessed | tf_op | source)
XLA Modules:
  0.0 65.8 jit_solution(13777227204915886368)
XLA Ops:
  0.0 2.4 %ymode.1 = f32[16,72,128]{2,1,0:T(8,128)} custom-call(f32[128,1024]{1,0:T(8,128)} %bitcast.3, f32[128,128]{1,0:T(8,128)} %constant.26.clone.mat_ref), custom_call_target="tpu_custom_call" | custom-call | tf_op jit(solution)/shard_map/ymode/pallas_call | solution.py:381
  2.4 9.2 %all-to-all-start = ((f32[16,72,128]{2,1,0:T(8,128)}), f32[16,72,128]{2,1,0:T(8,128)S(1)}, u32[]{:S(2)}, u32[]{:S(2)}) async-start(f32[16,72,128]{2,1,0:T(8,128)} %ymode.1), calls=%async_computation | async-start | bytes 1179648 | tf_op jit(solution)/shard_map/all_to_all | solution.py:368
  12.3 8.5 %all-to-all-done.in_ref = f32[16,72,128]{2,1,0:T(8,128)S(1)} async-done(((f32[16,72,128]{2,1,0:T(8,128)}), f32[16,72,128]{2,1,0:T(8,128)S(1)}, u32[]{:S(2)}, u32[]{:S(2)}) %all-to-all-start) | async-done | bytes 589856 | tf_op jit(solution)/shard_map/all_to_all | solution.py:368
  20.8 1.6 %xmode.1 = (f32[128,1024]{1,0:T(8,128)S(1)}, f32[16,8,128]{2,1,0:T(8,128)S(1)}) custom-call(s32[1]{0:T(128)S(6)} %copy.18.kind_ref, f32[32]{0:T(128)} %disp_ref.1, f32[32]{0:T(128)} %gain_ref.1, f32[32]{0:T(128)} %sat_ref.1, f32[32]{0:T(128)} %kerr_ref.1, f32[16,72,128]{2,1,0:T(8,128)S(1)} %all-to-all-done.in_ref, f32[128,128]{1,0:T(8,128)} %constant.27.clone.mat_ref), custom_call_target="tpu_custom_call" | custom-call | tf_op jit(solution)/shard_map/xmode/pallas_call | solution.py:386
  22.5 0.0 collective-permute-start
  22.5 3.0 %disperse.1 = f32[128,1024]{1,0:T(8,128)S(1)} custom-call(f32[128,1024]{1,0:T(8,128)S(1)} %get-tuple-element.9.modes_ref, f32[16,8,128]{2,1,0:T(8,128)S(1)} %get-tuple-element.10.tile_ref, f32[8,128]{1,0:T(8,128)} %constant.28.clone.w_ref, f32[2,8,128]{2,1,0:T(8,128)} %constant.29.clone.tw_ref, f32[256,256]{1,0:T(8,128)} %constant.30.clone.fwd_ref, ...), custom_call_target="tpu_custom_call" | custom-call | flops 805306368 | bytes 1048576 | tf_op jit(solution)/shard_map/disperse/pallas_call | solution.py:394
  25.5 6.5 %collective-permute-done.tile_ref = f32[16,8,128]{2,1,0:T(8,128)} collective-permute-done((f32[16,8,128]{2,1,0:T(8,128)S(1)}, f32[16,8,128]{2,1,0:T(8,128)}, u32[]{:S(2)}, u32[]{:S(2)}) %collective-permute-start) | collective-permute-done | bytes 65568 | tf_op jit(solution)/shard_map/ppermute | solution.py:373
  32.0 0.0 collective-permute-start.1
  32.0 5.0 %all-to-all-start.1 = ((f32[16,8,128]{2,1,0:T(8,128)}), f32[16,8,128]{2,1,0:T(8,128)S(1)}, u32[]{:S(2)}, u32[]{:S(2)}) async-start(f32[16,8,128]{2,1,0:T(8,128)} %collective-permute-done.tile_ref), calls=%async_computation.1 | async-start | bytes 131072 | tf_op jit(solution)/shard_map/all_to_all | solution.py:368
  37.0 6.3 %all-to-all-done.1.weight_ref = f32[16,8,128]{2,1,0:T(8,128)S(1)} async-done(((f32[16,8,128]{2,1,0:T(8,128)}), f32[16,8,128]{2,1,0:T(8,128)S(1)}, u32[]{:S(2)}, u32[]{:S(2)}) %all-to-all-start.1) | async-done | bytes 65568 | tf_op jit(solution)/shard_map/all_to_all | solution.py:368
  43.3 3.2 %lanczos.1.factor_ref = f32[2,64,128]{2,1,0:T(8,128)S(1)} custom-call(s32[1]{0:T(128)} %bitcast.1.shard_ref, f32[16,8,128]{2,1,0:T(8,128)S(1)} %all-to-all-done.1.weight_ref, f32[16,128]{1,0:T(8,128)} %constant.32.clone.lam_ref, f32[16,64,128]{2,1,0:T(8,128)} %constant.33.clone.own_ref), custom_call_target="tpu_custom_call" | custom-call | flops 402653184 | bytes 1048576 | tf_op jit(solution)/shard_map/lanczos/pallas_call | solution.py:406
  46.5 0.0 collective-permute-done.1.modes_ref
  46.5 1.4 %propagate.1 = f32[16,8,1024]{2,1,0:T(8,128)S(1)} custom-call(f32[2,64,128]{2,1,0:T(8,128)S(1)} %lanczos.1.factor_ref, f32[128,1024]{1,0:T(8,128)S(1)} %collective-permute-done.1.modes_ref, f32[128,128]{1,0:T(8,128)} %constant.34.clone.mat_ref), custom_call_target="tpu_custom_call" | custom-call | tf_op jit(solution)/shard_map/propagate/pallas_call | solution.py:418
  47.9 13.3 %all_to_all.15.in_ref = f32[16,8,1024]{2,1,0:T(8,128)S(1)} all-to-all(f32[16,8,1024]{2,1,0:T(8,128)S(1)} %propagate.1), channel_id=1, replica_groups=mesh['blk'=32,'shard'=16] {'shard'}, dimensions={0} | all-to-all | bytes 1048576 | tf_op jit(solution)/shard_map/all_to_all | solution.py:368
  61.3 4.6 %kerr.1 = f32[128,1024]{1,0:T(8,128)} custom-call(f32[16,8,128]{2,1,0:T(8,128)} %collective-permute-done.tile_ref, f32[16,8,1024]{2,1,0:T(8,128)S(1)} %all_to_all.15.in_ref, f32[128,128]{1,0:T(8,128)} %constant.35.clone.mat_ref, f32[2,8,128]{2,1,0:T(8,128)} %constant.29.clone.tw_ref, f32[256,256]{1,0:T(8,128)} %constant.30.clone.fwd_ref, ...), custom_call_target="tpu_custom_call" | custom-call | tf_op jit(solution)/shard_map/kerr/pallas_call | solution.py:427
Async XLA Ops:
  2.4 18.4 %all-to-all-start = ((f32[16,72,128]{2,1,0:T(8,128)}), f32[16,72,128]{2,1,0:T(8,128)S(1)}, u32[]{:S(2)}, u32[]{:S(2)}) async-start(f32[16,72,128]{2,1,0:T(8,128)} %ymode.1), calls=%async_computation | async-start | bytes 1179648 | tf_op jit(solution)/shard_map/all_to_all | solution.py:368
  22.5 9.5 %collective-permute-start = (f32[16,8,128]{2,1,0:T(8,128)S(1)}, f32[16,8,128]{2,1,0:T(8,128)}, u32[]{:S(2)}, u32[]{:S(2)}) collective-permute-start(f32[16,8,128]{2,1,0:T(8,128)S(1)} %get-tuple-element.10.tile_ref), channel_id=1, source_target_pairs={{0,16},{16,32},{32,48},{48,64},{64,80},{80,96},{96,112},{112,128},... | collective-permute-start | bytes 196616 | tf_op jit(solution)/shard_map/ppermute | solution.py:373
  32.0 14.5 %collective-permute-start.1 = (f32[128,1024]{1,0:T(8,128)S(1)}, f32[128,1024]{1,0:T(8,128)S(1)}, u32[]{:S(2)}, u32[]{:S(2)}) collective-permute-start(f32[128,1024]{1,0:T(8,128)S(1)} %disperse.1), channel_id=1, source_target_pairs={{0,16},{16,32},{32,48},{48,64},{64,80},{80,96},{96,112},{112,128},... | collective-permute-start | bytes 1572872 | tf_op jit(solution)/shard_map/ppermute | solution.py:373
  32.0 11.3 %all-to-all-start.1 = ((f32[16,8,128]{2,1,0:T(8,128)}), f32[16,8,128]{2,1,0:T(8,128)S(1)}, u32[]{:S(2)}, u32[]{:S(2)}) async-start(f32[16,8,128]{2,1,0:T(8,128)} %collective-permute-done.tile_ref), calls=%async_computation.1 | async-start | bytes 131072 | tf_op jit(solution)/shard_map/all_to_all | solution.py:368

commit v4 on v3

--- a/solution.py
+++ b/solution.py
@@ -51,7 +51,6 @@
     pair = values.reshape(NS, 2)
     lam = pair[:, None, :, None] + values[None, None, None, :] + np.zeros((1, 2, 1, 1))
     lam_all = lam.reshape(NS, 128)
-    lam_own = np.broadcast_to(lam_all[:, :64, None], (NS, 64, 128))
 
     inner = np.arange(NB)
     angle = 2.0 * np.pi * ((inner[:, None] * inner[None, :]) % NB) / NB
@@ -76,7 +75,6 @@
         to_xmode=f32(to_xmode),
         from_xmode=f32(to_xmode.T),
         lam_all=f32(lam_all),
-        lam_own=f32(lam_own),
         forward=f32(forward),
         backward=f32(backward),
         twiddle=f32(np.stack([tw_cos, tw_sin])),
@@ -157,7 +155,9 @@
         spec[lo:hi, NB : 2 * NB] = a * fi + b * fr
 
 
-def ymode_kernel(seed_ref, mat_ref, out_ref):
+def ymode_kernel(
+    seed_ref, mat_ref, lam_ref, kind_ref, disp_ref, gain_ref, sat_ref, kerr_ref, out_ref
+):
     total = jnp.zeros((8, 128), F32)
     for c in range(NK):
         block = seed_ref[:, c * 128 : (c + 1) * 128]
@@ -166,13 +166,17 @@
             total = total + square[8 * r : 8 * r + 8, :]
         modes = mm(mat_ref[...], block)
         out_ref[:, 8 * c : 8 * c + 8, :] = modes.reshape(NS, 8, 128)
+    row = lax.broadcasted_iota(jnp.int32, (8, 128), 0)
+    chosen = lax.broadcasted_iota(jnp.int32, (1, 32), 1) == kind_ref[...]
+    side = jnp.broadcast_to(jnp.sum(total, axis=0, keepdims=True), (8, 128))
+    for place, ref in ((2, disp_ref), (3, gain_ref), (4, sat_ref), (5, kerr_ref)):
+        value = jnp.sum(jnp.where(chosen, ref[...], 0.0), axis=1, keepdims=True)
+        side = jnp.where(row == place, value, side)
     for d in range(NS):
-        out_ref[d, 64:72, :] = total
-
-
-def xmode_kernel(
-    kind_ref, disp_ref, gain_ref, sat_ref, kerr_ref, in_ref, mat_ref, modes_ref, tile_ref
-):
+        out_ref[d, 64:72, :] = jnp.where(row == 6, lam_ref[d : d + 1, :], side)
+
+
+def xmode_kernel(in_ref, mat_ref, modes_ref, tile_ref):
     square = jnp.zeros((128, 128), F32)
     for c in range(NK):
         block = in_ref[:, 8 * c : 8 * c + 8, :].reshape(128, 128)
@@ -186,15 +190,12 @@
         precision=HIGHEST,
         preferred_element_type=F32,
     )
-    total = in_ref[0, 64:72, :]
+    side = in_ref[0, 64:72, :]
+    energy = side
     for d in range(1, NS):
-        total = total + in_ref[d, 64:72, :]
-    total = jnp.sum(total, axis=0, keepdims=True)
-    kind = kind_ref[0]
+        energy = energy + in_ref[d, 64:72, :]
     row = lax.broadcasted_iota(jnp.int32, (8, 128), 0)
-    tile = jnp.where(row == 1, total, weight)
-    for place, ref in ((2, disp_ref), (3, gain_ref), (4, sat_ref), (5, kerr_ref)):
-        tile = jnp.where(row == place, ref[kind], tile)
+    tile = jnp.where(row == 0, weight, jnp.where(row == 1, energy, side))
     for d in range(NS):
         tile_ref[d] = tile
 
@@ -267,13 +268,13 @@
     return real, imag
 
 
-def lanczos_kernel(shard_ref, weight_ref, lam_ref, own_ref, factor_ref):
+def lanczos_kernel(own_ref, weight_ref, factor_ref):
     weight = weight_ref[:, 0, :]
-    lam = lam_ref[...]
-    own = own_ref[0]
+    lam = weight_ref[:, 6, :]
+    own = jnp.broadcast_to(own_ref[0, 6:7, :], (8, 128))
     scale_zero = jnp.sqrt(whole_sum(weight) + epsilon)
     vector = jnp.sqrt(weight) / scale_zero
-    poly = jnp.ones((64, 128), F32) / scale_zero
+    poly = jnp.ones((8, 128), F32) / scale_zero
     before_vector, before_poly, coupling = None, None, None
     diagonals, couplings, polys = [], [], [poly]
     for step in range(KRYLOV):
@@ -294,13 +295,12 @@
             before_poly, poly = poly, grown / coupling
             polys.append(poly)
     real, imag = krylov_exp(diagonals, couplings)
-    gain_re = real[0:1, 0:1] * polys[0]
-    gain_im = imag[0:1, 0:1] * polys[0]
-    for j in range(1, KRYLOV):
-        gain_re = gain_re + real[j : j + 1, 0:1] * polys[j]
-        gain_im = gain_im + imag[j : j + 1, 0:1] * polys[j]
-    factor_ref[0] = gain_re * scale_zero
-    factor_ref[1] = gain_im * scale_zero
+    for place, part in ((0, real), (1, imag)):
+        gain = part[0:1, 0:1] * polys[0]
+        for j in range(1, KRYLOV):
+            gain = gain + part[j : j + 1, 0:1] * polys[j]
+        gain = gain * scale_zero
+        factor_ref[place] = jnp.broadcast_to(gain[0:1, :], (128, 128)).T[0:64, :]
 
 
 def propagate_kernel(factor_ref, modes_ref, mat_ref, out_ref, scaled):
@@ -348,7 +348,6 @@
         out_ref[64 + r0 : 64 + r0 + 8, :] = re * s + im * c
 
 
-SMEM = pl.BlockSpec(memory_space=pltpu.SMEM)
 VMEM = pl.BlockSpec(memory_space=pltpu.VMEM)
 
 
@@ -375,21 +374,27 @@
 
 def per_device(seed_field, segment_order, seg_disp, seg_kerr, seg_gain, seg_sat):
     t = tables()
-    shard = lax.axis_index("shard").astype(jnp.int32).reshape(1)
+    near_tables = {name: hold(jnp.asarray(value)) for name, value in t.items()}
     seed = seed_field.reshape(128, NT)
 
     ymodes = pl.pallas_call(
-        ymode_kernel, out_shape=near(NS, 72, 128), in_specs=[VMEM] * 2, out_specs=VMEM,
+        ymode_kernel,
+        out_shape=near(NS, 72, 128),
+        in_specs=[VMEM] * 8,
+        out_specs=VMEM,
         name="ymode",
-    )(seed, t["to_ymode"])
+    )(
+        seed, t["to_ymode"], t["lam_all"], segment_order.reshape(1, 1),
+        *(each.reshape(1, 32) for each in (seg_disp, seg_gain, seg_sat, seg_kerr)),
+    )
     gathered = exchange(ymodes)
     modes, tile = pl.pallas_call(
         xmode_kernel,
         out_shape=(near(128, NT), near(NS, 8, 128)),
-        in_specs=[SMEM] * 5 + [VMEM] * 2,
+        in_specs=[VMEM] * 2,
         out_specs=(VMEM,) * 2,
         name="xmode",
-    )(segment_order, seg_disp, seg_gain, seg_sat, seg_kerr, hold(gathered), t["to_xmode"])
+    )(hold(gathered), near_tables["to_xmode"])
     shifted = pass_on(tile)
     modes = pl.pallas_call(
         disperse_kernel,
@@ -399,22 +404,21 @@
         scratch_shapes=[pltpu.VMEM((512, 256), F32)] * 2,
         cost_estimate=cost(6 * 4 * 512 * 256 * 256, 2**20),
         name="disperse",
-    )(hold(modes), hold(tile), t["w"], t["twiddle"], t["forward"], t["backward"])
+    )(
+        hold(modes), hold(tile),
+        *(near_tables[name] for name in ("w", "twiddle", "forward", "backward")),
+    )
     modes, shifted = lax.optimization_barrier((modes, shifted))
     modes = pass_on(modes)
     weights = exchange(shifted)
     factor = pl.pallas_call(
         lanczos_kernel,
         out_shape=near(2, 64, 128),
-        grid_spec=pltpu.PrefetchScalarGridSpec(
-            num_scalar_prefetch=1,
-            grid=(1,),
-            in_specs=[VMEM, VMEM, pl.BlockSpec((1, 64, 128), lambda i, s: (s[0], 0, 0))],
-            out_specs=VMEM,
-        ),
+        in_specs=[VMEM] * 2,
+        out_specs=VMEM,
         cost_estimate=cost(6 * 2 * 512 * 256 * 256, 2**20),
         name="lanczos",
-    )(shard, hold(weights), t["lam_all"], t["lam_own"])
+    )(hold(shifted), hold(weights))
     xback = pl.pallas_call(
         propagate_kernel,
         out_shape=near(NS, 8, NT),
@@ -422,7 +426,7 @@
         out_specs=VMEM,
         scratch_shapes=[pltpu.VMEM((128, 128), F32)],
         name="propagate",
-    )(hold(factor), hold(modes), t["from_xmode"])
+    )(hold(factor), hold(modes), near_tables["from_xmode"])
     rows = exchange(xback)
     result = pl.pallas_call(
         kerr_kernel,
@@ -433,8 +437,11 @@
         + [pltpu.VMEM((256, 256), F32)] * 2,
         name="kerr",
     )(
-        hold(shifted), hold(rows), t["from_ymode"], t["twiddle"], t["forward"], t["backward"],
-        t["raman"],
+        hold(shifted), hold(rows),
+        *(
+            near_tables[name]
+            for name in ("from_ymode", "twiddle", "forward", "backward", "raman")
+        ),
     )
     return result.reshape(seed_field.shape)
 

time: 66.3 us -> 62.4 us (0.941)
  blocking collectives: 13.3 us -> 42.9 us
  starting transfers between devices: 14.2 us -> 0.01 us
  waiting for transfers between devices: 21.3 us -> 7.22 us
  Pallas kernels: 16.2 us -> 11 us
    all_to_all x1 -> x3, blocking collectives: 13.3 us -> 42.9 us  [exchange(): lax.all_to_all(value, 'shard', split_axis=0, concat_axis=0, tiled=True)]
    all_to_all x2 -> x0, waiting for transfers between devices: 14.8 us -> none  [exchange(): lax.all_to_all(value, 'shard', split_axis=0, concat_axis=0, tiled=True)]
    all_to_all x2 -> x0, starting transfers between devices: 14.2 us -> none  [exchange(): lax.all_to_all(value, 'shard', split_axis=0, concat_axis=0, tiled=True)]
    pallas_call x1, Pallas kernels: 4.57 us -> 3.45 us  [per_device(): pl.pallas_call(kerr_kernel, out_shape=jax.ShapeDtypeStruct((128, NT), F32...]
    pallas_call x1, Pallas kernels: 2.97 us -> 1.92 us  [per_device(): pl.pallas_call(disperse_kernel, out_shape=near(128, NT), in_specs=[VMEM]...]
    pallas_call x1, Pallas kernels: 1.65 us -> 0.78 us  [per_device(): pl.pallas_call(xmode_kernel, out_shape=(near(128, NT), near(NS, 8, 128)),...]
    pallas_call x1, Pallas kernels: 1.43 us -> 0.6 us  [per_device(): pl.pallas_call(propagate_kernel, out_shape=near(NS, 8, NT), in_specs=[VME...]
    pallas_call x1, Pallas kernels: 2.45 us -> 1.7 us  [per_device(): pl.pallas_call(ymode_kernel, out_shape=near(NS, 72, 128), in_specs=[VMEM]...]
  transfers between devices with their start and end apart: 4 -> 2, of which waited for: 3 -> 1; matrix products, arithmetic and copies ran while one was open for 0% -> 0% of each run, Pallas kernels for 9% -> 7%
where the time goes in v4:
time: 62.4 us; the launch traced here: 62.1 us
  blocking collectives  42.9 us (69%)
  Pallas kernels  11 us (18%)
  waiting for transfers between devices  7.22 us (12%)
  between operations  0.75 us (1%)
    all_to_all x3, blocking collectives, exchange(): lax.all_to_all(value, 'shard', split_axis=0, concat_axis=0, tiled=True)  42.9 us
    ppermute x2, waiting for transfers between devices, pass_on(): lax.ppermute(value, 'blk', [(b, (b + 1) % count) for b in range(count)])  7.22 us
    pallas_call x1, Pallas kernels, per_device(): pl.pallas_call(kerr_kernel, out_shape=jax.ShapeDtypeStruct((128, NT), F32...  3.45 us
    pallas_call x1, Pallas kernels, per_device(): pl.pallas_call(lanczos_kernel, out_shape=near(2, 64, 128), in_specs=[VMEM...  2.56 us
    pallas_call x1, Pallas kernels, per_device(): pl.pallas_call(disperse_kernel, out_shape=near(128, NT), in_specs=[VMEM]...  1.92 us
    pallas_call x1, Pallas kernels, per_device(): pl.pallas_call(ymode_kernel, out_shape=near(NS, 72, 128), in_specs=[VMEM]...  1.7 us
  transfers between devices with their start and end apart: 2, of which 1 were waited for; matrix products, arithmetic and copies ran while one was open for 0% of the time, Pallas kernels for 7%

profile of v4, /device:TPU:8, one launch (start us, length us, event | category | flops | bytes accessed | tf_op | source)
XLA Modules:
  0.0 62.1 jit_solution(2187522029328902928)
XLA Ops:
  0.7 1.7 %ymode.1 = f32[16,72,128]{2,1,0:T(8,128)S(1)} custom-call(f32[128,1024]{1,0:T(8,128)} %bitcast.8, f32[128,128]{1,0:T(8,128)} %constant.20.clone.mat_ref, f32[16,128]{1,0:T(8,128)} %constant.24.clone.lam_ref, s32[1,1]{1,0:T(1,128)} %bitcast.7.kind_ref, f32[1,32]{1,0:T(1,128)} %bitcast.9, f32[1,32]{1,0:T(1,128)} %bitcast.10, f32[1,32]{1,0:T(1,128)} %bitcast.11, ...), custom_call_target="tpu_custom_call" | custom-call | tf_op jit(solution)/shard_map/ymode/pallas_call | solution.py:380
  2.4 0.0 copy-start.3
  2.4 18.2 %all_to_all.15.in_ref = f32[16,72,128]{2,1,0:T(8,128)S(1)} all-to-all(f32[16,72,128]{2,1,0:T(8,128)S(1)} %ymode.1), channel_id=1, replica_groups=mesh['blk'=32,'shard'=16] {'shard'}, dimensions={0} | all-to-all | bytes 1179648 | tf_op jit(solution)/shard_map/all_to_all | solution.py:367
  20.5 0.0 copy-done.3
  20.6 0.0 copy-start
  20.6 0.0 copy-start.1
  20.6 0.0 copy-start.5
  20.6 0.0 copy-start.7
  20.6 0.8 %xmode.1 = (f32[128,1024]{1,0:T(8,128)S(1)}, f32[16,8,128]{2,1,0:T(8,128)S(1)}) custom-call(f32[16,72,128]{2,1,0:T(8,128)S(1)} %all_to_all.15.in_ref, f32[128,128]{1,0:T(8,128)S(1)} %copy-done.3), custom_call_target="tpu_custom_call" | custom-call | tf_op jit(solution)/shard_map/xmode/pallas_call | solution.py:391
  21.4 0.0 collective-permute-start
  21.4 0.1 copy-done
  21.5 0.1 copy-done.1
  21.6 0.0 copy-done.5
  21.6 0.0 copy-done.7
  21.6 1.9 %disperse.1 = f32[128,1024]{1,0:T(8,128)S(1)} custom-call(f32[128,1024]{1,0:T(8,128)S(1)} %get-tuple-element.9.modes_ref, f32[16,8,128]{2,1,0:T(8,128)S(1)} %get-tuple-element.10.tile_ref, f32[8,128]{1,0:T(8,128)S(1)} %copy-done.7, f32[2,8,128]{2,1,0:T(8,128)S(1)} %copy-done.5, f32[256,256]{1,0:T(8,128)S(1)} %copy-done.1, f32[256,256]{1,0:T(8,128)S(1)} %copy-done), custom_call_target="tpu_custom_call" | custom-call | flops 805306368 | bytes 1048576 | tf_op jit(solution)/shard_map/disperse/pallas_call | solution.py:399
  23.5 7.2 %collective-permute-done.own_ref.tile_ref = f32[16,8,128]{2,1,0:T(8,128)S(1)} collective-permute-done((f32[16,8,128]{2,1,0:T(8,128)S(1)}, f32[16,8,128]{2,1,0:T(8,128)S(1)}, u32[]{:S(2)}, u32[]{:S(2)}) %collective-permute-start) | collective-permute-done | bytes 65568 | tf_op jit(solution)/shard_map/ppermute | solution.py:372
  30.7 0.0 collective-permute-start.1
  30.7 11.3 %all_to_all.16.weight_ref = f32[16,8,128]{2,1,0:T(8,128)S(1)} all-to-all(f32[16,8,128]{2,1,0:T(8,128)S(1)} %collective-permute-done.own_ref.tile_ref), channel_id=1, replica_groups=mesh['blk'=32,'shard'=16] {'shard'}, dimensions={0} | all-to-all | bytes 131072 | tf_op jit(solution)/shard_map/all_to_all | solution.py:367
  42.0 0.0 copy-start.2
  42.0 2.6 %lanczos.1.factor_ref = f32[2,64,128]{2,1,0:T(8,128)S(1)} custom-call(f32[16,8,128]{2,1,0:T(8,128)S(1)} %collective-permute-done.own_ref.tile_ref, f32[16,8,128]{2,1,0:T(8,128)S(1)} %all_to_all.16.weight_ref), custom_call_target="tpu_custom_call" | custom-call | flops 402653184 | bytes 1048576 | tf_op jit(solution)/shard_map/lanczos/pallas_call | solution.py:414
  44.6 0.0 collective-permute-done.1.modes_ref
  44.6 0.0 copy-done.2
  44.6 0.6 propagate.1
  45.2 0.0 copy-start.4
  45.2 0.0 copy-start.6
  45.2 13.4 %all_to_all.17.in_ref = f32[16,8,1024]{2,1,0:T(8,128)S(1)} all-to-all(f32[16,8,1024]{2,1,0:T(8,128)S(1)} %propagate.1), channel_id=1, replica_groups=mesh['blk'=32,'shard'=16] {'shard'}, dimensions={0} | all-to-all | bytes 1048576 | tf_op jit(solution)/shard_map/all_to_all | solution.py:367
  58.7 0.0 copy-done.4
  58.7 0.0 copy-done.6
  58.7 3.4 %kerr.1 = f32[128,1024]{1,0:T(8,128)} custom-call(f32[16,8,128]{2,1,0:T(8,128)S(1)} %collective-permute-done.own_ref.tile_ref, f32[16,8,1024]{2,1,0:T(8,128)S(1)} %all_to_all.17.in_ref, f32[128,128]{1,0:T(8,128)S(1)} %copy-done.4, f32[2,8,128]{2,1,0:T(8,128)S(1)} %copy-done.5, f32[256,256]{1,0:T(8,128)S(1)} %copy-done.1, f32[256,256]{1,0:T(8,128)S(1)} %copy-done, ...), custom_call_target="tpu_custom_call" | custom-call | tf_op jit(solution)/shard_map/kerr/pallas_call | solution.py:431
Async XLA Ops:
  2.4 18.2 %copy-start.3 = (f32[128,128]{1,0:T(8,128)S(1)}, f32[128,128]{1,0:T(8,128)}, u32[]{:S(2)}) copy-start(f32[128,128]{1,0:T(8,128)} %constant.22.clone.mat_ref) | copy-start | bytes 196612
  20.6 1.0 %copy-start = (f32[256,256]{1,0:T(8,128)S(1)}, f32[256,256]{1,0:T(8,128)}, u32[]{:S(2)}) copy-start(f32[256,256]{1,0:T(8,128)} %constant.26.clone.bwd_ref) | copy-start | bytes 786436
  20.6 1.0 %copy-start.1 = (f32[256,256]{1,0:T(8,128)S(1)}, f32[256,256]{1,0:T(8,128)}, u32[]{:S(2)}) copy-start(f32[256,256]{1,0:T(8,128)} %constant.25.clone.fwd_ref) | copy-start | bytes 786436
  20.6 1.0 %copy-start.5 = (f32[2,8,128]{2,1,0:T(8,128)S(1)}, f32[2,8,128]{2,1,0:T(8,128)}, u32[]{:S(2)}) copy-start(f32[2,8,128]{2,1,0:T(8,128)} %constant.27.clone.tw_ref) | copy-start | bytes 24580
  20.6 1.0 %copy-start.7 = (f32[8,128]{1,0:T(8,128)S(1)}, f32[8,128]{1,0:T(8,128)}, u32[]{:S(2)}) copy-start(f32[8,128]{1,0:T(8,128)} %constant.28.clone.w_ref) | copy-start | bytes 12292
  21.4 9.4 %collective-permute-start = (f32[16,8,128]{2,1,0:T(8,128)S(1)}, f32[16,8,128]{2,1,0:T(8,128)S(1)}, u32[]{:S(2)}, u32[]{:S(2)}) collective-permute-start(f32[16,8,128]{2,1,0:T(8,128)S(1)} %get-tuple-element.10.tile_ref), channel_id=1, source_target_pairs={{0,16},{16,32},{32,48},{48,64},{64,80},{80,96},{96,112},{112,128},... | collective-permute-start | bytes 196616 | tf_op jit(solution)/shard_map/ppermute | solution.py:372
  30.7 13.8 %collective-permute-start.1 = (f32[128,1024]{1,0:T(8,128)S(1)}, f32[128,1024]{1,0:T(8,128)S(1)}, u32[]{:S(2)}, u32[]{:S(2)}) collective-permute-start(f32[128,1024]{1,0:T(8,128)S(1)} %disperse.1), channel_id=1, source_target_pairs={{0,16},{16,32},{32,48},{48,64},{64,80},{80,96},{96,112},{112,128},... | collective-permute-start | bytes 1572872 | tf_op jit(solution)/shard_map/ppermute | solution.py:372
  42.0 2.6 %copy-start.2 = (f32[128,128]{1,0:T(8,128)S(1)}, f32[128,128]{1,0:T(8,128)}, u32[]{:S(2)}) copy-start(f32[128,128]{1,0:T(8,128)} %constant.23.clone.mat_ref) | copy-start | bytes 196612
  45.2 13.5 %copy-start.4 = (f32[128,128]{1,0:T(8,128)S(1)}, f32[128,128]{1,0:T(8,128)}, u32[]{:S(2)}) copy-start(f32[128,128]{1,0:T(8,128)} %constant.21.clone.mat_ref) | copy-start | bytes 196612
  45.2 13.5 %copy-start.6 = (f32[2,8,128]{2,1,0:T(8,128)S(1)}, f32[2,8,128]{2,1,0:T(8,128)}, u32[]{:S(2)}) copy-start(f32[2,8,128]{2,1,0:T(8,128)} %constant.29.clone.raman_ref) | copy-start | bytes 24580

commit v5 on v4

--- a/solution.py
+++ b/solution.py
@@ -75,12 +75,26 @@
         to_xmode=f32(to_xmode),
         from_xmode=f32(to_xmode.T),
         lam_all=f32(lam_all),
+        forward_split=split(f32(forward)),
+        backward_split=split(f32(backward)),
         forward=f32(forward),
         backward=f32(backward),
         twiddle=f32(np.stack([tw_cos, tw_sin])),
         w=f32(w),
         raman=f32(np.stack([ram_re, ram_im])),
     )
+
+
+def split(table):
+    high = table.astype(jnp.bfloat16)
+    return np.stack([high, (table - high.astype(np.float32)).astype(jnp.bfloat16)])
+
+
+def mm_split(a, b_ref):
+    high = a.astype(jnp.bfloat16)
+    low = (a - high.astype(F32)).astype(jnp.bfloat16)
+    dot = functools.partial(jnp.dot, preferred_element_type=F32)
+    return dot(high, b_ref[0]) + (dot(high, b_ref[1]) + dot(low, b_ref[0]))
 
 
 def mm(a, b):
@@ -176,7 +190,7 @@
         out_ref[d, 64:72, :] = jnp.where(row == 6, lam_ref[d : d + 1, :], side)
 
 
-def xmode_kernel(in_ref, mat_ref, modes_ref, tile_ref):
+def xmode_kernel(in_ref, mat_ref, modes_ref, side_ref, tile_ref):
     square = jnp.zeros((128, 128), F32)
     for c in range(NK):
         block = in_ref[:, 8 * c : 8 * c + 8, :].reshape(128, 128)
@@ -195,9 +209,29 @@
     for d in range(1, NS):
         energy = energy + in_ref[d, 64:72, :]
     row = lax.broadcasted_iota(jnp.int32, (8, 128), 0)
-    tile = jnp.where(row == 0, weight, jnp.where(row == 1, energy, side))
+    side_ref[...] = jnp.where(row == 1, energy, side)
+    lane = lax.broadcasted_iota(jnp.int32, (8, 128), 1)
+    tile = jnp.where(lane < 64, weight + pltpu.roll(weight, 64, 1), side[5:6, :])
     for d in range(NS):
-        tile_ref[d] = tile
+        tile_ref[d] = tile[0:1, :]
+
+
+def turn(angle):
+    count = jnp.floor(angle * np.float32(2.0 / np.pi) + 0.5)
+    x = angle - count * 1.5703125
+    x = x - count * 4.837512969970703e-4
+    x = x - count * 7.549789948768648e-8
+    x = jnp.clip(x, -0.8, 0.8)
+    z = x * x
+    sine = ((-1.9515295891e-4 * z + 8.3321608736e-3) * z - 1.6666654611e-1) * z * x + x
+    cosine = ((2.443315711809948e-5 * z - 1.388731625493765e-3) * z + 4.166664568298827e-2) * z
+    cosine = cosine * z - 0.5 * z + 1.0
+    quarter = count.astype(jnp.int32)
+    odd = (quarter & 1) == 1
+    c, s = jnp.where(odd, sine, cosine), jnp.where(odd, cosine, sine)
+    c = jnp.where(((quarter + 1) & 2) == 2, -c, c)
+    s = jnp.where((quarter & 2) == 2, -s, s)
+    return c, s
 
 
 def whole_sum(value):
@@ -205,7 +239,7 @@
 
 
 def disperse_kernel(
-    modes_ref, tile_ref, w_ref, tw_ref, fwd_ref, bwd_ref, out_ref, one, two
+    modes_ref, side_ref, w_ref, tw_ref, fwd_ref, bwd_ref, out_ref, one, two
 ):
 
     def load(part, r0, a):
@@ -214,9 +248,9 @@
     outer_forward(load, 64, tw_ref, one)
     two[...] = mm(one[...], fwd_ref[...])
 
-    energy = whole_sum(tile_ref[0, 1:2, :])
-    dispersion, gain_peak = tile_ref[0, 2:3, :], tile_ref[0, 3:4, :]
-    gain = gain_peak / (1.0 + energy / (NG * NG * NT) / tile_ref[0, 4:5, :])
+    energy = whole_sum(side_ref[1:2, :])
+    dispersion, gain_peak = side_ref[2:3, :], side_ref[3:4, :]
+    gain = gain_peak / (1.0 + energy / (NG * NG * NT) / side_ref[4:5, :])
     w = w_ref[...]
     relative = w / gain_width
     amplitude = jnp.exp(0.5 * gain / (1.0 + relative * relative) - loss_rate) * (1.0 / NT)
@@ -268,43 +302,54 @@
     return real, imag
 
 
-def lanczos_kernel(own_ref, weight_ref, factor_ref):
-    weight = weight_ref[:, 0, :]
-    lam = weight_ref[:, 6, :]
-    own = jnp.broadcast_to(own_ref[0, 6:7, :], (8, 128))
-    scale_zero = jnp.sqrt(whole_sum(weight) + epsilon)
-    vector = jnp.sqrt(weight) / scale_zero
-    poly = jnp.ones((8, 128), F32) / scale_zero
-    before_vector, before_poly, coupling = None, None, None
-    diagonals, couplings, polys = [], [], [poly]
+def mode_gains(weight, lam, own):
+    rest = jnp.sqrt(weight)
+    grown = jnp.ones((8, 128), F32)
+    diagonals, couplings, polys = [], [], []
     for step in range(KRYLOV):
-        image = lam * vector
+        spread = lam * rest
+        square = whole_sum(rest * rest) + epsilon
+        diagonal = whole_sum(spread * rest)
         if step:
-            image = image - coupling * before_vector
-        diagonal = whole_sum(vector * image)
+            overlap = whole_sum(rest * vector)
+        inverse = lax.rsqrt(square)
+        coupling = square * inverse
+        diagonal = diagonal * inverse * inverse
+        if step:
+            diagonal = diagonal - overlap
         diagonals.append(diagonal)
+        couplings.append(coupling)
+        poly = grown * inverse
+        polys.append(poly)
         if step + 1 < KRYLOV:
-            image = image - diagonal * vector
+            rest = rest * inverse
+            image = spread * inverse
             grown = own * poly
             if step:
-                grown = grown - coupling * before_poly
-            grown = grown - diagonal * poly
-            coupling = jnp.sqrt(whole_sum(image * image) + epsilon)
-            couplings.append(coupling)
-            before_vector, vector = vector, image / coupling
-            before_poly, poly = poly, grown / coupling
-            polys.append(poly)
-    real, imag = krylov_exp(diagonals, couplings)
-    for place, part in ((0, real), (1, imag)):
+                image = image - coupling * vector
+                grown = grown - coupling * before
+            vector, before = rest, poly
+            rest = image - diagonal * vector
+            grown = grown - diagonal * before
+    scale_zero = couplings[0]
+    real, imag = krylov_exp(diagonals, couplings[1:])
+    gains = []
+    for part in (real, imag):
         gain = part[0:1, 0:1] * polys[0]
         for j in range(1, KRYLOV):
             gain = gain + part[j : j + 1, 0:1] * polys[j]
-        gain = gain * scale_zero
-        factor_ref[place] = jnp.broadcast_to(gain[0:1, :], (128, 128)).T[0:64, :]
-
-
-def propagate_kernel(factor_ref, modes_ref, mat_ref, out_ref, scaled):
-    gain_re, gain_im = factor_ref[0], factor_ref[1]
+        gains.append(gain * scale_zero)
+    return gains
+
+
+def propagate_kernel(side_ref, weight_ref, lam_ref, modes_ref, mat_ref, out_ref, scaled):
+    own = jnp.broadcast_to(side_ref[6:7, :], (8, 128))
+    lane = lax.broadcasted_iota(jnp.int32, (NS, 128), 1)
+    weight = jnp.where(lane < 64, weight_ref[:, 0, :], 0.0)
+    gains = mode_gains(weight, lam_ref[...], own)
+    gain_re, gain_im = (
+        jnp.broadcast_to(gain[0:1, :], (128, 128)).T[0:64, :] for gain in gains
+    )
     for c in range(NK):
         a = modes_ref[0:64, c * 128 : (c + 1) * 128]
         b = modes_ref[64:128, c * 128 : (c + 1) * 128]
@@ -316,9 +361,9 @@
 
 def kerr_kernel(
     tile_ref, in_ref, mat_ref, tw_ref, fwd_ref, bwd_ref, raman_ref,
-    out_ref, field, delayed, one, two
+    out_ref, field, delayed, one, two, done, sems
 ):
-    kerr = tile_ref[0, 5:6, 0:1]
+    kerr = tile_ref[0, 0:1, 64:65]
     field[...] = mm(mat_ref[...], in_ref[...].reshape(128, NT))
 
     def load(side, r0, a):
@@ -328,9 +373,9 @@
         return re * re + im * im
 
     outer_forward(load, 32, tw_ref, one)
-    two[...] = mm(one[...], fwd_ref[...])
+    two[...] = mm_split(one[...], fwd_ref)
     filter_spectrum(two, 32, raman_ref[0], raman_ref[1])
-    one[...] = mm(two[...], bwd_ref[...])
+    one[...] = mm_split(two[...], bwd_ref)
 
     def store(r0, a, re, im):
         lanes = slice(a * NB, (a + 1) * NB)
@@ -339,16 +384,26 @@
 
     outer_backward(one, 32, tw_ref, store)
 
+    copies = []
     for r0 in range(0, 64, 8):
         re, im = field[r0 : r0 + 8, :], field[64 + r0 : 64 + r0 + 8, :]
         late = delayed[r0 : r0 + 8, :]
         rotation = kerr * ((1.0 - raman_share) * (re * re + im * im) + raman_share * late)
-        c, s = jnp.cos(rotation), jnp.sin(rotation)
-        out_ref[r0 : r0 + 8, :] = re * c - im * s
-        out_ref[64 + r0 : 64 + r0 + 8, :] = re * s + im * c
+        c, s = turn(rotation)
+        done[r0 : r0 + 8, :] = re * c - im * s
+        done[64 + r0 : 64 + r0 + 8, :] = re * s + im * c
+        if r0 % 16 == 8:
+            for lo in (r0 - 8, 64 + r0 - 8):
+                rows = pl.ds(lo, 16)
+                copy = pltpu.make_async_copy(done.at[rows], out_ref.at[rows], sems.at[lo // 16])
+                copy.start()
+                copies.append(copy)
+    for copy in copies:
+        copy.wait()
 
 
 VMEM = pl.BlockSpec(memory_space=pltpu.VMEM)
+HBM = pl.BlockSpec(memory_space=pltpu.HBM)
 
 
 def near(*shape):
@@ -388,11 +443,11 @@
         *(each.reshape(1, 32) for each in (seg_disp, seg_gain, seg_sat, seg_kerr)),
     )
     gathered = exchange(ymodes)
-    modes, tile = pl.pallas_call(
+    modes, side, tile = pl.pallas_call(
         xmode_kernel,
-        out_shape=(near(128, NT), near(NS, 8, 128)),
+        out_shape=(near(128, NT), near(8, 128), near(NS, 1, 128)),
         in_specs=[VMEM] * 2,
-        out_specs=(VMEM,) * 2,
+        out_specs=(VMEM,) * 3,
         name="xmode",
     )(hold(gathered), near_tables["to_xmode"])
     shifted = pass_on(tile)
@@ -405,42 +460,38 @@
         cost_estimate=cost(6 * 4 * 512 * 256 * 256, 2**20),
         name="disperse",
     )(
-        hold(modes), hold(tile),
+        hold(modes), hold(side),
         *(near_tables[name] for name in ("w", "twiddle", "forward", "backward")),
     )
     modes, shifted = lax.optimization_barrier((modes, shifted))
     modes = pass_on(modes)
     weights = exchange(shifted)
-    factor = pl.pallas_call(
-        lanczos_kernel,
-        out_shape=near(2, 64, 128),
-        in_specs=[VMEM] * 2,
-        out_specs=VMEM,
-        cost_estimate=cost(6 * 2 * 512 * 256 * 256, 2**20),
-        name="lanczos",
-    )(hold(shifted), hold(weights))
     xback = pl.pallas_call(
         propagate_kernel,
         out_shape=near(NS, 8, NT),
-        in_specs=[VMEM] * 3,
+        in_specs=[VMEM] * 5,
         out_specs=VMEM,
         scratch_shapes=[pltpu.VMEM((128, 128), F32)],
         name="propagate",
-    )(hold(factor), hold(modes), near_tables["from_xmode"])
+    )(
+        hold(side), hold(weights), near_tables["lam_all"], hold(modes),
+        near_tables["from_xmode"],
+    )
     rows = exchange(xback)
     result = pl.pallas_call(
         kerr_kernel,
         out_shape=jax.ShapeDtypeStruct((128, NT), F32),
         in_specs=[VMEM] * 7,
-        out_specs=VMEM,
+        out_specs=HBM,
         scratch_shapes=[pltpu.VMEM((128, NT), F32), pltpu.VMEM((64, NT), F32)]
-        + [pltpu.VMEM((256, 256), F32)] * 2,
+        + [pltpu.VMEM((256, 256), F32)] * 2
+        + [pltpu.VMEM((128, NT), F32), pltpu.SemaphoreType.DMA((8,))],
         name="kerr",
     )(
         hold(shifted), hold(rows),
         *(
             near_tables[name]
-            for name in ("from_ymode", "twiddle", "forward", "backward", "raman")
+            for name in ("from_ymode", "twiddle", "forward_split", "backward_split", "raman")
         ),
     )
     return result.reshape(seed_field.shape)

time: 62.4 us -> 59.7 us (0.957)
  Pallas kernels: 11 us -> 9.21 us
  waiting for transfers between devices: 7.22 us -> 6.08 us
    pallas_call x2 -> x1, Pallas kernels: 3.34 us -> 0.85 us  [per_device(): pl.pallas_call(xmode_kernel, out_shape=(near(128, NT), near(8, 128), near...]
    pallas_call x1, Pallas kernels: 0.6 us -> 2.34 us  [per_device(): pl.pallas_call(propagate_kernel, out_shape=near(NS, 8, NT), in_specs=[VME...]
    ppermute x2, waiting for transfers between devices: 7.22 us -> 6.08 us  [pass_on(): lax.ppermute(value, 'blk', [(b, (b + 1) % count) for b in range(count)])]
    pallas_call x1, Pallas kernels: 3.45 us -> 2.41 us  [per_device(): pl.pallas_call(kerr_kernel, out_shape=jax.ShapeDtypeStruct((128, NT), F32...]
  transfers between devices with their start and end apart: 2 -> 2, of which waited for: 1 -> 1; matrix products, arithmetic and copies ran while one was open for 0% -> 0% of each run, Pallas kernels for 7% -> 3%
where the time goes in v5:
time: 59.7 us; the launch traced here: 59.4 us
  blocking collectives  42.6 us (71%)
  Pallas kernels  9.21 us (15%)
  waiting for transfers between devices  6.08 us (10%)
  between operations  0.77 us (1%)
  local copies, waits for them, and re-layouts  0.76 us (1%)
    all_to_all x3, blocking collectives, exchange(): lax.all_to_all(value, 'shard', split_axis=0, concat_axis=0, tiled=True)  42.6 us
    ppermute x2, waiting for transfers between devices, pass_on(): lax.ppermute(value, 'blk', [(b, (b + 1) % count) for b in range(count)])  6.08 us
    pallas_call x1, Pallas kernels, per_device(): pl.pallas_call(kerr_kernel, out_shape=jax.ShapeDtypeStruct((128, NT), F32...  2.41 us
    pallas_call x1, Pallas kernels, per_device(): pl.pallas_call(propagate_kernel, out_shape=near(NS, 8, NT), in_specs=[VME...  2.34 us
    pallas_call x1, Pallas kernels, per_device(): pl.pallas_call(disperse_kernel, out_shape=near(128, NT), in_specs=[VMEM]...  1.91 us
    pallas_call x1, Pallas kernels, per_device(): pl.pallas_call(ymode_kernel, out_shape=near(NS, 72, 128), in_specs=[VMEM]...  1.7 us
  transfers between devices with their start and end apart: 2, of which 1 were waited for; matrix products, arithmetic and copies ran while one was open for 0% of the time, Pallas kernels for 3%

profile of v5, /device:TPU:8, one launch (start us, length us, event | category | flops | bytes accessed | tf_op | source)
XLA Modules:
  0.0 59.4 jit_solution(10396443641310437830)
XLA Ops:
  0.7 1.7 %ymode.1 = f32[16,72,128]{2,1,0:T(8,128)S(1)} custom-call(f32[128,1024]{1,0:T(8,128)} %bitcast.8, f32[128,128]{1,0:T(8,128)} %constant.24.clone.mat_ref, f32[16,128]{1,0:T(8,128)} %constant.28.clone.lam_ref, s32[1,1]{1,0:T(1,128)} %bitcast.7.kind_ref, f32[1,32]{1,0:T(1,128)} %bitcast.9, f32[1,32]{1,0:T(1,128)} %bitcast.10, f32[1,32]{1,0:T(1,128)} %bitcast.11, ...), custom_call_target="tpu_custom_call" | custom-call | tf_op jit(solution)/shard_map/ymode/pallas_call | solution.py:435
  2.4 0.0 copy-start.4
  2.4 18.2 %all_to_all.15.in_ref = f32[16,72,128]{2,1,0:T(8,128)S(1)} all-to-all(f32[16,72,128]{2,1,0:T(8,128)S(1)} %ymode.1), channel_id=1, replica_groups=mesh['blk'=32,'shard'=16] {'shard'}, dimensions={0} | all-to-all | bytes 1179648 | tf_op jit(solution)/shard_map/all_to_all | solution.py:422
  20.5 0.0 copy-done.4
  20.6 0.0 copy-start.6
  20.6 0.0 copy-start.8
  20.6 0.0 copy-start.9
  20.6 0.9 %xmode.1 = (f32[128,1024]{1,0:T(8,128)S(1)}, f32[8,128]{1,0:T(8,128)S(1)}, f32[16,1,128]{2,1,0:T(1,128)S(1)}) custom-call(f32[16,72,128]{2,1,0:T(8,128)S(1)} %all_to_all.15.in_ref, f32[128,128]{1,0:T(8,128)S(1)} %copy-done.4), custom_call_target="tpu_custom_call" | custom-call | tf_op jit(solution)/shard_map/xmode/pallas_call | solution.py:446
  21.4 0.0 copy-start.10
  21.4 0.0 collective-permute-start
  21.4 0.0 copy-done.6
  21.5 0.1 copy-done.8
  21.5 0.1 copy-done.9
  21.6 0.6 copy-done.10
  22.2 0.0 copy-start.3
  22.2 1.9 %disperse.1 = f32[128,1024]{1,0:T(8,128)S(1)} custom-call(f32[128,1024]{1,0:T(8,128)S(1)} %get-tuple-element.10.modes_ref, f32[8,128]{1,0:T(8,128)S(1)} %get-tuple-element.11.side_ref, f32[8,128]{1,0:T(8,128)S(1)} %copy-done.10, f32[2,8,128]{2,1,0:T(8,128)S(1)} %copy-done.6, f32[256,256]{1,0:T(8,128)S(1)} %copy-done.9, f32[256,256]{1,0:T(8,128)S(1)} %copy-done.8), custom_call_target="tpu_custom_call" | custom-call | flops 805306368 | bytes 1048576 | tf_op jit(solution)/shard_map/disperse/pallas_call | solution.py:454
  24.1 0.0 copy-start.5
  24.1 6.1 %collective-permute-done.tile_ref = f32[16,1,128]{2,1,0:T(1,128)S(1)} collective-permute-done((f32[16,1,128]{2,1,0:T(1,128)S(1)}, f32[16,1,128]{2,1,0:T(1,128)S(1)}, u32[]{:S(2)}, u32[]{:S(2)}) %collective-permute-start) | collective-permute-done | bytes 8224 | tf_op jit(solution)/shard_map/ppermute | solution.py:427
  30.2 0.0 collective-permute-start.1
  30.2 11.2 %all_to_all.16.weight_ref = f32[16,1,128]{2,1,0:T(1,128)S(1)} all-to-all(f32[16,1,128]{2,1,0:T(1,128)S(1)} %collective-permute-done.tile_ref), channel_id=1, replica_groups=mesh['blk'=32,'shard'=16] {'shard'}, dimensions={0} | all-to-all | bytes 16384 | tf_op jit(solution)/shard_map/all_to_all | solution.py:422
  41.3 0.0 collective-permute-done.1.modes_ref
  41.3 0.0 copy-done.3
  41.3 0.0 copy-done.5
  41.4 2.3 %propagate.1 = f32[16,8,1024]{2,1,0:T(8,128)S(1)} custom-call(f32[8,128]{1,0:T(8,128)S(1)} %get-tuple-element.11.side_ref, f32[16,1,128]{2,1,0:T(1,128)S(1)} %all_to_all.16.weight_ref, f32[16,128]{1,0:T(8,128)S(1)} %copy-done.5, f32[128,1024]{1,0:T(8,128)S(1)} %collective-permute-done.1.modes_ref, f32[128,128]{1,0:T(8,128)S(1)} %copy-done.3), custom_call_target="tpu_custom_call" | custom-call | tf_op jit(solution)/shard_map/propagate/pallas_call | solution.py:469
  43.7 0.0 copy-start
  43.7 0.0 copy-start.1
  43.7 0.0 copy-start.2
  43.7 0.0 copy-start.7
  43.8 13.2 %all_to_all.17.in_ref = f32[16,8,1024]{2,1,0:T(8,128)S(1)} all-to-all(f32[16,8,1024]{2,1,0:T(8,128)S(1)} %propagate.1), channel_id=1, replica_groups=mesh['blk'=32,'shard'=16] {'shard'}, dimensions={0} | all-to-all | bytes 1048576 | tf_op jit(solution)/shard_map/all_to_all | solution.py:422
  57.0 0.0 copy-done
  57.0 0.0 copy-done.1
  57.0 0.0 copy-done.2
  57.0 0.0 copy-done.7
  57.0 2.4 %kerr.1 = f32[128,1024]{1,0:T(8,128)} custom-call(f32[16,1,128]{2,1,0:T(1,128)S(1)} %collective-permute-done.tile_ref, f32[16,8,1024]{2,1,0:T(8,128)S(1)} %all_to_all.17.in_ref, f32[128,128]{1,0:T(8,128)S(1)} %copy-done.2, f32[2,8,128]{2,1,0:T(8,128)S(1)} %copy-done.6, bf16[2,256,256]{2,1,0:T(8,128)(2,1)S(1)} %copy-done.1, bf16[2,256,256]{2,1,0:T(8,128)(2,1)S(1)} %copy-done, ...), custom_call_target="tpu_custom_call" | custom-call | tf_op jit(solution)/shard_map/kerr/pallas_call | solution.py:481
Async XLA Ops:
  2.4 18.2 %copy-start.4 = (f32[128,128]{1,0:T(8,128)S(1)}, f32[128,128]{1,0:T(8,128)}, u32[]{:S(2)}) copy-start(f32[128,128]{1,0:T(8,128)} %constant.26.clone.mat_ref) | copy-start | bytes 196612
  20.6 0.9 %copy-start.6 = (f32[2,8,128]{2,1,0:T(8,128)S(1)}, f32[2,8,128]{2,1,0:T(8,128)}, u32[]{:S(2)}) copy-start(f32[2,8,128]{2,1,0:T(8,128)} %constant.33.clone.tw_ref) | copy-start | bytes 24580
  20.6 1.0 %copy-start.8 = (f32[256,256]{1,0:T(8,128)S(1)}, f32[256,256]{1,0:T(8,128)}, u32[]{:S(2)}) copy-start(f32[256,256]{1,0:T(8,128)} %constant.32.clone.bwd_ref) | copy-start | bytes 786436
  20.6 1.0 %copy-start.9 = (f32[256,256]{1,0:T(8,128)S(1)}, f32[256,256]{1,0:T(8,128)}, u32[]{:S(2)}) copy-start(f32[256,256]{1,0:T(8,128)} %constant.31.clone.fwd_ref) | copy-start | bytes 786436
  21.4 0.7 %copy-start.10 = (f32[8,128]{1,0:T(8,128)S(1)}, f32[8,128]{1,0:T(8,128)}, u32[]{:S(2)}) copy-start(f32[8,128]{1,0:T(8,128)} %constant.34.clone.w_ref) | copy-start | bytes 12292
  21.4 8.8 %collective-permute-start = (f32[16,1,128]{2,1,0:T(1,128)S(1)}, f32[16,1,128]{2,1,0:T(1,128)S(1)}, u32[]{:S(2)}, u32[]{:S(2)}) collective-permute-start(f32[16,1,128]{2,1,0:T(1,128)S(1)} %get-tuple-element.12), channel_id=1, source_target_pairs={{0,16},{16,32},{32,48},{48,64},{64,80},{80,96},{96,112},{112,128},... | collective-permute-start | bytes 24584 | tf_op jit(solution)/shard_map/ppermute | solution.py:427
  22.2 19.2 %copy-start.3 = (f32[128,128]{1,0:T(8,128)S(1)}, f32[128,128]{1,0:T(8,128)}, u32[]{:S(2)}) copy-start(f32[128,128]{1,0:T(8,128)} %constant.27.clone.mat_ref) | copy-start | bytes 196612
  24.1 17.3 %copy-start.5 = (f32[16,128]{1,0:T(8,128)S(1)}, f32[16,128]{1,0:T(8,128)}, u32[]{:S(2)}) copy-start(f32[16,128]{1,0:T(8,128)} %constant.28.clone.lam_ref) | copy-start | bytes 24580
  30.2 11.2 %collective-permute-start.1 = (f32[128,1024]{1,0:T(8,128)S(1)}, f32[128,1024]{1,0:T(8,128)S(1)}, u32[]{:S(2)}, u32[]{:S(2)}) collective-permute-start(f32[128,1024]{1,0:T(8,128)S(1)} %disperse.1), channel_id=1, source_target_pairs={{0,16},{16,32},{32,48},{48,64},{64,80},{80,96},{96,112},{112,128},... | collective-permute-start | bytes 1572872 | tf_op jit(solution)/shard_map/ppermute | solution.py:427
  43.7 13.3 %copy-start = (bf16[2,256,256]{2,1,0:T(8,128)(2,1)S(1)}, bf16[2,256,256]{2,1,0:T(8,128)(2,1)}, u32[]{:S(2)}) copy-start(bf16[2,256,256]{2,1,0:T(8,128)(2,1)} %constant.30.clone.bwd_ref) | copy-start | bytes 786436
  43.7 13.3 %copy-start.1 = (bf16[2,256,256]{2,1,0:T(8,128)(2,1)S(1)}, bf16[2,256,256]{2,1,0:T(8,128)(2,1)}, u32[]{:S(2)}) copy-start(bf16[2,256,256]{2,1,0:T(8,128)(2,1)} %constant.29.clone.fwd_ref) | copy-start | bytes 786436
  43.7 13.3 %copy-start.2 = (f32[128,128]{1,0:T(8,128)S(1)}, f32[128,128]{1,0:T(8,128)}, u32[]{:S(2)}) copy-start(f32[128,128]{1,0:T(8,128)} %constant.25.clone.mat_ref) | copy-start | bytes 196612
  43.7 13.2 %copy-start.7 = (f32[2,8,128]{2,1,0:T(8,128)S(1)}, f32[2,8,128]{2,1,0:T(8,128)}, u32[]{:S(2)}) copy-start(f32[2,8,128]{2,1,0:T(8,128)} %constant.35.clone.raman_ref) | copy-start | bytes 24580

commit v6 on v5

--- a/solution.py
+++ b/solution.py
@@ -1,4 +1,5 @@
 import functools
+import math
 
 import jax
 import jax.numpy as jnp
@@ -9,10 +10,12 @@
 from jax.sharding import PartitionSpec as P
 
 KRYLOV = 8
+EXPANDED = 5
 NS = 16
 NG = 32
 NT = 1024
 NK = 8
+WIDE = 2
 NB = 128
 
 epsilon = 1e-06
@@ -70,24 +73,44 @@
 
     f32 = lambda a: np.ascontiguousarray(a, dtype=np.float32)
     return dict(
-        to_ymode=f32(to_ymode),
-        from_ymode=f32(to_ymode.T),
-        to_xmode=f32(to_xmode),
-        from_xmode=f32(to_xmode.T),
+        to_ymode=widen(f32(to_ymode)),
+        from_ymode=widen(f32(to_ymode.T)),
+        to_xmode=widen(f32(to_xmode)),
+        from_xmode=widen(f32(to_xmode.T)),
         lam_all=f32(lam_all),
         forward_split=split(f32(forward)),
         backward_split=split(f32(backward)),
         forward=f32(forward),
         backward=f32(backward),
-        twiddle=f32(np.stack([tw_cos, tw_sin])),
-        w=f32(w),
-        raman=f32(np.stack([ram_re, ram_im])),
+        lines=f32(np.stack([tw_cos, tw_sin, w, ram_re, ram_im])),
     )
 
 
 def split(table):
     high = table.astype(jnp.bfloat16)
     return np.stack([high, (table - high.astype(np.float32)).astype(jnp.bfloat16)])
+
+
+def parts_of(value):
+    high = value.astype(jnp.bfloat16)
+    rest = value - high.astype(F32)
+    middle = rest.astype(jnp.bfloat16)
+    low = (rest - middle.astype(F32)).astype(jnp.bfloat16)
+    return high, middle, low
+
+
+def widen(table):
+    high = table.astype(jnp.bfloat16)
+    rest = table - high.astype(np.float32)
+    middle = rest.astype(jnp.bfloat16)
+    low = (rest - middle.astype(np.float32)).astype(jnp.bfloat16)
+    return np.concatenate([high, middle, low, high, middle, high], axis=1)
+
+
+def mm_wide(table, b):
+    high, middle, low = parts_of(b)
+    stacked = jnp.concatenate([high, high, high, middle, middle, low], axis=0)
+    return jnp.dot(table, stacked, preferred_element_type=F32)
 
 
 def mm_split(a, b_ref):
@@ -173,13 +196,16 @@
     seed_ref, mat_ref, lam_ref, kind_ref, disp_ref, gain_ref, sat_ref, kerr_ref, out_ref
 ):
     total = jnp.zeros((8, 128), F32)
-    for c in range(NK):
-        block = seed_ref[:, c * 128 : (c + 1) * 128]
+    for c0 in range(0, NK, WIDE):
+        block = seed_ref[:, c0 * 128 : (c0 + WIDE) * 128]
         square = block * block
-        for r in range(16):
-            total = total + square[8 * r : 8 * r + 8, :]
-        modes = mm(mat_ref[...], block)
-        out_ref[:, 8 * c : 8 * c + 8, :] = modes.reshape(NS, 8, 128)
+        modes = mm_wide(mat_ref[...], block)
+        for c in range(WIDE):
+            lanes = slice(c * 128, c * 128 + 128)
+            for r in range(16):
+                total = total + square[8 * r : 8 * r + 8, lanes]
+            place = 8 * (c0 + c)
+            out_ref[:, place : place + 8, :] = modes[:, lanes].reshape(NS, 8, 128)
     row = lax.broadcasted_iota(jnp.int32, (8, 128), 0)
     chosen = lax.broadcasted_iota(jnp.int32, (1, 32), 1) == kind_ref[...]
     side = jnp.broadcast_to(jnp.sum(total, axis=0, keepdims=True), (8, 128))
@@ -192,11 +218,15 @@
 
 def xmode_kernel(in_ref, mat_ref, modes_ref, side_ref, tile_ref):
     square = jnp.zeros((128, 128), F32)
-    for c in range(NK):
-        block = in_ref[:, 8 * c : 8 * c + 8, :].reshape(128, 128)
-        modes = mm(mat_ref[...], block)
-        modes_ref[:, c * 128 : (c + 1) * 128] = modes
-        square = square + modes * modes
+    for c0 in range(0, NK, WIDE):
+        block = jnp.concatenate(
+            [in_ref[:, 8 * c : 8 * c + 8, :].reshape(128, 128) for c in range(c0, c0 + WIDE)],
+            axis=1,
+        )
+        modes = mm_wide(mat_ref[...], block)
+        modes_ref[:, c0 * 128 : (c0 + WIDE) * 128] = modes
+        for c in range(WIDE):
+            square = square + modes[:, c * 128 : c * 128 + 128] ** 2
     weight = lax.dot_general(
         jnp.ones((8, 128), F32),
         square,
@@ -239,7 +269,7 @@
 
 
 def disperse_kernel(
-    modes_ref, side_ref, w_ref, tw_ref, fwd_ref, bwd_ref, out_ref, one, two
+    modes_ref, side_ref, tw_ref, fwd_ref, bwd_ref, out_ref, one, two
 ):
 
     def load(part, r0, a):
@@ -251,7 +281,7 @@
     energy = whole_sum(side_ref[1:2, :])
     dispersion, gain_peak = side_ref[2:3, :], side_ref[3:4, :]
     gain = gain_peak / (1.0 + energy / (NG * NG * NT) / side_ref[4:5, :])
-    w = w_ref[...]
+    w = tw_ref[2]
     relative = w / gain_width
     amplitude = jnp.exp(0.5 * gain / (1.0 + relative * relative) - loss_rate) * (1.0 / NT)
     angle = disp_scale * dispersion * w * w
@@ -273,11 +303,20 @@
     return total
 
 
+def expanded_ratios():
+    series = np.array([1.0 / math.factorial(k) for k in range(taylor_terms + 1)])
+    series = series / 2.0 ** (EXPANDED * np.arange(taylor_terms + 1))
+    for _ in range(EXPANDED):
+        series = np.convolve(series, series)
+    series = series[series >= np.finfo(np.float32).tiny]
+    return [float(ratio) for ratio in series[1:] / series[:-1]]
+
+
 def krylov_exp(diagonals, couplings):
     row = lax.broadcasted_iota(jnp.int32, (8, 128), 0)
     lane = lax.broadcasted_iota(jnp.int32, (8, 128), 1)
     zero = jnp.zeros((8, 128), F32)
-    scale = step_length / 2.0**squarings
+    scale = step_length / 2.0 ** (squarings - EXPANDED)
     mid, low, high = zero, zero, zero
     for j in range(KRYLOV):
         mid = jnp.where(row == j, diagonals[j] * scale, mid)
@@ -286,15 +325,15 @@
             low = jnp.where(row == j + 1, couplings[j] * scale, low)
     term = jnp.where(row == lane, 1.0, 0.0).astype(F32)
     real, imag = term, zero
-    for order in range(1, taylor_terms + 1):
+    for order, ratio in enumerate(expanded_ratios(), 1):
         term = mid * term + low * pltpu.roll(term, 1, 0) + high * pltpu.roll(term, 7, 0)
-        term = term * (1.0 / order)
+        term = term * ratio
         signed = -term if order % 4 in (2, 3) else term
         if order % 2:
             imag = imag + signed
         else:
             real = real + signed
-    for _ in range(squarings):
+    for _ in range(squarings - EXPANDED):
         real, imag = (
             small_product(real, real) - small_product(imag, imag),
             2.0 * small_product(real, imag),
@@ -350,21 +389,23 @@
     gain_re, gain_im = (
         jnp.broadcast_to(gain[0:1, :], (128, 128)).T[0:64, :] for gain in gains
     )
-    for c in range(NK):
-        a = modes_ref[0:64, c * 128 : (c + 1) * 128]
-        b = modes_ref[64:128, c * 128 : (c + 1) * 128]
-        scaled[0:64, :] = gain_re * a - gain_im * b
-        scaled[64:128, :] = gain_im * a + gain_re * b
-        back = mm(mat_ref[...], scaled[...])
-        out_ref[:, :, c * 128 : (c + 1) * 128] = back.reshape(NS, 8, 128)
+    for c0 in range(0, NK, WIDE):
+        for c in range(c0, c0 + WIDE):
+            lanes = slice(c * 128, c * 128 + 128)
+            a, b = modes_ref[0:64, lanes], modes_ref[64:128, lanes]
+            scaled[0:64, lanes] = gain_re * a - gain_im * b
+            scaled[64:128, lanes] = gain_im * a + gain_re * b
+        lanes = slice(c0 * 128, (c0 + WIDE) * 128)
+        back = mm_wide(mat_ref[...], scaled[:, lanes])
+        out_ref[:, :, lanes] = back.reshape(NS, 8, WIDE * 128)
 
 
 def kerr_kernel(
-    tile_ref, in_ref, mat_ref, tw_ref, fwd_ref, bwd_ref, raman_ref,
+    tile_ref, in_ref, mat_ref, tw_ref, fwd_ref, bwd_ref,
     out_ref, field, delayed, one, two, done, sems
 ):
     kerr = tile_ref[0, 0:1, 64:65]
-    field[...] = mm(mat_ref[...], in_ref[...].reshape(128, NT))
+    field[...] = mm_wide(mat_ref[...], in_ref[...].reshape(128, NT))
 
     def load(side, r0, a):
         lanes = slice(a * NB, (a + 1) * NB)
@@ -374,7 +415,7 @@
 
     outer_forward(load, 32, tw_ref, one)
     two[...] = mm_split(one[...], fwd_ref)
-    filter_spectrum(two, 32, raman_ref[0], raman_ref[1])
+    filter_spectrum(two, 32, tw_ref[3], tw_ref[4])
     one[...] = mm_split(two[...], bwd_ref)
 
     def store(r0, a, re, im):
@@ -454,14 +495,14 @@
     modes = pl.pallas_call(
         disperse_kernel,
         out_shape=near(128, NT),
-        in_specs=[VMEM] * 6,
+        in_specs=[VMEM] * 5,
         out_specs=VMEM,
         scratch_shapes=[pltpu.VMEM((512, 256), F32)] * 2,
         cost_estimate=cost(6 * 4 * 512 * 256 * 256, 2**20),
         name="disperse",
     )(
         hold(modes), hold(side),
-        *(near_tables[name] for name in ("w", "twiddle", "forward", "backward")),
+        *(near_tables[name] for name in ("lines", "forward", "backward")),
     )
     modes, shifted = lax.optimization_barrier((modes, shifted))
     modes = pass_on(modes)
@@ -471,7 +512,7 @@
         out_shape=near(NS, 8, NT),
         in_specs=[VMEM] * 5,
         out_specs=VMEM,
-        scratch_shapes=[pltpu.VMEM((128, 128), F32)],
+        scratch_shapes=[pltpu.VMEM((128, NT), F32)],
         name="propagate",
     )(
         hold(side), hold(weights), near_tables["lam_all"], hold(modes),
@@ -481,7 +522,7 @@
     result = pl.pallas_call(
         kerr_kernel,
         out_shape=jax.ShapeDtypeStruct((128, NT), F32),
-        in_specs=[VMEM] * 7,
+        in_specs=[VMEM] * 6,
         out_specs=HBM,
         scratch_shapes=[pltpu.VMEM((128, NT), F32), pltpu.VMEM((64, NT), F32)]
         + [pltpu.VMEM((256, 256), F32)] * 2
@@ -491,7 +532,7 @@
         hold(shifted), hold(rows),
         *(
             near_tables[name]
-            for name in ("from_ymode", "twiddle", "forward_split", "backward_split", "raman")
+            for name in ("from_ymode", "lines", "forward_split", "backward_split")
         ),
     )
     return result.reshape(seed_field.shape)

time: 59.7 us -> 58.7 us (0.983)
  Pallas kernels: 9.21 us -> 8.31 us
where the time goes in v6:
time: 58.7 us; the launch traced here: 58.4 us
  blocking collectives  42.5 us (72%)
  Pallas kernels  8.31 us (14%)
  waiting for transfers between devices  6.56 us (11%)
  between operations  0.74 us (1%)
    all_to_all x3, blocking collectives, exchange(): lax.all_to_all(value, 'shard', split_axis=0, concat_axis=0, tiled=True)  42.5 us
    ppermute x2, waiting for transfers between devices, pass_on(): lax.ppermute(value, 'blk', [(b, (b + 1) % count) for b in range(count)])  6.56 us
    pallas_call x1, Pallas kernels, per_device(): pl.pallas_call(kerr_kernel, out_shape=jax.ShapeDtypeStruct((128, NT), F32...  2.22 us
    pallas_call x1, Pallas kernels, per_device(): pl.pallas_call(disperse_kernel, out_shape=near(128, NT), in_specs=[VMEM]...  1.91 us
    pallas_call x1, Pallas kernels, per_device(): pl.pallas_call(propagate_kernel, out_shape=near(NS, 8, NT), in_specs=[VME...  1.79 us
    pallas_call x1, Pallas kernels, per_device(): pl.pallas_call(ymode_kernel, out_shape=near(NS, 72, 128), in_specs=[VMEM]...  1.61 us
  transfers between devices with their start and end apart: 2, of which 1 were waited for; matrix products, arithmetic and copies ran while one was open for 0% of the time, Pallas kernels for 3%

profile of v6, /device:TPU:8, one launch (start us, length us, event | category | flops | bytes accessed | tf_op | source)
XLA Modules:
  0.0 58.4 jit_solution(9842778526202781074)
XLA Ops:
  0.7 1.6 %ymode.1 = f32[16,72,128]{2,1,0:T(8,128)S(1)} custom-call(f32[128,1024]{1,0:T(8,128)} %bitcast.8, bf16[128,768]{1,0:T(8,128)(2,1)} %constant.20.clone.mat_ref, f32[16,128]{1,0:T(8,128)} %constant.24.clone.lam_ref, s32[1,1]{1,0:T(1,128)} %bitcast.7.kind_ref, f32[1,32]{1,0:T(1,128)} %bitcast.9, f32[1,32]{1,0:T(1,128)} %bitcast.10, f32[1,32]{1,0:T(1,128)} %bitcast.11, ...), custom_call_target="tpu_custom_call" | custom-call | tf_op jit(solution)/shard_map/ymode/pallas_call | solution.py:476
  2.3 0.0 copy-start.4
  2.3 18.2 %all_to_all.15.in_ref = f32[16,72,128]{2,1,0:T(8,128)S(1)} all-to-all(f32[16,72,128]{2,1,0:T(8,128)S(1)} %ymode.1), channel_id=1, replica_groups=mesh['blk'=32,'shard'=16] {'shard'}, dimensions={0} | all-to-all | bytes 1179648 | tf_op jit(solution)/shard_map/all_to_all | solution.py:463
  20.4 0.0 copy-done.4
  20.5 0.0 copy-start.6
  20.5 0.0 copy-start.7
  20.5 0.0 copy-start.8
  20.5 0.8 %xmode.1 = (f32[128,1024]{1,0:T(8,128)S(1)}, f32[8,128]{1,0:T(8,128)S(1)}, f32[16,1,128]{2,1,0:T(1,128)S(1)}) custom-call(f32[16,72,128]{2,1,0:T(8,128)S(1)} %all_to_all.15.in_ref, bf16[128,768]{1,0:T(8,128)(2,1)S(1)} %copy-done.4), custom_call_target="tpu_custom_call" | custom-call | tf_op jit(solution)/shard_map/xmode/pallas_call | solution.py:487
  21.2 0.0 collective-permute-start
  21.2 0.0 copy-done.6
  21.3 0.2 copy-done.7
  21.4 0.1 copy-done.8
  21.5 0.0 copy-start.3
  21.5 1.9 %disperse.1 = f32[128,1024]{1,0:T(8,128)S(1)} custom-call(f32[128,1024]{1,0:T(8,128)S(1)} %get-tuple-element.10.modes_ref, f32[8,128]{1,0:T(8,128)S(1)} %get-tuple-element.11.side_ref, f32[5,8,128]{2,1,0:T(8,128)S(1)} %copy-done.6, f32[256,256]{1,0:T(8,128)S(1)} %copy-done.8, f32[256,256]{1,0:T(8,128)S(1)} %copy-done.7), custom_call_target="tpu_custom_call" | custom-call | flops 805306368 | bytes 1048576 | tf_op jit(solution)/shard_map/disperse/pallas_call | solution.py:495
  23.4 0.0 copy-start.5
  23.4 6.6 %collective-permute-done.tile_ref = f32[16,1,128]{2,1,0:T(1,128)S(1)} collective-permute-done((f32[16,1,128]{2,1,0:T(1,128)S(1)}, f32[16,1,128]{2,1,0:T(1,128)S(1)}, u32[]{:S(2)}, u32[]{:S(2)}) %collective-permute-start) | collective-permute-done | bytes 8224 | tf_op jit(solution)/shard_map/ppermute | solution.py:468
  30.0 0.0 collective-permute-start.1
  30.0 11.2 %all_to_all.16.weight_ref = f32[16,1,128]{2,1,0:T(1,128)S(1)} all-to-all(f32[16,1,128]{2,1,0:T(1,128)S(1)} %collective-permute-done.tile_ref), channel_id=1, replica_groups=mesh['blk'=32,'shard'=16] {'shard'}, dimensions={0} | all-to-all | bytes 16384 | tf_op jit(solution)/shard_map/all_to_all | solution.py:463
  41.1 0.0 collective-permute-done.1.modes_ref
  41.2 0.0 copy-done.3
  41.2 0.0 copy-done.5
  41.2 1.8 %propagate.1 = f32[16,8,1024]{2,1,0:T(8,128)S(1)} custom-call(f32[8,128]{1,0:T(8,128)S(1)} %get-tuple-element.11.side_ref, f32[16,1,128]{2,1,0:T(1,128)S(1)} %all_to_all.16.weight_ref, f32[16,128]{1,0:T(8,128)S(1)} %copy-done.5, f32[128,1024]{1,0:T(8,128)S(1)} %collective-permute-done.1.modes_ref, bf16[128,768]{1,0:T(8,128)(2,1)S(1)} %copy-done.3), custom_call_target="tpu_custom_call" | custom-call | tf_op jit(solution)/shard_map/propagate/pallas_call | solution.py:510
  43.0 0.0 copy-start
  43.0 0.0 copy-start.1
  43.0 0.0 copy-start.2
  43.0 13.2 %all_to_all.17.in_ref = f32[16,8,1024]{2,1,0:T(8,128)S(1)} all-to-all(f32[16,8,1024]{2,1,0:T(8,128)S(1)} %propagate.1), channel_id=1, replica_groups=mesh['blk'=32,'shard'=16] {'shard'}, dimensions={0} | all-to-all | bytes 1048576 | tf_op jit(solution)/shard_map/all_to_all | solution.py:463
  56.2 0.0 copy-done
  56.2 0.0 copy-done.1
  56.2 0.0 copy-done.2
  56.2 2.2 %kerr.1 = f32[128,1024]{1,0:T(8,128)} custom-call(f32[16,1,128]{2,1,0:T(1,128)S(1)} %collective-permute-done.tile_ref, f32[16,8,1024]{2,1,0:T(8,128)S(1)} %all_to_all.17.in_ref, bf16[128,768]{1,0:T(8,128)(2,1)S(1)} %copy-done.2, f32[5,8,128]{2,1,0:T(8,128)S(1)} %copy-done.6, bf16[2,256,256]{2,1,0:T(8,128)(2,1)S(1)} %copy-done.1, bf16[2,256,256]{2,1,0:T(8,128)(2,1)S(1)} %copy-done), custom_call_target="tpu_custom_call" | custom-call | tf_op jit(solution)/shard_map/kerr/pallas_call | solution.py:522
Async XLA Ops:
  2.3 18.2 %copy-start.4 = (bf16[128,768]{1,0:T(8,128)(2,1)S(1)}, bf16[128,768]{1,0:T(8,128)(2,1)}, u32[]{:S(2)}) copy-start(bf16[128,768]{1,0:T(8,128)(2,1)} %constant.22.clone.mat_ref) | copy-start | bytes 589828
  20.5 0.8 %copy-start.6 = (f32[5,8,128]{2,1,0:T(8,128)S(1)}, f32[5,8,128]{2,1,0:T(8,128)}, u32[]{:S(2)}) copy-start(f32[5,8,128]{2,1,0:T(8,128)} %constant.29.clone.tw_ref) | copy-start | bytes 61444
  20.5 1.0 %copy-start.7 = (f32[256,256]{1,0:T(8,128)S(1)}, f32[256,256]{1,0:T(8,128)}, u32[]{:S(2)}) copy-start(f32[256,256]{1,0:T(8,128)} %constant.28.clone.bwd_ref) | copy-start | bytes 786436
  20.5 1.0 %copy-start.8 = (f32[256,256]{1,0:T(8,128)S(1)}, f32[256,256]{1,0:T(8,128)}, u32[]{:S(2)}) copy-start(f32[256,256]{1,0:T(8,128)} %constant.27.clone.fwd_ref) | copy-start | bytes 786436
  21.2 8.7 %collective-permute-start = (f32[16,1,128]{2,1,0:T(1,128)S(1)}, f32[16,1,128]{2,1,0:T(1,128)S(1)}, u32[]{:S(2)}, u32[]{:S(2)}) collective-permute-start(f32[16,1,128]{2,1,0:T(1,128)S(1)} %get-tuple-element.12), channel_id=1, source_target_pairs={{0,16},{16,32},{32,48},{48,64},{64,80},{80,96},{96,112},{112,128},... | collective-permute-start | bytes 24584 | tf_op jit(solution)/shard_map/ppermute | solution.py:468
  21.5 19.7 %copy-start.3 = (bf16[128,768]{1,0:T(8,128)(2,1)S(1)}, bf16[128,768]{1,0:T(8,128)(2,1)}, u32[]{:S(2)}) copy-start(bf16[128,768]{1,0:T(8,128)(2,1)} %constant.23.clone.mat_ref) | copy-start | bytes 589828
  23.4 17.7 %copy-start.5 = (f32[16,128]{1,0:T(8,128)S(1)}, f32[16,128]{1,0:T(8,128)}, u32[]{:S(2)}) copy-start(f32[16,128]{1,0:T(8,128)} %constant.24.clone.lam_ref) | copy-start | bytes 24580
  30.0 11.2 %collective-permute-start.1 = (f32[128,1024]{1,0:T(8,128)S(1)}, f32[128,1024]{1,0:T(8,128)S(1)}, u32[]{:S(2)}, u32[]{:S(2)}) collective-permute-start(f32[128,1024]{1,0:T(8,128)S(1)} %disperse.1), channel_id=1, source_target_pairs={{0,16},{16,32},{32,48},{48,64},{64,80},{80,96},{96,112},{112,128},... | collective-permute-start | bytes 1572872 | tf_op jit(solution)/shard_map/ppermute | solution.py:468
  43.0 13.3 %copy-start = (bf16[2,256,256]{2,1,0:T(8,128)(2,1)S(1)}, bf16[2,256,256]{2,1,0:T(8,128)(2,1)}, u32[]{:S(2)}) copy-start(bf16[2,256,256]{2,1,0:T(8,128)(2,1)} %constant.26.clone.bwd_ref) | copy-start | bytes 786436
  43.0 13.2 %copy-start.1 = (bf16[2,256,256]{2,1,0:T(8,128)(2,1)S(1)}, bf16[2,256,256]{2,1,0:T(8,128)(2,1)}, u32[]{:S(2)}) copy-start(bf16[2,256,256]{2,1,0:T(8,128)(2,1)} %constant.25.clone.fwd_ref) | copy-start | bytes 786436
  43.0 13.2 %copy-start.2 = (bf16[128,768]{1,0:T(8,128)(2,1)S(1)}, bf16[128,768]{1,0:T(8,128)(2,1)}, u32[]{:S(2)}) copy-start(bf16[128,768]{1,0:T(8,128)(2,1)} %constant.21.clone.mat_ref) | copy-start | bytes 589828

commit v7 on v6

--- a/solution.py
+++ b/solution.py
@@ -10,7 +10,7 @@
 from jax.sharding import PartitionSpec as P
 
 KRYLOV = 8
-EXPANDED = 5
+EXPANDED = 6
 NS = 16
 NG = 32
 NT = 1024
@@ -192,6 +192,10 @@
         spec[lo:hi, NB : 2 * NB] = a * fi + b * fr
 
 
+def whole_sum(value):
+    return jnp.sum(jnp.sum(value, axis=0, keepdims=True), axis=1, keepdims=True)
+
+
 def ymode_kernel(
     seed_ref, mat_ref, lam_ref, kind_ref, disp_ref, gain_ref, sat_ref, kerr_ref, out_ref
 ):
@@ -205,22 +209,25 @@
             for r in range(16):
                 total = total + square[8 * r : 8 * r + 8, lanes]
             place = 8 * (c0 + c)
-            out_ref[:, place : place + 8, :] = modes[:, lanes].reshape(NS, 8, 128)
-    row = lax.broadcasted_iota(jnp.int32, (8, 128), 0)
+            for d in range(NS):
+                out_ref[d, place : place + 8, 0, :] = modes[8 * d : 8 * d + 8, lanes]
+    lane = lax.broadcasted_iota(jnp.int32, (NS, 128), 1)
     chosen = lax.broadcasted_iota(jnp.int32, (1, 32), 1) == kind_ref[...]
-    side = jnp.broadcast_to(jnp.sum(total, axis=0, keepdims=True), (8, 128))
-    for place, ref in ((2, disp_ref), (3, gain_ref), (4, sat_ref), (5, kerr_ref)):
+    side = jnp.where(lane < 64, lam_ref[...], whole_sum(total))
+    for place, ref in ((65, disp_ref), (66, gain_ref), (67, sat_ref), (68, kerr_ref)):
         value = jnp.sum(jnp.where(chosen, ref[...], 0.0), axis=1, keepdims=True)
-        side = jnp.where(row == place, value, side)
-    for d in range(NS):
-        out_ref[d, 64:72, :] = jnp.where(row == 6, lam_ref[d : d + 1, :], side)
+        side = jnp.where(lane == place, value, side)
+    out_ref[:, 64, 0, :] = side
 
 
 def xmode_kernel(in_ref, mat_ref, modes_ref, side_ref, tile_ref):
     square = jnp.zeros((128, 128), F32)
     for c0 in range(0, NK, WIDE):
         block = jnp.concatenate(
-            [in_ref[:, 8 * c : 8 * c + 8, :].reshape(128, 128) for c in range(c0, c0 + WIDE)],
+            [
+                jnp.concatenate([in_ref[d, 8 * c : 8 * c + 8, 0, :] for d in range(NS)], axis=0)
+                for c in range(c0, c0 + WIDE)
+            ],
             axis=1,
         )
         modes = mm_wide(mat_ref[...], block)
@@ -234,14 +241,11 @@
         precision=HIGHEST,
         preferred_element_type=F32,
     )
-    side = in_ref[0, 64:72, :]
-    energy = side
-    for d in range(1, NS):
-        energy = energy + in_ref[d, 64:72, :]
-    row = lax.broadcasted_iota(jnp.int32, (8, 128), 0)
-    side_ref[...] = jnp.where(row == 1, energy, side)
-    lane = lax.broadcasted_iota(jnp.int32, (8, 128), 1)
-    tile = jnp.where(lane < 64, weight + pltpu.roll(weight, 64, 1), side[5:6, :])
+    lane = lax.broadcasted_iota(jnp.int32, (1, 128), 1)
+    sides = in_ref[:, 64, 0, :]
+    side = jnp.where(lane == 64, jnp.sum(sides, axis=0, keepdims=True), sides[0:1, :])
+    side_ref[...] = jnp.broadcast_to(side, (8, 128))
+    tile = jnp.where(lane < 64, (weight + pltpu.roll(weight, 64, 1))[0:1, :], side[:, 68:69])
     for d in range(NS):
         tile_ref[d] = tile[0:1, :]
 
@@ -264,10 +268,6 @@
     return c, s
 
 
-def whole_sum(value):
-    return jnp.sum(jnp.sum(value, axis=0, keepdims=True), axis=1, keepdims=True)
-
-
 def disperse_kernel(
     modes_ref, side_ref, tw_ref, fwd_ref, bwd_ref, out_ref, one, two
 ):
@@ -278,9 +278,9 @@
     outer_forward(load, 64, tw_ref, one)
     two[...] = mm(one[...], fwd_ref[...])
 
-    energy = whole_sum(side_ref[1:2, :])
-    dispersion, gain_peak = side_ref[2:3, :], side_ref[3:4, :]
-    gain = gain_peak / (1.0 + energy / (NG * NG * NT) / side_ref[4:5, :])
+    energy = side_ref[0:1, 64:65]
+    dispersion, gain_peak = side_ref[0:1, 65:66], side_ref[0:1, 66:67]
+    gain = gain_peak / (1.0 + energy / (NG * NG * NT) / side_ref[0:1, 67:68])
     w = tw_ref[2]
     relative = w / gain_width
     amplitude = jnp.exp(0.5 * gain / (1.0 + relative * relative) - loss_rate) * (1.0 / NT)
@@ -382,8 +382,8 @@
 
 
 def propagate_kernel(side_ref, weight_ref, lam_ref, modes_ref, mat_ref, out_ref, scaled):
-    own = jnp.broadcast_to(side_ref[6:7, :], (8, 128))
     lane = lax.broadcasted_iota(jnp.int32, (NS, 128), 1)
+    own = jnp.where(lane[0:8, :] < 64, side_ref[...], pltpu.roll(side_ref[...], 64, 1))
     weight = jnp.where(lane < 64, weight_ref[:, 0, :], 0.0)
     gains = mode_gains(weight, lam_ref[...], own)
     gain_re, gain_im = (
@@ -475,7 +475,7 @@
 
     ymodes = pl.pallas_call(
         ymode_kernel,
-        out_shape=near(NS, 72, 128),
+        out_shape=near(NS, 65, 1, 128),
         in_specs=[VMEM] * 8,
         out_specs=VMEM,
         name="ymode",

time: 58.7 us -> 58.4 us (level)
  blocking collectives: 42.5 us -> 41.8 us
    all_to_all x3, blocking collectives: 42.5 us -> 41.8 us  [exchange(): lax.all_to_all(value, 'shard', split_axis=0, concat_axis=0, tiled=True)]
where the time goes in v7:
time: 58.4 us; the launch traced here: 58.2 us
  blocking collectives  41.8 us (72%)
  Pallas kernels  8.52 us (15%)
  waiting for transfers between devices  6.96 us (12%)
  between operations  0.75 us (1%)
    all_to_all x3, blocking collectives, exchange(): lax.all_to_all(value, 'shard', split_axis=0, concat_axis=0, tiled=True)  41.8 us
    ppermute x2, waiting for transfers between devices, pass_on(): lax.ppermute(value, 'blk', [(b, (b + 1) % count) for b in range(count)])  6.96 us
    pallas_call x1, Pallas kernels, per_device(): pl.pallas_call(kerr_kernel, out_shape=jax.ShapeDtypeStruct((128, NT), F32...  2.22 us
    pallas_call x1, Pallas kernels, per_device(): pl.pallas_call(disperse_kernel, out_shape=near(128, NT), in_specs=[VMEM]...  1.92 us
    pallas_call x1, Pallas kernels, per_device(): pl.pallas_call(ymode_kernel, out_shape=near(NS, 65, 1, 128), in_specs=[VM...  1.77 us
    pallas_call x1, Pallas kernels, per_device(): pl.pallas_call(propagate_kernel, out_shape=near(NS, 8, NT), in_specs=[VME...  1.7 us
  transfers between devices with their start and end apart: 2, of which 1 were waited for; matrix products, arithmetic and copies ran while one was open for 0% of the time, Pallas kernels for 3%

profile of v7, /device:TPU:8, one launch (start us, length us, event | category | flops | bytes accessed | tf_op | source)
XLA Modules:
  0.0 58.2 jit_solution(6747283466994833525)
XLA Ops:
  0.7 1.8 %ymode.1 = f32[16,65,1,128]{3,2,1,0:T(1,128)S(1)} custom-call(f32[128,1024]{1,0:T(8,128)} %bitcast.8, bf16[128,768]{1,0:T(8,128)(2,1)} %constant.20.clone.mat_ref, f32[16,128]{1,0:T(8,128)} %constant.24.clone.lam_ref, s32[1,1]{1,0:T(1,128)} %bitcast.7.kind_ref, f32[1,32]{1,0:T(1,128)} %bitcast.9, f32[1,32]{1,0:T(1,128)} %bitcast.10, f32[1,32]{1,0:T(1,128)} %bitcast.11, ...), custom_call_target="tpu_custom_call" | custom-call | tf_op jit(solution)/shard_map/ymode/pallas_call | solution.py:476
  2.4 0.0 copy-start.4
  2.4 17.8 %all_to_all.15.in_ref = f32[16,65,1,128]{3,2,1,0:T(1,128)S(1)} all-to-all(f32[16,65,1,128]{3,2,1,0:T(1,128)S(1)} %ymode.1), channel_id=1, replica_groups=mesh['blk'=32,'shard'=16] {'shard'}, dimensions={0} | all-to-all | bytes 1064960 | tf_op jit(solution)/shard_map/all_to_all | solution.py:463
  20.2 0.0 copy-done.4
  20.2 0.0 copy-start.6
  20.2 0.0 copy-start.7
  20.2 0.0 copy-start.8
  20.2 0.9 %xmode.1 = (f32[128,1024]{1,0:T(8,128)S(1)}, f32[8,128]{1,0:T(8,128)S(1)}, f32[16,1,128]{2,1,0:T(1,128)S(1)}) custom-call(f32[16,65,1,128]{3,2,1,0:T(1,128)S(1)} %all_to_all.15.in_ref, bf16[128,768]{1,0:T(8,128)(2,1)S(1)} %copy-done.4), custom_call_target="tpu_custom_call" | custom-call | tf_op jit(solution)/shard_map/xmode/pallas_call | solution.py:487
  21.1 0.0 collective-permute-start
  21.1 0.0 copy-done.6
  21.2 0.0 copy-done.7
  21.2 0.1 copy-done.8
  21.2 0.0 copy-start.3
  21.2 1.9 %disperse.1 = f32[128,1024]{1,0:T(8,128)S(1)} custom-call(f32[128,1024]{1,0:T(8,128)S(1)} %get-tuple-element.10.modes_ref, f32[8,128]{1,0:T(8,128)S(1)} %get-tuple-element.11.side_ref, f32[5,8,128]{2,1,0:T(8,128)S(1)} %copy-done.6, f32[256,256]{1,0:T(8,128)S(1)} %copy-done.8, f32[256,256]{1,0:T(8,128)S(1)} %copy-done.7), custom_call_target="tpu_custom_call" | custom-call | flops 805306368 | bytes 1048576 | tf_op jit(solution)/shard_map/disperse/pallas_call | solution.py:495
  23.2 0.0 copy-start.5
  23.2 7.0 %collective-permute-done.tile_ref = f32[16,1,128]{2,1,0:T(1,128)S(1)} collective-permute-done((f32[16,1,128]{2,1,0:T(1,128)S(1)}, f32[16,1,128]{2,1,0:T(1,128)S(1)}, u32[]{:S(2)}, u32[]{:S(2)}) %collective-permute-start) | collective-permute-done | bytes 8224 | tf_op jit(solution)/shard_map/ppermute | solution.py:468
  30.1 0.0 collective-permute-start.1
  30.1 10.8 %all_to_all.16.weight_ref = f32[16,1,128]{2,1,0:T(1,128)S(1)} all-to-all(f32[16,1,128]{2,1,0:T(1,128)S(1)} %collective-permute-done.tile_ref), channel_id=1, replica_groups=mesh['blk'=32,'shard'=16] {'shard'}, dimensions={0} | all-to-all | bytes 16384 | tf_op jit(solution)/shard_map/all_to_all | solution.py:463
  41.0 0.0 collective-permute-done.1.modes_ref
  41.0 0.0 copy-done.3
  41.0 0.0 copy-done.5
  41.0 1.7 %propagate.1 = f32[16,8,1024]{2,1,0:T(8,128)S(1)} custom-call(f32[8,128]{1,0:T(8,128)S(1)} %get-tuple-element.11.side_ref, f32[16,1,128]{2,1,0:T(1,128)S(1)} %all_to_all.16.weight_ref, f32[16,128]{1,0:T(8,128)S(1)} %copy-done.5, f32[128,1024]{1,0:T(8,128)S(1)} %collective-permute-done.1.modes_ref, bf16[128,768]{1,0:T(8,128)(2,1)S(1)} %copy-done.3), custom_call_target="tpu_custom_call" | custom-call | tf_op jit(solution)/shard_map/propagate/pallas_call | solution.py:510
  42.7 0.0 copy-start
  42.7 0.0 copy-start.1
  42.7 0.0 copy-start.2
  42.7 13.2 %all_to_all.17.in_ref = f32[16,8,1024]{2,1,0:T(8,128)S(1)} all-to-all(f32[16,8,1024]{2,1,0:T(8,128)S(1)} %propagate.1), channel_id=1, replica_groups=mesh['blk'=32,'shard'=16] {'shard'}, dimensions={0} | all-to-all | bytes 1048576 | tf_op jit(solution)/shard_map/all_to_all | solution.py:463
  55.9 0.0 copy-done
  55.9 0.0 copy-done.1
  55.9 0.0 copy-done.2
  55.9 2.2 %kerr.1 = f32[128,1024]{1,0:T(8,128)} custom-call(f32[16,1,128]{2,1,0:T(1,128)S(1)} %collective-permute-done.tile_ref, f32[16,8,1024]{2,1,0:T(8,128)S(1)} %all_to_all.17.in_ref, bf16[128,768]{1,0:T(8,128)(2,1)S(1)} %copy-done.2, f32[5,8,128]{2,1,0:T(8,128)S(1)} %copy-done.6, bf16[2,256,256]{2,1,0:T(8,128)(2,1)S(1)} %copy-done.1, bf16[2,256,256]{2,1,0:T(8,128)(2,1)S(1)} %copy-done), custom_call_target="tpu_custom_call" | custom-call | tf_op jit(solution)/shard_map/kerr/pallas_call | solution.py:522
Async XLA Ops:
  2.4 17.8 %copy-start.4 = (bf16[128,768]{1,0:T(8,128)(2,1)S(1)}, bf16[128,768]{1,0:T(8,128)(2,1)}, u32[]{:S(2)}) copy-start(bf16[128,768]{1,0:T(8,128)(2,1)} %constant.22.clone.mat_ref) | copy-start | bytes 589828
  20.2 1.0 %copy-start.6 = (f32[5,8,128]{2,1,0:T(8,128)S(1)}, f32[5,8,128]{2,1,0:T(8,128)}, u32[]{:S(2)}) copy-start(f32[5,8,128]{2,1,0:T(8,128)} %constant.29.clone.tw_ref) | copy-start | bytes 61444
  20.2 1.0 %copy-start.7 = (f32[256,256]{1,0:T(8,128)S(1)}, f32[256,256]{1,0:T(8,128)}, u32[]{:S(2)}) copy-start(f32[256,256]{1,0:T(8,128)} %constant.28.clone.bwd_ref) | copy-start | bytes 786436
  20.2 1.0 %copy-start.8 = (f32[256,256]{1,0:T(8,128)S(1)}, f32[256,256]{1,0:T(8,128)}, u32[]{:S(2)}) copy-start(f32[256,256]{1,0:T(8,128)} %constant.27.clone.fwd_ref) | copy-start | bytes 786436
  21.1 9.0 %collective-permute-start = (f32[16,1,128]{2,1,0:T(1,128)S(1)}, f32[16,1,128]{2,1,0:T(1,128)S(1)}, u32[]{:S(2)}, u32[]{:S(2)}) collective-permute-start(f32[16,1,128]{2,1,0:T(1,128)S(1)} %get-tuple-element.12), channel_id=1, source_target_pairs={{0,16},{16,32},{32,48},{48,64},{64,80},{80,96},{96,112},{112,128},... | collective-permute-start | bytes 24584 | tf_op jit(solution)/shard_map/ppermute | solution.py:468
  21.2 19.7 %copy-start.3 = (bf16[128,768]{1,0:T(8,128)(2,1)S(1)}, bf16[128,768]{1,0:T(8,128)(2,1)}, u32[]{:S(2)}) copy-start(bf16[128,768]{1,0:T(8,128)(2,1)} %constant.23.clone.mat_ref) | copy-start | bytes 589828
  23.2 17.8 %copy-start.5 = (f32[16,128]{1,0:T(8,128)S(1)}, f32[16,128]{1,0:T(8,128)}, u32[]{:S(2)}) copy-start(f32[16,128]{1,0:T(8,128)} %constant.24.clone.lam_ref) | copy-start | bytes 24580
  30.1 10.8 %collective-permute-start.1 = (f32[128,1024]{1,0:T(8,128)S(1)}, f32[128,1024]{1,0:T(8,128)S(1)}, u32[]{:S(2)}, u32[]{:S(2)}) collective-permute-start(f32[128,1024]{1,0:T(8,128)S(1)} %disperse.1), channel_id=1, source_target_pairs={{0,16},{16,32},{32,48},{48,64},{64,80},{80,96},{96,112},{112,128},... | collective-permute-start | bytes 1572872 | tf_op jit(solution)/shard_map/ppermute | solution.py:468
  42.7 13.3 %copy-start = (bf16[2,256,256]{2,1,0:T(8,128)(2,1)S(1)}, bf16[2,256,256]{2,1,0:T(8,128)(2,1)}, u32[]{:S(2)}) copy-start(bf16[2,256,256]{2,1,0:T(8,128)(2,1)} %constant.26.clone.bwd_ref) | copy-start | bytes 786436
  42.7 13.2 %copy-start.1 = (bf16[2,256,256]{2,1,0:T(8,128)(2,1)S(1)}, bf16[2,256,256]{2,1,0:T(8,128)(2,1)}, u32[]{:S(2)}) copy-start(bf16[2,256,256]{2,1,0:T(8,128)(2,1)} %constant.25.clone.fwd_ref) | copy-start | bytes 786436
  42.7 13.2 %copy-start.2 = (bf16[128,768]{1,0:T(8,128)(2,1)S(1)}, bf16[128,768]{1,0:T(8,128)(2,1)}, u32[]{:S(2)}) copy-start(bf16[128,768]{1,0:T(8,128)(2,1)} %constant.21.clone.mat_ref) | copy-start | bytes 589828

commit v8 on v7

--- a/solution.py
+++ b/solution.py
@@ -231,7 +231,7 @@
             axis=1,
         )
         modes = mm_wide(mat_ref[...], block)
-        modes_ref[:, c0 * 128 : (c0 + WIDE) * 128] = modes
+        modes_ref[0:128, c0 * 128 : (c0 + WIDE) * 128] = modes
         for c in range(WIDE):
             square = square + modes[:, c * 128 : c * 128 + 128] ** 2
     weight = lax.dot_general(
@@ -245,7 +245,9 @@
     sides = in_ref[:, 64, 0, :]
     side = jnp.where(lane == 64, jnp.sum(sides, axis=0, keepdims=True), sides[0:1, :])
     side_ref[...] = jnp.broadcast_to(side, (8, 128))
-    tile = jnp.where(lane < 64, (weight + pltpu.roll(weight, 64, 1))[0:1, :], side[:, 68:69])
+    modes_ref[128:136, 0:128] = jnp.broadcast_to(side, (8, 128))
+    modes_ref[128:136, 128:NT] = jnp.zeros((8, NT - 128), F32)
+    tile = (weight + pltpu.roll(weight, 64, 1))[0:1, :]
     for d in range(NS):
         tile_ref[d] = tile[0:1, :]
 
@@ -269,7 +271,7 @@
 
 
 def disperse_kernel(
-    modes_ref, side_ref, tw_ref, fwd_ref, bwd_ref, out_ref, one, two
+    modes_ref, tw_ref, fwd_ref, bwd_ref, out_ref, one, two
 ):
 
     def load(part, r0, a):
@@ -278,9 +280,9 @@
     outer_forward(load, 64, tw_ref, one)
     two[...] = mm(one[...], fwd_ref[...])
 
-    energy = side_ref[0:1, 64:65]
-    dispersion, gain_peak = side_ref[0:1, 65:66], side_ref[0:1, 66:67]
-    gain = gain_peak / (1.0 + energy / (NG * NG * NT) / side_ref[0:1, 67:68])
+    energy = modes_ref[128:129, 64:65]
+    dispersion, gain_peak = modes_ref[128:129, 65:66], modes_ref[128:129, 66:67]
+    gain = gain_peak / (1.0 + energy / (NG * NG * NT) / modes_ref[128:129, 67:68])
     w = tw_ref[2]
     relative = w / gain_width
     amplitude = jnp.exp(0.5 * gain / (1.0 + relative * relative) - loss_rate) * (1.0 / NT)
@@ -381,13 +383,19 @@
     return gains
 
 
-def propagate_kernel(side_ref, weight_ref, lam_ref, modes_ref, mat_ref, out_ref, scaled):
+def lanczos_kernel(side_ref, weight_ref, lam_ref, factor_ref):
     lane = lax.broadcasted_iota(jnp.int32, (NS, 128), 1)
     own = jnp.where(lane[0:8, :] < 64, side_ref[...], pltpu.roll(side_ref[...], 64, 1))
     weight = jnp.where(lane < 64, weight_ref[:, 0, :], 0.0)
-    gains = mode_gains(weight, lam_ref[...], own)
+    gain_re, gain_im = mode_gains(weight, lam_ref[...], own)
+    row = lax.broadcasted_iota(jnp.int32, (8, 128), 0)
+    factor_ref[...] = jnp.where(row == 0, gain_re, gain_im)
+
+
+def propagate_kernel(factor_ref, modes_ref, mat_ref, out_ref, scaled):
     gain_re, gain_im = (
-        jnp.broadcast_to(gain[0:1, :], (128, 128)).T[0:64, :] for gain in gains
+        jnp.broadcast_to(factor_ref[row : row + 1, :], (128, 128)).T[0:64, :]
+        for row in range(2)
     )
     for c0 in range(0, NK, WIDE):
         for c in range(c0, c0 + WIDE):
@@ -401,10 +409,10 @@
 
 
 def kerr_kernel(
-    tile_ref, in_ref, mat_ref, tw_ref, fwd_ref, bwd_ref,
+    modes_ref, in_ref, mat_ref, tw_ref, fwd_ref, bwd_ref,
     out_ref, field, delayed, one, two, done, sems
 ):
-    kerr = tile_ref[0, 0:1, 64:65]
+    kerr = modes_ref[128:129, 68:69]
     field[...] = mm_wide(mat_ref[...], in_ref[...].reshape(128, NT))
 
     def load(side, r0, a):
@@ -486,38 +494,40 @@
     gathered = exchange(ymodes)
     modes, side, tile = pl.pallas_call(
         xmode_kernel,
-        out_shape=(near(128, NT), near(8, 128), near(NS, 1, 128)),
+        out_shape=(near(136, NT), near(8, 128), near(NS, 1, 128)),
         in_specs=[VMEM] * 2,
         out_specs=(VMEM,) * 3,
         name="xmode",
     )(hold(gathered), near_tables["to_xmode"])
-    shifted = pass_on(tile)
-    modes = pl.pallas_call(
+    shifted = pass_on(modes)
+    weights = exchange(tile)
+    factor = pl.pallas_call(
+        lanczos_kernel,
+        out_shape=near(8, 128),
+        in_specs=[VMEM] * 3,
+        out_specs=VMEM,
+        cost_estimate=cost(6 * 2 * 512 * 256 * 256, 2**20),
+        name="lanczos",
+    )(hold(side), hold(weights), near_tables["lam_all"])
+    shifted, factor = lax.optimization_barrier((shifted, factor))
+    factor = pass_on(factor)
+    dispersed = pl.pallas_call(
         disperse_kernel,
         out_shape=near(128, NT),
-        in_specs=[VMEM] * 5,
+        in_specs=[VMEM] * 4,
         out_specs=VMEM,
         scratch_shapes=[pltpu.VMEM((512, 256), F32)] * 2,
         cost_estimate=cost(6 * 4 * 512 * 256 * 256, 2**20),
         name="disperse",
-    )(
-        hold(modes), hold(side),
-        *(near_tables[name] for name in ("lines", "forward", "backward")),
-    )
-    modes, shifted = lax.optimization_barrier((modes, shifted))
-    modes = pass_on(modes)
-    weights = exchange(shifted)
+    )(hold(shifted), *(near_tables[name] for name in ("lines", "forward", "backward")))
     xback = pl.pallas_call(
         propagate_kernel,
         out_shape=near(NS, 8, NT),
-        in_specs=[VMEM] * 5,
+        in_specs=[VMEM] * 3,
         out_specs=VMEM,
         scratch_shapes=[pltpu.VMEM((128, NT), F32)],
         name="propagate",
-    )(
-        hold(side), hold(weights), near_tables["lam_all"], hold(modes),
-        near_tables["from_xmode"],
-    )
+    )(hold(factor), hold(dispersed), near_tables["from_xmode"])
     rows = exchange(xback)
     result = pl.pallas_call(
         kerr_kernel,

time: 58.4 us -> 57.3 us (0.981)
  the two profiles are of different devices: /device:TPU:8 before, /device:TPU:97 now
where the time goes in v8:
time: 57.3 us; the launch traced here: 57 us
  blocking collectives  41.6 us (73%)
  Pallas kernels  8.52 us (15%)
  starting transfers between devices  6.04 us (11%)
  between operations  0.76 us (1%)
    all_to_all x3, blocking collectives, exchange(): lax.all_to_all(value, 'shard', split_axis=0, concat_axis=0, tiled=True)  41.6 us
    ppermute x2, starting transfers between devices, pass_on(): lax.ppermute(value, 'blk', [(b, (b + 1) % count) for b in range(count)])  6.04 us
    pallas_call x1, Pallas kernels, per_device(): pl.pallas_call(kerr_kernel, out_shape=jax.ShapeDtypeStruct((128, NT), F32...  2.21 us
    pallas_call x1, Pallas kernels, per_device(): pl.pallas_call(disperse_kernel, out_shape=near(128, NT), in_specs=[VMEM]...  1.91 us
    pallas_call x1, Pallas kernels, per_device(): pl.pallas_call(ymode_kernel, out_shape=near(NS, 65, 1, 128), in_specs=[VM...  1.77 us
    pallas_call x1, Pallas kernels, per_device(): pl.pallas_call(lanczos_kernel, out_shape=near(8, 128), in_specs=[VMEM] *...  1.2 us
  transfers between devices with their start and end apart: 2, of which 0 were waited for; matrix products, arithmetic and copies ran while one was open for 0% of the time, Pallas kernels for 5%

profile of v8, /device:TPU:97, one launch (start us, length us, event | category | flops | bytes accessed | tf_op | source)
XLA Modules:
  0.0 57.0 jit_solution(10951525944987395752)
XLA Ops:
  0.7 1.8 %ymode.1 = f32[16,65,1,128]{3,2,1,0:T(1,128)S(1)} custom-call(f32[128,1024]{1,0:T(8,128)} %bitcast.8, bf16[128,768]{1,0:T(8,128)(2,1)} %constant.20.clone.mat_ref, f32[16,128]{1,0:T(8,128)} %constant.24.clone.lam_ref, s32[1,1]{1,0:T(1,128)} %bitcast.7.kind_ref, f32[1,32]{1,0:T(1,128)} %bitcast.9, f32[1,32]{1,0:T(1,128)} %bitcast.10, f32[1,32]{1,0:T(1,128)} %bitcast.11, ...), custom_call_target="tpu_custom_call" | custom-call | tf_op jit(solution)/shard_map/ymode/pallas_call | solution.py:484
  2.4 0.0 copy-start.4
  2.4 17.5 %all_to_all.15.in_ref = f32[16,65,1,128]{3,2,1,0:T(1,128)S(1)} all-to-all(f32[16,65,1,128]{3,2,1,0:T(1,128)S(1)} %ymode.1), channel_id=1, replica_groups=mesh['blk'=32,'shard'=16] {'shard'}, dimensions={0} | all-to-all | bytes 1064960 | tf_op jit(solution)/shard_map/all_to_all | solution.py:471
  19.9 0.0 copy-done.4
  19.9 0.9 %xmode.1 = (f32[136,1024]{1,0:T(8,128)S(1)}, f32[8,128]{1,0:T(8,128)S(1)}, f32[16,1,128]{2,1,0:T(1,128)S(1)}) custom-call(f32[16,65,1,128]{3,2,1,0:T(1,128)S(1)} %all_to_all.15.in_ref, bf16[128,768]{1,0:T(8,128)(2,1)S(1)} %copy-done.4), custom_call_target="tpu_custom_call" | custom-call | tf_op jit(solution)/shard_map/xmode/pallas_call | solution.py:495
  20.8 4.7 %collective-permute-start = (f32[136,1024]{1,0:T(8,128)S(1)}, f32[136,1024]{1,0:T(8,128)S(1)}, u32[]{:S(2)}, u32[]{:S(2)}) collective-permute-start(f32[136,1024]{1,0:T(8,128)S(1)} %get-tuple-element.10), channel_id=1, source_target_pairs={{0,16},{16,32},{32,48},{48,64},{64,80},{80,96},{96,112},{112,128},... | collective-permute-start | bytes 1671176 | tf_op jit(solution)/shard_map/ppermute | solution.py:476
  25.6 0.0 copy-start.6
  25.6 9.4 %all_to_all.16.weight_ref = f32[16,1,128]{2,1,0:T(1,128)S(1)} all-to-all(f32[16,1,128]{2,1,0:T(1,128)S(1)} %get-tuple-element.12), channel_id=1, replica_groups=mesh['blk'=32,'shard'=16] {'shard'}, dimensions={0} | all-to-all | bytes 16384 | tf_op jit(solution)/shard_map/all_to_all | solution.py:471
  34.9 0.0 copy-done.6
  34.9 0.0 copy-start.5
  34.9 0.0 copy-start.7
  34.9 0.0 copy-start.8
  35.0 1.2 %lanczos.1 = f32[8,128]{1,0:T(8,128)S(1)} custom-call(f32[8,128]{1,0:T(8,128)S(1)} %get-tuple-element.11.side_ref, f32[16,1,128]{2,1,0:T(1,128)S(1)} %all_to_all.16.weight_ref, f32[16,128]{1,0:T(8,128)S(1)} %copy-done.6), custom_call_target="tpu_custom_call" | custom-call | flops 402653184 | bytes 1048576 | tf_op jit(solution)/shard_map/lanczos/pallas_call | solution.py:504
  36.2 0.0 copy-start.3
  36.2 0.0 collective-permute-done.modes_ref
  36.2 1.3 %collective-permute-start.1 = (f32[8,128]{1,0:T(8,128)S(1)}, f32[8,128]{1,0:T(8,128)S(1)}, u32[]{:S(2)}, u32[]{:S(2)}) collective-permute-start(f32[8,128]{1,0:T(8,128)S(1)} %lanczos.1), channel_id=1, source_target_pairs={{0,16},{16,32},{32,48},{48,64},{64,80},{80,96},{96,112},{112,128},... | collective-permute-start | bytes 12296 | tf_op jit(solution)/shard_map/ppermute | solution.py:476
  37.5 0.0 copy-done.5
  37.5 0.0 copy-done.7
  37.5 0.0 copy-done.8
  37.5 1.9 %disperse.1.modes_ref = f32[128,1024]{1,0:T(8,128)S(1)} custom-call(f32[136,1024]{1,0:T(8,128)S(1)} %collective-permute-done.modes_ref, f32[5,8,128]{2,1,0:T(8,128)S(1)} %copy-done.5, f32[256,256]{1,0:T(8,128)S(1)} %copy-done.8, f32[256,256]{1,0:T(8,128)S(1)} %copy-done.7), custom_call_target="tpu_custom_call" | custom-call | flops 805306368 | bytes 1048576 | tf_op jit(solution)/shard_map/disperse/pallas_call | solution.py:514
  39.4 0.0 collective-permute-done.1.factor_ref
  39.4 0.0 copy-done.3
  39.5 0.5 propagate.1
  40.0 0.0 copy-start
  40.0 0.0 copy-start.1
  40.0 0.0 copy-start.2
  40.0 14.8 %all_to_all.17.in_ref = f32[16,8,1024]{2,1,0:T(8,128)S(1)} all-to-all(f32[16,8,1024]{2,1,0:T(8,128)S(1)} %propagate.1), channel_id=1, replica_groups=mesh['blk'=32,'shard'=16] {'shard'}, dimensions={0} | all-to-all | bytes 1048576 | tf_op jit(solution)/shard_map/all_to_all | solution.py:471
  54.8 0.0 copy-done
  54.8 0.0 copy-done.1
  54.8 0.0 copy-done.2
  54.8 2.2 %kerr.1 = f32[128,1024]{1,0:T(8,128)} custom-call(f32[136,1024]{1,0:T(8,128)S(1)} %collective-permute-done.modes_ref, f32[16,8,1024]{2,1,0:T(8,128)S(1)} %all_to_all.17.in_ref, bf16[128,768]{1,0:T(8,128)(2,1)S(1)} %copy-done.2, f32[5,8,128]{2,1,0:T(8,128)S(1)} %copy-done.5, bf16[2,256,256]{2,1,0:T(8,128)(2,1)S(1)} %copy-done.1, bf16[2,256,256]{2,1,0:T(8,128)(2,1)S(1)} %copy-done), custom_call_target="tpu_custom_call" | custom-call | tf_op jit(solution)/shard_map/kerr/pallas_call | solution.py:532
Async XLA Ops:
  2.4 17.5 %copy-start.4 = (bf16[128,768]{1,0:T(8,128)(2,1)S(1)}, bf16[128,768]{1,0:T(8,128)(2,1)}, u32[]{:S(2)}) copy-start(bf16[128,768]{1,0:T(8,128)(2,1)} %constant.22.clone.mat_ref) | copy-start | bytes 589828
  20.8 15.3 %collective-permute-start = (f32[136,1024]{1,0:T(8,128)S(1)}, f32[136,1024]{1,0:T(8,128)S(1)}, u32[]{:S(2)}, u32[]{:S(2)}) collective-permute-start(f32[136,1024]{1,0:T(8,128)S(1)} %get-tuple-element.10), channel_id=1, source_target_pairs={{0,16},{16,32},{32,48},{48,64},{64,80},{80,96},{96,112},{112,128},... | collective-permute-start | bytes 1671176 | tf_op jit(solution)/shard_map/ppermute | solution.py:476
  25.6 9.4 %copy-start.6 = (f32[16,128]{1,0:T(8,128)S(1)}, f32[16,128]{1,0:T(8,128)}, u32[]{:S(2)}) copy-start(f32[16,128]{1,0:T(8,128)} %constant.24.clone.lam_ref) | copy-start | bytes 24580
  34.9 2.6 %copy-start.5 = (f32[5,8,128]{2,1,0:T(8,128)S(1)}, f32[5,8,128]{2,1,0:T(8,128)}, u32[]{:S(2)}) copy-start(f32[5,8,128]{2,1,0:T(8,128)} %constant.29.clone.tw_ref) | copy-start | bytes 61444
  34.9 2.6 %copy-start.7 = (f32[256,256]{1,0:T(8,128)S(1)}, f32[256,256]{1,0:T(8,128)}, u32[]{:S(2)}) copy-start(f32[256,256]{1,0:T(8,128)} %constant.28.clone.bwd_ref) | copy-start | bytes 786436
  34.9 2.6 %copy-start.8 = (f32[256,256]{1,0:T(8,128)S(1)}, f32[256,256]{1,0:T(8,128)}, u32[]{:S(2)}) copy-start(f32[256,256]{1,0:T(8,128)} %constant.27.clone.fwd_ref) | copy-start | bytes 786436
  36.2 3.3 %copy-start.3 = (bf16[128,768]{1,0:T(8,128)(2,1)S(1)}, bf16[128,768]{1,0:T(8,128)(2,1)}, u32[]{:S(2)}) copy-start(bf16[128,768]{1,0:T(8,128)(2,1)} %constant.23.clone.mat_ref) | copy-start | bytes 589828
  36.2 3.3 %collective-permute-start.1 = (f32[8,128]{1,0:T(8,128)S(1)}, f32[8,128]{1,0:T(8,128)S(1)}, u32[]{:S(2)}, u32[]{:S(2)}) collective-permute-start(f32[8,128]{1,0:T(8,128)S(1)} %lanczos.1), channel_id=1, source_target_pairs={{0,16},{16,32},{32,48},{48,64},{64,80},{80,96},{96,112},{112,128},... | collective-permute-start | bytes 12296 | tf_op jit(solution)/shard_map/ppermute | solution.py:476
  40.0 14.8 %copy-start = (bf16[2,256,256]{2,1,0:T(8,128)(2,1)S(1)}, bf16[2,256,256]{2,1,0:T(8,128)(2,1)}, u32[]{:S(2)}) copy-start(bf16[2,256,256]{2,1,0:T(8,128)(2,1)} %constant.26.clone.bwd_ref) | copy-start | bytes 786436
  40.0 14.8 %copy-start.1 = (bf16[2,256,256]{2,1,0:T(8,128)(2,1)S(1)}, bf16[2,256,256]{2,1,0:T(8,128)(2,1)}, u32[]{:S(2)}) copy-start(bf16[2,256,256]{2,1,0:T(8,128)(2,1)} %constant.25.clone.fwd_ref) | copy-start | bytes 786436
  40.0 14.8 %copy-start.2 = (bf16[128,768]{1,0:T(8,128)(2,1)S(1)}, bf16[128,768]{1,0:T(8,128)(2,1)}, u32[]{:S(2)}) copy-start(bf16[128,768]{1,0:T(8,128)(2,1)} %constant.21.clone.mat_ref) | copy-start | bytes 589828

commit v9 on v8

--- a/solution.py
+++ b/solution.py
@@ -234,22 +234,17 @@
         modes_ref[0:128, c0 * 128 : (c0 + WIDE) * 128] = modes
         for c in range(WIDE):
             square = square + modes[:, c * 128 : c * 128 + 128] ** 2
-    weight = lax.dot_general(
-        jnp.ones((8, 128), F32),
-        square,
-        (((1,), (1,)), ((), ())),
-        precision=HIGHEST,
-        preferred_element_type=F32,
-    )
+    both = square[0:64, :] + square[64:128, :]
+    both = jnp.concatenate([both, both], axis=0)
+    tile = jnp.sum(both.T, axis=0, keepdims=True)
     lane = lax.broadcasted_iota(jnp.int32, (1, 128), 1)
     sides = in_ref[:, 64, 0, :]
     side = jnp.where(lane == 64, jnp.sum(sides, axis=0, keepdims=True), sides[0:1, :])
     side_ref[...] = jnp.broadcast_to(side, (8, 128))
     modes_ref[128:136, 0:128] = jnp.broadcast_to(side, (8, 128))
     modes_ref[128:136, 128:NT] = jnp.zeros((8, NT - 128), F32)
-    tile = (weight + pltpu.roll(weight, 64, 1))[0:1, :]
     for d in range(NS):
-        tile_ref[d] = tile[0:1, :]
+        tile_ref[d] = tile
 
 
 def turn(angle):

time: 57.3 us -> 57 us (level)
  no operation moved by 1% of the time
where the time goes in v9:
time: 57 us; the launch traced here: 56.7 us
  blocking collectives  41.6 us (73%)
  Pallas kernels  8.28 us (15%)
  starting transfers between devices  6.05 us (11%)
  between operations  0.77 us (1%)
    all_to_all x3, blocking collectives, exchange(): lax.all_to_all(value, 'shard', split_axis=0, concat_axis=0, tiled=True)  41.6 us
    ppermute x2, starting transfers between devices, pass_on(): lax.ppermute(value, 'blk', [(b, (b + 1) % count) for b in range(count)])  6.05 us
    pallas_call x1, Pallas kernels, per_device(): pl.pallas_call(kerr_kernel, out_shape=jax.ShapeDtypeStruct((128, NT), F32...  2.21 us
    pallas_call x1, Pallas kernels, per_device(): pl.pallas_call(disperse_kernel, out_shape=near(128, NT), in_specs=[VMEM]...  1.91 us
    pallas_call x1, Pallas kernels, per_device(): pl.pallas_call(ymode_kernel, out_shape=near(NS, 65, 1, 128), in_specs=[VM...  1.77 us
    pallas_call x1, Pallas kernels, per_device(): pl.pallas_call(lanczos_kernel, out_shape=near(8, 128), in_specs=[VMEM] *...  1.2 us
  transfers between devices with their start and end apart: 2, of which 0 were waited for; matrix products, arithmetic and copies ran while one was open for 0% of the time, Pallas kernels for 5%

profile of v9, /device:TPU:97, one launch (start us, length us, event | category | flops | bytes accessed | tf_op | source)
XLA Modules:
  0.0 56.7 jit_solution(1626184209386999897)
XLA Ops:
  0.7 1.8 %ymode.1 = f32[16,65,1,128]{3,2,1,0:T(1,128)S(1)} custom-call(f32[128,1024]{1,0:T(8,128)} %bitcast.8, bf16[128,768]{1,0:T(8,128)(2,1)} %constant.20.clone.mat_ref, f32[16,128]{1,0:T(8,128)} %constant.24.clone.lam_ref, s32[1,1]{1,0:T(1,128)} %bitcast.7.kind_ref, f32[1,32]{1,0:T(1,128)} %bitcast.9, f32[1,32]{1,0:T(1,128)} %bitcast.10, f32[1,32]{1,0:T(1,128)} %bitcast.11, ...), custom_call_target="tpu_custom_call" | custom-call | tf_op jit(solution)/shard_map/ymode/pallas_call | solution.py:479
  2.4 0.0 copy-start.4
  2.4 17.5 %all_to_all.15.in_ref = f32[16,65,1,128]{3,2,1,0:T(1,128)S(1)} all-to-all(f32[16,65,1,128]{3,2,1,0:T(1,128)S(1)} %ymode.1), channel_id=1, replica_groups=mesh['blk'=32,'shard'=16] {'shard'}, dimensions={0} | all-to-all | bytes 1064960 | tf_op jit(solution)/shard_map/all_to_all | solution.py:466
  19.9 0.0 copy-done.4
  19.9 0.7 %xmode.1 = (f32[136,1024]{1,0:T(8,128)S(1)}, f32[8,128]{1,0:T(8,128)S(1)}, f32[16,1,128]{2,1,0:T(1,128)S(1)}) custom-call(f32[16,65,1,128]{3,2,1,0:T(1,128)S(1)} %all_to_all.15.in_ref, bf16[128,768]{1,0:T(8,128)(2,1)S(1)} %copy-done.4), custom_call_target="tpu_custom_call" | custom-call | tf_op jit(solution)/shard_map/xmode/pallas_call | solution.py:490
  20.6 4.7 %collective-permute-start = (f32[136,1024]{1,0:T(8,128)S(1)}, f32[136,1024]{1,0:T(8,128)S(1)}, u32[]{:S(2)}, u32[]{:S(2)}) collective-permute-start(f32[136,1024]{1,0:T(8,128)S(1)} %get-tuple-element.10), channel_id=1, source_target_pairs={{0,16},{16,32},{32,48},{48,64},{64,80},{80,96},{96,112},{112,128},... | collective-permute-start | bytes 1671176 | tf_op jit(solution)/shard_map/ppermute | solution.py:471
  25.3 0.0 copy-start.6
  25.3 9.4 %all_to_all.16.weight_ref = f32[16,1,128]{2,1,0:T(1,128)S(1)} all-to-all(f32[16,1,128]{2,1,0:T(1,128)S(1)} %get-tuple-element.12), channel_id=1, replica_groups=mesh['blk'=32,'shard'=16] {'shard'}, dimensions={0} | all-to-all | bytes 16384 | tf_op jit(solution)/shard_map/all_to_all | solution.py:466
  34.7 0.0 copy-done.6
  34.7 0.0 copy-start.5
  34.7 0.0 copy-start.7
  34.7 0.0 copy-start.8
  34.7 1.2 %lanczos.1 = f32[8,128]{1,0:T(8,128)S(1)} custom-call(f32[8,128]{1,0:T(8,128)S(1)} %get-tuple-element.11.side_ref, f32[16,1,128]{2,1,0:T(1,128)S(1)} %all_to_all.16.weight_ref, f32[16,128]{1,0:T(8,128)S(1)} %copy-done.6), custom_call_target="tpu_custom_call" | custom-call | flops 402653184 | bytes 1048576 | tf_op jit(solution)/shard_map/lanczos/pallas_call | solution.py:499
  35.9 0.0 copy-start.3
  35.9 0.0 collective-permute-done.modes_ref
  35.9 1.3 %collective-permute-start.1 = (f32[8,128]{1,0:T(8,128)S(1)}, f32[8,128]{1,0:T(8,128)S(1)}, u32[]{:S(2)}, u32[]{:S(2)}) collective-permute-start(f32[8,128]{1,0:T(8,128)S(1)} %lanczos.1), channel_id=1, source_target_pairs={{0,16},{16,32},{32,48},{48,64},{64,80},{80,96},{96,112},{112,128},... | collective-permute-start | bytes 12296 | tf_op jit(solution)/shard_map/ppermute | solution.py:471
  37.3 0.0 copy-done.5
  37.3 0.0 copy-done.7
  37.3 0.0 copy-done.8
  37.3 1.9 %disperse.1.modes_ref = f32[128,1024]{1,0:T(8,128)S(1)} custom-call(f32[136,1024]{1,0:T(8,128)S(1)} %collective-permute-done.modes_ref, f32[5,8,128]{2,1,0:T(8,128)S(1)} %copy-done.5, f32[256,256]{1,0:T(8,128)S(1)} %copy-done.8, f32[256,256]{1,0:T(8,128)S(1)} %copy-done.7), custom_call_target="tpu_custom_call" | custom-call | flops 805306368 | bytes 1048576 | tf_op jit(solution)/shard_map/disperse/pallas_call | solution.py:509
  39.2 0.0 collective-permute-done.1.factor_ref
  39.2 0.0 copy-done.3
  39.2 0.5 propagate.1
  39.8 0.0 copy-start
  39.8 0.0 copy-start.1
  39.8 0.0 copy-start.2
  39.8 14.7 %all_to_all.17.in_ref = f32[16,8,1024]{2,1,0:T(8,128)S(1)} all-to-all(f32[16,8,1024]{2,1,0:T(8,128)S(1)} %propagate.1), channel_id=1, replica_groups=mesh['blk'=32,'shard'=16] {'shard'}, dimensions={0} | all-to-all | bytes 1048576 | tf_op jit(solution)/shard_map/all_to_all | solution.py:466
  54.5 0.0 copy-done
  54.5 0.0 copy-done.1
  54.5 0.0 copy-done.2
  54.5 2.2 %kerr.1 = f32[128,1024]{1,0:T(8,128)} custom-call(f32[136,1024]{1,0:T(8,128)S(1)} %collective-permute-done.modes_ref, f32[16,8,1024]{2,1,0:T(8,128)S(1)} %all_to_all.17.in_ref, bf16[128,768]{1,0:T(8,128)(2,1)S(1)} %copy-done.2, f32[5,8,128]{2,1,0:T(8,128)S(1)} %copy-done.5, bf16[2,256,256]{2,1,0:T(8,128)(2,1)S(1)} %copy-done.1, bf16[2,256,256]{2,1,0:T(8,128)(2,1)S(1)} %copy-done), custom_call_target="tpu_custom_call" | custom-call | tf_op jit(solution)/shard_map/kerr/pallas_call | solution.py:527
Async XLA Ops:
  2.4 17.5 %copy-start.4 = (bf16[128,768]{1,0:T(8,128)(2,1)S(1)}, bf16[128,768]{1,0:T(8,128)(2,1)}, u32[]{:S(2)}) copy-start(bf16[128,768]{1,0:T(8,128)(2,1)} %constant.22.clone.mat_ref) | copy-start | bytes 589828
  20.6 15.3 %collective-permute-start = (f32[136,1024]{1,0:T(8,128)S(1)}, f32[136,1024]{1,0:T(8,128)S(1)}, u32[]{:S(2)}, u32[]{:S(2)}) collective-permute-start(f32[136,1024]{1,0:T(8,128)S(1)} %get-tuple-element.10), channel_id=1, source_target_pairs={{0,16},{16,32},{32,48},{48,64},{64,80},{80,96},{96,112},{112,128},... | collective-permute-start | bytes 1671176 | tf_op jit(solution)/shard_map/ppermute | solution.py:471
  25.3 9.4 %copy-start.6 = (f32[16,128]{1,0:T(8,128)S(1)}, f32[16,128]{1,0:T(8,128)}, u32[]{:S(2)}) copy-start(f32[16,128]{1,0:T(8,128)} %constant.24.clone.lam_ref) | copy-start | bytes 24580
  34.7 2.6 %copy-start.5 = (f32[5,8,128]{2,1,0:T(8,128)S(1)}, f32[5,8,128]{2,1,0:T(8,128)}, u32[]{:S(2)}) copy-start(f32[5,8,128]{2,1,0:T(8,128)} %constant.29.clone.tw_ref) | copy-start | bytes 61444
  34.7 2.6 %copy-start.7 = (f32[256,256]{1,0:T(8,128)S(1)}, f32[256,256]{1,0:T(8,128)}, u32[]{:S(2)}) copy-start(f32[256,256]{1,0:T(8,128)} %constant.28.clone.bwd_ref) | copy-start | bytes 786436
  34.7 2.6 %copy-start.8 = (f32[256,256]{1,0:T(8,128)S(1)}, f32[256,256]{1,0:T(8,128)}, u32[]{:S(2)}) copy-start(f32[256,256]{1,0:T(8,128)} %constant.27.clone.fwd_ref) | copy-start | bytes 786436
  35.9 3.3 %copy-start.3 = (bf16[128,768]{1,0:T(8,128)(2,1)S(1)}, bf16[128,768]{1,0:T(8,128)(2,1)}, u32[]{:S(2)}) copy-start(bf16[128,768]{1,0:T(8,128)(2,1)} %constant.23.clone.mat_ref) | copy-start | bytes 589828
  35.9 3.3 %collective-permute-start.1 = (f32[8,128]{1,0:T(8,128)S(1)}, f32[8,128]{1,0:T(8,128)S(1)}, u32[]{:S(2)}, u32[]{:S(2)}) collective-permute-start(f32[8,128]{1,0:T(8,128)S(1)} %lanczos.1), channel_id=1, source_target_pairs={{0,16},{16,32},{32,48},{48,64},{64,80},{80,96},{96,112},{112,128},... | collective-permute-start | bytes 12296 | tf_op jit(solution)/shard_map/ppermute | solution.py:471
  39.8 14.8 %copy-start = (bf16[2,256,256]{2,1,0:T(8,128)(2,1)S(1)}, bf16[2,256,256]{2,1,0:T(8,128)(2,1)}, u32[]{:S(2)}) copy-start(bf16[2,256,256]{2,1,0:T(8,128)(2,1)} %constant.26.clone.bwd_ref) | copy-start | bytes 786436
  39.8 14.8 %copy-start.1 = (bf16[2,256,256]{2,1,0:T(8,128)(2,1)S(1)}, bf16[2,256,256]{2,1,0:T(8,128)(2,1)}, u32[]{:S(2)}) copy-start(bf16[2,256,256]{2,1,0:T(8,128)(2,1)} %constant.25.clone.fwd_ref) | copy-start | bytes 786436
  39.8 14.7 %copy-start.2 = (bf16[128,768]{1,0:T(8,128)(2,1)S(1)}, bf16[128,768]{1,0:T(8,128)(2,1)}, u32[]{:S(2)}) copy-start(bf16[128,768]{1,0:T(8,128)(2,1)} %constant.21.clone.mat_ref) | copy-start | bytes 589828

commit v10 on v9

--- a/solution.py
+++ b/solution.py
@@ -273,7 +273,7 @@
         return modes_ref[64 * part + r0 : 64 * part + r0 + 8, a * NB : (a + 1) * NB]
 
     outer_forward(load, 64, tw_ref, one)
-    two[...] = mm(one[...], fwd_ref[...])
+    two[...] = mm_split(one[...], fwd_ref)
 
     energy = modes_ref[128:129, 64:65]
     dispersion, gain_peak = modes_ref[128:129, 65:66], modes_ref[128:129, 66:67]
@@ -284,7 +284,7 @@
     angle = disp_scale * dispersion * w * w
     filter_spectrum(two, 64, amplitude * jnp.cos(angle), amplitude * jnp.sin(angle))
 
-    one[...] = mm(two[...], bwd_ref[...])
+    one[...] = mm_split(two[...], bwd_ref)
 
     def store(r0, a, re, im):
         out_ref[r0 : r0 + 8, a * NB : (a + 1) * NB] = re
@@ -514,7 +514,7 @@
         scratch_shapes=[pltpu.VMEM((512, 256), F32)] * 2,
         cost_estimate=cost(6 * 4 * 512 * 256 * 256, 2**20),
         name="disperse",
-    )(hold(shifted), *(near_tables[name] for name in ("lines", "forward", "backward")))
+    )(hold(shifted), *(near_tables[name] for name in ("lines", "forward_split", "backward_split")))
     xback = pl.pallas_call(
         propagate_kernel,
         out_shape=near(NS, 8, NT),

time: 57 us -> 56.8 us (level)
  the two profiles are of different devices: /device:TPU:97 before, /device:TPU:8 now
where the time goes in v10:
time: 56.8 us; the launch traced here: 56.5 us
  blocking collectives  41.6 us (73%)
  Pallas kernels  7.4 us (13%)
  waiting for transfers between devices  6.67 us (12%)
  between operations  0.75 us (1%)
    all_to_all x3, blocking collectives, exchange(): lax.all_to_all(value, 'shard', split_axis=0, concat_axis=0, tiled=True)  41.6 us
    ppermute x2, waiting for transfers between devices, pass_on(): lax.ppermute(value, 'blk', [(b, (b + 1) % count) for b in range(count)])  6.67 us
    pallas_call x1, Pallas kernels, per_device(): pl.pallas_call(kerr_kernel, out_shape=jax.ShapeDtypeStruct((128, NT), F32...  2.21 us
    pallas_call x1, Pallas kernels, per_device(): pl.pallas_call(ymode_kernel, out_shape=near(NS, 65, 1, 128), in_specs=[VM...  1.77 us
    pallas_call x1, Pallas kernels, per_device(): pl.pallas_call(lanczos_kernel, out_shape=near(8, 128), in_specs=[VMEM] *...  1.2 us
  transfers between devices with their start and end apart: 2, of which 2 were waited for; matrix products, arithmetic and copies ran while one was open for 0% of the time, Pallas kernels for 4%

profile of v10, /device:TPU:8, one launch (start us, length us, event | category | flops | bytes accessed | tf_op | source)
XLA Modules:
  0.0 56.5 jit_solution(11762094702696897338)
XLA Ops:
  0.7 1.8 %ymode.1 = f32[16,65,1,128]{3,2,1,0:T(1,128)S(1)} custom-call(f32[128,1024]{1,0:T(8,128)} %bitcast.8, bf16[128,768]{1,0:T(8,128)(2,1)} %constant.16.clone.mat_ref, f32[16,128]{1,0:T(8,128)} %constant.20.clone.lam_ref, s32[1,1]{1,0:T(1,128)} %bitcast.7.kind_ref, f32[1,32]{1,0:T(1,128)} %bitcast.9, f32[1,32]{1,0:T(1,128)} %bitcast.10, f32[1,32]{1,0:T(1,128)} %bitcast.11, ...), custom_call_target="tpu_custom_call" | custom-call | tf_op jit(solution)/shard_map/ymode/pallas_call | solution.py:479
  2.4 0.0 copy-start.4
  2.4 17.8 %all_to_all.15.in_ref = f32[16,65,1,128]{3,2,1,0:T(1,128)S(1)} all-to-all(f32[16,65,1,128]{3,2,1,0:T(1,128)S(1)} %ymode.1), channel_id=1, replica_groups=mesh['blk'=32,'shard'=16] {'shard'}, dimensions={0} | all-to-all | bytes 1064960 | tf_op jit(solution)/shard_map/all_to_all | solution.py:466
  20.2 0.0 copy-done.4
  20.2 0.7 %xmode.1 = (f32[136,1024]{1,0:T(8,128)S(1)}, f32[8,128]{1,0:T(8,128)S(1)}, f32[16,1,128]{2,1,0:T(1,128)S(1)}) custom-call(f32[16,65,1,128]{3,2,1,0:T(1,128)S(1)} %all_to_all.15.in_ref, bf16[128,768]{1,0:T(8,128)(2,1)S(1)} %copy-done.4), custom_call_target="tpu_custom_call" | custom-call | tf_op jit(solution)/shard_map/xmode/pallas_call | solution.py:490
  20.9 0.0 collective-permute-start
  20.9 0.0 copy-start.6
  20.9 10.6 %all_to_all.16.weight_ref = f32[16,1,128]{2,1,0:T(1,128)S(1)} all-to-all(f32[16,1,128]{2,1,0:T(1,128)S(1)} %get-tuple-element.12), channel_id=1, replica_groups=mesh['blk'=32,'shard'=16] {'shard'}, dimensions={0} | all-to-all | bytes 16384 | tf_op jit(solution)/shard_map/all_to_all | solution.py:466
  31.6 0.0 copy-done.6
  31.6 0.0 copy-start
  31.6 0.0 copy-start.1
  31.6 0.0 copy-start.5
  31.6 1.2 %lanczos.1 = f32[8,128]{1,0:T(8,128)S(1)} custom-call(f32[8,128]{1,0:T(8,128)S(1)} %get-tuple-element.11.side_ref, f32[16,1,128]{2,1,0:T(1,128)S(1)} %all_to_all.16.weight_ref, f32[16,128]{1,0:T(8,128)S(1)} %copy-done.6), custom_call_target="tpu_custom_call" | custom-call | flops 402653184 | bytes 1048576 | tf_op jit(solution)/shard_map/lanczos/pallas_call | solution.py:499
  32.8 0.0 copy-start.3
  32.8 3.0 %collective-permute-done.modes_ref = f32[136,1024]{1,0:T(8,128)S(1)} collective-permute-done((f32[136,1024]{1,0:T(8,128)S(1)}, f32[136,1024]{1,0:T(8,128)S(1)}, u32[]{:S(2)}, u32[]{:S(2)}) %collective-permute-start) | collective-permute-done | bytes 557088 | tf_op jit(solution)/shard_map/ppermute | solution.py:471
  35.8 0.0 collective-permute-start.1
  35.8 0.0 copy-done
  35.8 0.0 copy-done.1
  35.8 0.0 copy-done.5
  35.8 1.0 %disperse.1.modes_ref = f32[128,1024]{1,0:T(8,128)S(1)} custom-call(f32[136,1024]{1,0:T(8,128)S(1)} %collective-permute-done.modes_ref, f32[5,8,128]{2,1,0:T(8,128)S(1)} %copy-done.5, bf16[2,256,256]{2,1,0:T(8,128)(2,1)S(1)} %copy-done.1, bf16[2,256,256]{2,1,0:T(8,128)(2,1)S(1)} %copy-done), custom_call_target="tpu_custom_call" | custom-call | flops 805306368 | bytes 1048576 | tf_op jit(solution)/shard_map/disperse/pallas_call | solution.py:509
  36.8 3.7 %collective-permute-done.1.factor_ref = f32[8,128]{1,0:T(8,128)S(1)} collective-permute-done((f32[8,128]{1,0:T(8,128)S(1)}, f32[8,128]{1,0:T(8,128)S(1)}, u32[]{:S(2)}, u32[]{:S(2)}) %collective-permute-start.1) | collective-permute-done | bytes 4128 | tf_op jit(solution)/shard_map/ppermute | solution.py:471
  40.5 0.0 copy-done.3
  40.5 0.5 propagate.1
  41.1 0.0 copy-start.2
  41.1 13.2 %all_to_all.17.in_ref = f32[16,8,1024]{2,1,0:T(8,128)S(1)} all-to-all(f32[16,8,1024]{2,1,0:T(8,128)S(1)} %propagate.1), channel_id=1, replica_groups=mesh['blk'=32,'shard'=16] {'shard'}, dimensions={0} | all-to-all | bytes 1048576 | tf_op jit(solution)/shard_map/all_to_all | solution.py:466
  54.3 0.0 copy-done.2
  54.3 2.2 %kerr.1 = f32[128,1024]{1,0:T(8,128)} custom-call(f32[136,1024]{1,0:T(8,128)S(1)} %collective-permute-done.modes_ref, f32[16,8,1024]{2,1,0:T(8,128)S(1)} %all_to_all.17.in_ref, bf16[128,768]{1,0:T(8,128)(2,1)S(1)} %copy-done.2, f32[5,8,128]{2,1,0:T(8,128)S(1)} %copy-done.5, bf16[2,256,256]{2,1,0:T(8,128)(2,1)S(1)} %copy-done.1, bf16[2,256,256]{2,1,0:T(8,128)(2,1)S(1)} %copy-done), custom_call_target="tpu_custom_call" | custom-call | tf_op jit(solution)/shard_map/kerr/pallas_call | solution.py:527
Async XLA Ops:
  2.4 17.8 %copy-start.4 = (bf16[128,768]{1,0:T(8,128)(2,1)S(1)}, bf16[128,768]{1,0:T(8,128)(2,1)}, u32[]{:S(2)}) copy-start(bf16[128,768]{1,0:T(8,128)(2,1)} %constant.18.clone.mat_ref) | copy-start | bytes 589828
  20.9 14.9 %collective-permute-start = (f32[136,1024]{1,0:T(8,128)S(1)}, f32[136,1024]{1,0:T(8,128)S(1)}, u32[]{:S(2)}, u32[]{:S(2)}) collective-permute-start(f32[136,1024]{1,0:T(8,128)S(1)} %get-tuple-element.10), channel_id=1, source_target_pairs={{0,16},{16,32},{32,48},{48,64},{64,80},{80,96},{96,112},{112,128},... | collective-permute-start | bytes 1671176 | tf_op jit(solution)/shard_map/ppermute | solution.py:471
  20.9 10.6 %copy-start.6 = (f32[16,128]{1,0:T(8,128)S(1)}, f32[16,128]{1,0:T(8,128)}, u32[]{:S(2)}) copy-start(f32[16,128]{1,0:T(8,128)} %constant.20.clone.lam_ref) | copy-start | bytes 24580
  31.6 4.2 %copy-start = (bf16[2,256,256]{2,1,0:T(8,128)(2,1)S(1)}, bf16[2,256,256]{2,1,0:T(8,128)(2,1)}, u32[]{:S(2)}) copy-start(bf16[2,256,256]{2,1,0:T(8,128)(2,1)} %constant.22.clone.bwd_ref) | copy-start | bytes 786436
  31.6 4.2 %copy-start.1 = (bf16[2,256,256]{2,1,0:T(8,128)(2,1)S(1)}, bf16[2,256,256]{2,1,0:T(8,128)(2,1)}, u32[]{:S(2)}) copy-start(bf16[2,256,256]{2,1,0:T(8,128)(2,1)} %constant.21.clone.fwd_ref) | copy-start | bytes 786436
  31.6 4.2 %copy-start.5 = (f32[5,8,128]{2,1,0:T(8,128)S(1)}, f32[5,8,128]{2,1,0:T(8,128)}, u32[]{:S(2)}) copy-start(f32[5,8,128]{2,1,0:T(8,128)} %constant.23.clone.tw_ref) | copy-start | bytes 61444
  32.8 7.7 %copy-start.3 = (bf16[128,768]{1,0:T(8,128)(2,1)S(1)}, bf16[128,768]{1,0:T(8,128)(2,1)}, u32[]{:S(2)}) copy-start(bf16[128,768]{1,0:T(8,128)(2,1)} %constant.19.clone.mat_ref) | copy-start | bytes 589828
  35.8 4.7 %collective-permute-start.1 = (f32[8,128]{1,0:T(8,128)S(1)}, f32[8,128]{1,0:T(8,128)S(1)}, u32[]{:S(2)}, u32[]{:S(2)}) collective-permute-start(f32[8,128]{1,0:T(8,128)S(1)} %lanczos.1), channel_id=1, source_target_pairs={{0,16},{16,32},{32,48},{48,64},{64,80},{80,96},{96,112},{112,128},... | collective-permute-start | bytes 12296 | tf_op jit(solution)/shard_map/ppermute | solution.py:471
  41.1 13.2 %copy-start.2 = (bf16[128,768]{1,0:T(8,128)(2,1)S(1)}, bf16[128,768]{1,0:T(8,128)(2,1)}, u32[]{:S(2)}) copy-start(bf16[128,768]{1,0:T(8,128)(2,1)} %constant.17.clone.mat_ref) | copy-start | bytes 589828

commit v11 on v10

--- a/solution.py
+++ b/solution.py
@@ -104,12 +104,12 @@
     rest = table - high.astype(np.float32)
     middle = rest.astype(jnp.bfloat16)
     low = (rest - middle.astype(np.float32)).astype(jnp.bfloat16)
-    return np.concatenate([high, middle, low, high, middle, high], axis=1)
+    return np.concatenate([high, middle, high], axis=1)
 
 
 def mm_wide(table, b):
     high, middle, low = parts_of(b)
-    stacked = jnp.concatenate([high, high, high, middle, middle, low], axis=0)
+    stacked = jnp.concatenate([high, high, middle], axis=0)
     return jnp.dot(table, stacked, preferred_element_type=F32)
 
 

time: 56.8 us -> 56.4 us (level)
  no operation moved by 1% of the time
where the time goes in v11:
time: 56.4 us; the launch traced here: 56.1 us
  blocking collectives  41.6 us (74%)
  Pallas kernels  7.02 us (12%)
  waiting for transfers between devices  6.67 us (12%)
  between operations  0.75 us (1%)
    all_to_all x3, blocking collectives, exchange(): lax.all_to_all(value, 'shard', split_axis=0, concat_axis=0, tiled=True)  41.6 us
    ppermute x2, waiting for transfers between devices, pass_on(): lax.ppermute(value, 'blk', [(b, (b + 1) % count) for b in range(count)])  6.67 us
    pallas_call x1, Pallas kernels, per_device(): pl.pallas_call(kerr_kernel, out_shape=jax.ShapeDtypeStruct((128, NT), F32...  2.14 us
    pallas_call x1, Pallas kernels, per_device(): pl.pallas_call(ymode_kernel, out_shape=near(NS, 65, 1, 128), in_specs=[VM...  1.64 us
    pallas_call x1, Pallas kernels, per_device(): pl.pallas_call(lanczos_kernel, out_shape=near(8, 128), in_specs=[VMEM] *...  1.2 us
  transfers between devices with their start and end apart: 2, of which 2 were waited for; matrix products, arithmetic and copies ran while one was open for 0% of the time, Pallas kernels for 4%

profile of v11, /device:TPU:8, one launch (start us, length us, event | category | flops | bytes accessed | tf_op | source)
XLA Modules:
  0.0 56.1 jit_solution(18324822930300473264)
XLA Ops:
  0.7 1.6 %ymode.1 = f32[16,65,1,128]{3,2,1,0:T(1,128)S(1)} custom-call(f32[128,1024]{1,0:T(8,128)} %bitcast.8, bf16[128,384]{1,0:T(8,128)(2,1)} %constant.16.clone.mat_ref, f32[16,128]{1,0:T(8,128)} %constant.20.clone.lam_ref, s32[1,1]{1,0:T(1,128)} %bitcast.7.kind_ref, f32[1,32]{1,0:T(1,128)} %bitcast.9, f32[1,32]{1,0:T(1,128)} %bitcast.10, f32[1,32]{1,0:T(1,128)} %bitcast.11, ...), custom_call_target="tpu_custom_call" | custom-call | tf_op jit(solution)/shard_map/ymode/pallas_call | solution.py:479
  2.3 0.0 copy-start.4
  2.3 17.8 %all_to_all.15.in_ref = f32[16,65,1,128]{3,2,1,0:T(1,128)S(1)} all-to-all(f32[16,65,1,128]{3,2,1,0:T(1,128)S(1)} %ymode.1), channel_id=1, replica_groups=mesh['blk'=32,'shard'=16] {'shard'}, dimensions={0} | all-to-all | bytes 1064960 | tf_op jit(solution)/shard_map/all_to_all | solution.py:466
  20.1 0.0 copy-done.4
  20.1 0.6 %xmode.1 = (f32[136,1024]{1,0:T(8,128)S(1)}, f32[8,128]{1,0:T(8,128)S(1)}, f32[16,1,128]{2,1,0:T(1,128)S(1)}) custom-call(f32[16,65,1,128]{3,2,1,0:T(1,128)S(1)} %all_to_all.15.in_ref, bf16[128,384]{1,0:T(8,128)(2,1)S(1)} %copy-done.4), custom_call_target="tpu_custom_call" | custom-call | tf_op jit(solution)/shard_map/xmode/pallas_call | solution.py:490
  20.7 0.0 collective-permute-start
  20.7 0.0 copy-start.6
  20.7 10.6 %all_to_all.16.weight_ref = f32[16,1,128]{2,1,0:T(1,128)S(1)} all-to-all(f32[16,1,128]{2,1,0:T(1,128)S(1)} %get-tuple-element.12), channel_id=1, replica_groups=mesh['blk'=32,'shard'=16] {'shard'}, dimensions={0} | all-to-all | bytes 16384 | tf_op jit(solution)/shard_map/all_to_all | solution.py:466
  31.4 0.0 copy-done.6
  31.4 0.0 copy-start
  31.4 0.0 copy-start.1
  31.4 0.0 copy-start.5
  31.4 1.2 %lanczos.1 = f32[8,128]{1,0:T(8,128)S(1)} custom-call(f32[8,128]{1,0:T(8,128)S(1)} %get-tuple-element.11.side_ref, f32[16,1,128]{2,1,0:T(1,128)S(1)} %all_to_all.16.weight_ref, f32[16,128]{1,0:T(8,128)S(1)} %copy-done.6), custom_call_target="tpu_custom_call" | custom-call | flops 402653184 | bytes 1048576 | tf_op jit(solution)/shard_map/lanczos/pallas_call | solution.py:499
  32.6 0.0 copy-start.3
  32.6 3.0 %collective-permute-done.modes_ref = f32[136,1024]{1,0:T(8,128)S(1)} collective-permute-done((f32[136,1024]{1,0:T(8,128)S(1)}, f32[136,1024]{1,0:T(8,128)S(1)}, u32[]{:S(2)}, u32[]{:S(2)}) %collective-permute-start) | collective-permute-done | bytes 557088 | tf_op jit(solution)/shard_map/ppermute | solution.py:471
  35.6 0.0 collective-permute-start.1
  35.6 0.0 copy-done
  35.6 0.0 copy-done.1
  35.6 0.0 copy-done.5
  35.6 1.0 %disperse.1.modes_ref = f32[128,1024]{1,0:T(8,128)S(1)} custom-call(f32[136,1024]{1,0:T(8,128)S(1)} %collective-permute-done.modes_ref, f32[5,8,128]{2,1,0:T(8,128)S(1)} %copy-done.5, bf16[2,256,256]{2,1,0:T(8,128)(2,1)S(1)} %copy-done.1, bf16[2,256,256]{2,1,0:T(8,128)(2,1)S(1)} %copy-done), custom_call_target="tpu_custom_call" | custom-call | flops 805306368 | bytes 1048576 | tf_op jit(solution)/shard_map/disperse/pallas_call | solution.py:509
  36.6 3.7 %collective-permute-done.1.factor_ref = f32[8,128]{1,0:T(8,128)S(1)} collective-permute-done((f32[8,128]{1,0:T(8,128)S(1)}, f32[8,128]{1,0:T(8,128)S(1)}, u32[]{:S(2)}, u32[]{:S(2)}) %collective-permute-start.1) | collective-permute-done | bytes 4128 | tf_op jit(solution)/shard_map/ppermute | solution.py:471
  40.3 0.0 copy-done.3
  40.3 0.4 propagate.1
  40.7 0.0 copy-start.2
  40.7 13.2 %all_to_all.17.in_ref = f32[16,8,1024]{2,1,0:T(8,128)S(1)} all-to-all(f32[16,8,1024]{2,1,0:T(8,128)S(1)} %propagate.1), channel_id=1, replica_groups=mesh['blk'=32,'shard'=16] {'shard'}, dimensions={0} | all-to-all | bytes 1048576 | tf_op jit(solution)/shard_map/all_to_all | solution.py:466
  54.0 0.0 copy-done.2
  54.0 2.1 %kerr.1 = f32[128,1024]{1,0:T(8,128)} custom-call(f32[136,1024]{1,0:T(8,128)S(1)} %collective-permute-done.modes_ref, f32[16,8,1024]{2,1,0:T(8,128)S(1)} %all_to_all.17.in_ref, bf16[128,384]{1,0:T(8,128)(2,1)S(1)} %copy-done.2, f32[5,8,128]{2,1,0:T(8,128)S(1)} %copy-done.5, bf16[2,256,256]{2,1,0:T(8,128)(2,1)S(1)} %copy-done.1, bf16[2,256,256]{2,1,0:T(8,128)(2,1)S(1)} %copy-done), custom_call_target="tpu_custom_call" | custom-call | tf_op jit(solution)/shard_map/kerr/pallas_call | solution.py:527
Async XLA Ops:
  2.3 17.8 %copy-start.4 = (bf16[128,384]{1,0:T(8,128)(2,1)S(1)}, bf16[128,384]{1,0:T(8,128)(2,1)}, u32[]{:S(2)}) copy-start(bf16[128,384]{1,0:T(8,128)(2,1)} %constant.18.clone.mat_ref) | copy-start | bytes 294916
  20.7 14.9 %collective-permute-start = (f32[136,1024]{1,0:T(8,128)S(1)}, f32[136,1024]{1,0:T(8,128)S(1)}, u32[]{:S(2)}, u32[]{:S(2)}) collective-permute-start(f32[136,1024]{1,0:T(8,128)S(1)} %get-tuple-element.10), channel_id=1, source_target_pairs={{0,16},{16,32},{32,48},{48,64},{64,80},{80,96},{96,112},{112,128},... | collective-permute-start | bytes 1671176 | tf_op jit(solution)/shard_map/ppermute | solution.py:471
  20.7 10.7 %copy-start.6 = (f32[16,128]{1,0:T(8,128)S(1)}, f32[16,128]{1,0:T(8,128)}, u32[]{:S(2)}) copy-start(f32[16,128]{1,0:T(8,128)} %constant.20.clone.lam_ref) | copy-start | bytes 24580
  31.4 4.2 %copy-start = (bf16[2,256,256]{2,1,0:T(8,128)(2,1)S(1)}, bf16[2,256,256]{2,1,0:T(8,128)(2,1)}, u32[]{:S(2)}) copy-start(bf16[2,256,256]{2,1,0:T(8,128)(2,1)} %constant.22.clone.bwd_ref) | copy-start | bytes 786436
  31.4 4.2 %copy-start.1 = (bf16[2,256,256]{2,1,0:T(8,128)(2,1)S(1)}, bf16[2,256,256]{2,1,0:T(8,128)(2,1)}, u32[]{:S(2)}) copy-start(bf16[2,256,256]{2,1,0:T(8,128)(2,1)} %constant.21.clone.fwd_ref) | copy-start | bytes 786436
  31.4 4.2 %copy-start.5 = (f32[5,8,128]{2,1,0:T(8,128)S(1)}, f32[5,8,128]{2,1,0:T(8,128)}, u32[]{:S(2)}) copy-start(f32[5,8,128]{2,1,0:T(8,128)} %constant.23.clone.tw_ref) | copy-start | bytes 61444
  32.6 7.7 %copy-start.3 = (bf16[128,384]{1,0:T(8,128)(2,1)S(1)}, bf16[128,384]{1,0:T(8,128)(2,1)}, u32[]{:S(2)}) copy-start(bf16[128,384]{1,0:T(8,128)(2,1)} %constant.19.clone.mat_ref) | copy-start | bytes 294916
  35.6 4.7 %collective-permute-start.1 = (f32[8,128]{1,0:T(8,128)S(1)}, f32[8,128]{1,0:T(8,128)S(1)}, u32[]{:S(2)}, u32[]{:S(2)}) collective-permute-start(f32[8,128]{1,0:T(8,128)S(1)} %lanczos.1), channel_id=1, source_target_pairs={{0,16},{16,32},{32,48},{48,64},{64,80},{80,96},{96,112},{112,128},... | collective-permute-start | bytes 12296 | tf_op jit(solution)/shard_map/ppermute | solution.py:471
  40.7 13.2 %copy-start.2 = (bf16[128,384]{1,0:T(8,128)(2,1)S(1)}, bf16[128,384]{1,0:T(8,128)(2,1)}, u32[]{:S(2)}) copy-start(bf16[128,384]{1,0:T(8,128)(2,1)} %constant.17.clone.mat_ref) | copy-start | bytes 294916

commit v12 on v11

--- a/solution.py
+++ b/solution.py
@@ -504,7 +504,6 @@
         cost_estimate=cost(6 * 2 * 512 * 256 * 256, 2**20),
         name="lanczos",
     )(hold(side), hold(weights), near_tables["lam_all"])
-    shifted, factor = lax.optimization_barrier((shifted, factor))
     factor = pass_on(factor)
     dispersed = pl.pallas_call(
         disperse_kernel,

time: 56.4 us -> 56.4 us (level)
  starting transfers between devices: 0.02 us -> 0.78 us
  waiting for transfers between devices: 6.67 us -> 5.91 us
    ppermute x2, waiting for transfers between devices: 6.67 us -> 5.91 us  [pass_on(): lax.ppermute(value, 'blk', [(b, (b + 1) % count) for b in range(count)])]
    ppermute x2, starting transfers between devices: 0.02 us -> 0.78 us  [pass_on(): lax.ppermute(value, 'blk', [(b, (b + 1) % count) for b in range(count)])]
where the time goes in v12:
time: 56.4 us; the launch traced here: 56.1 us
  blocking collectives  41.6 us (74%)
  Pallas kernels  7.03 us (12%)
  waiting for transfers between devices  5.91 us (10%)
  starting transfers between devices  0.78 us (1%)
  between operations  0.74 us (1%)
    all_to_all x3, blocking collectives, exchange(): lax.all_to_all(value, 'shard', split_axis=0, concat_axis=0, tiled=True)  41.6 us
    ppermute x2, waiting for transfers between devices, pass_on(): lax.ppermute(value, 'blk', [(b, (b + 1) % count) for b in range(count)])  5.91 us
    pallas_call x1, Pallas kernels, per_device(): pl.pallas_call(kerr_kernel, out_shape=jax.ShapeDtypeStruct((128, NT), F32...  2.15 us
    pallas_call x1, Pallas kernels, per_device(): pl.pallas_call(ymode_kernel, out_shape=near(NS, 65, 1, 128), in_specs=[VM...  1.64 us
    pallas_call x1, Pallas kernels, per_device(): pl.pallas_call(lanczos_kernel, out_shape=near(8, 128), in_specs=[VMEM] *...  1.2 us
  transfers between devices with their start and end apart: 2, of which 2 were waited for; matrix products, arithmetic and copies ran while one was open for 0% of the time, Pallas kernels for 4%

profile of v12, /device:TPU:8, one launch (start us, length us, event | category | flops | bytes accessed | tf_op | source)
XLA Modules:
  0.0 56.1 jit_solution(3719431824842520085)
XLA Ops:
  0.7 1.6 %ymode.1 = f32[16,65,1,128]{3,2,1,0:T(1,128)S(1)} custom-call(f32[128,1024]{1,0:T(8,128)} %bitcast.8, bf16[128,384]{1,0:T(8,128)(2,1)} %constant.16.clone.mat_ref, f32[16,128]{1,0:T(8,128)} %constant.20.clone.lam_ref, s32[1,1]{1,0:T(1,128)} %bitcast.7.kind_ref, f32[1,32]{1,0:T(1,128)} %bitcast.9, f32[1,32]{1,0:T(1,128)} %bitcast.10, f32[1,32]{1,0:T(1,128)} %bitcast.11, ...), custom_call_target="tpu_custom_call" | custom-call | tf_op jit(solution)/shard_map/ymode/pallas_call | solution.py:479
  2.3 0.0 copy-start.4
  2.3 17.8 %all_to_all.15.in_ref = f32[16,65,1,128]{3,2,1,0:T(1,128)S(1)} all-to-all(f32[16,65,1,128]{3,2,1,0:T(1,128)S(1)} %ymode.1), channel_id=1, replica_groups=mesh['blk'=32,'shard'=16] {'shard'}, dimensions={0} | all-to-all | bytes 1064960 | tf_op jit(solution)/shard_map/all_to_all | solution.py:466
  20.1 0.0 copy-done.4
  20.1 0.6 %xmode.1 = (f32[136,1024]{1,0:T(8,128)S(1)}, f32[8,128]{1,0:T(8,128)S(1)}, f32[16,1,128]{2,1,0:T(1,128)S(1)}) custom-call(f32[16,65,1,128]{3,2,1,0:T(1,128)S(1)} %all_to_all.15.in_ref, bf16[128,384]{1,0:T(8,128)(2,1)S(1)} %copy-done.4), custom_call_target="tpu_custom_call" | custom-call | tf_op jit(solution)/shard_map/xmode/pallas_call | solution.py:490
  20.7 0.0 collective-permute-start
  20.7 0.0 copy-start.6
  20.7 10.6 %all_to_all.16.weight_ref = f32[16,1,128]{2,1,0:T(1,128)S(1)} all-to-all(f32[16,1,128]{2,1,0:T(1,128)S(1)} %get-tuple-element.10), channel_id=1, replica_groups=mesh['blk'=32,'shard'=16] {'shard'}, dimensions={0} | all-to-all | bytes 16384 | tf_op jit(solution)/shard_map/all_to_all | solution.py:466
  31.4 0.0 copy-done.6
  31.4 0.0 copy-start
  31.4 0.0 copy-start.1
  31.4 0.0 copy-start.5
  31.4 1.2 %lanczos.1 = f32[8,128]{1,0:T(8,128)S(1)} custom-call(f32[8,128]{1,0:T(8,128)S(1)} %get-tuple-element.9.side_ref, f32[16,1,128]{2,1,0:T(1,128)S(1)} %all_to_all.16.weight_ref, f32[16,128]{1,0:T(8,128)S(1)} %copy-done.6), custom_call_target="tpu_custom_call" | custom-call | flops 402653184 | bytes 1048576 | tf_op jit(solution)/shard_map/lanczos/pallas_call | solution.py:499
  32.6 0.0 copy-start.3
  32.6 0.8 %collective-permute-start.1 = (f32[8,128]{1,0:T(8,128)S(1)}, f32[8,128]{1,0:T(8,128)S(1)}, u32[]{:S(2)}, u32[]{:S(2)}) collective-permute-start(f32[8,128]{1,0:T(8,128)S(1)} %lanczos.1), channel_id=1, source_target_pairs={{0,16},{16,32},{32,48},{48,64},{64,80},{80,96},{96,112},{112,128},... | collective-permute-start | bytes 12296 | tf_op jit(solution)/shard_map/ppermute | solution.py:471
  33.4 2.2 %collective-permute-done.modes_ref = f32[136,1024]{1,0:T(8,128)S(1)} collective-permute-done((f32[136,1024]{1,0:T(8,128)S(1)}, f32[136,1024]{1,0:T(8,128)S(1)}, u32[]{:S(2)}, u32[]{:S(2)}) %collective-permute-start) | collective-permute-done | bytes 557088 | tf_op jit(solution)/shard_map/ppermute | solution.py:471
  35.6 0.0 copy-done
  35.6 0.0 copy-done.1
  35.6 0.0 copy-done.5
  35.6 1.0 %disperse.1.modes_ref = f32[128,1024]{1,0:T(8,128)S(1)} custom-call(f32[136,1024]{1,0:T(8,128)S(1)} %collective-permute-done.modes_ref, f32[5,8,128]{2,1,0:T(8,128)S(1)} %copy-done.5, bf16[2,256,256]{2,1,0:T(8,128)(2,1)S(1)} %copy-done.1, bf16[2,256,256]{2,1,0:T(8,128)(2,1)S(1)} %copy-done), custom_call_target="tpu_custom_call" | custom-call | flops 805306368 | bytes 1048576 | tf_op jit(solution)/shard_map/disperse/pallas_call | solution.py:508
  36.6 3.7 %collective-permute-done.1.factor_ref = f32[8,128]{1,0:T(8,128)S(1)} collective-permute-done((f32[8,128]{1,0:T(8,128)S(1)}, f32[8,128]{1,0:T(8,128)S(1)}, u32[]{:S(2)}, u32[]{:S(2)}) %collective-permute-start.1) | collective-permute-done | bytes 4128 | tf_op jit(solution)/shard_map/ppermute | solution.py:471
  40.3 0.0 copy-done.3
  40.3 0.4 propagate.1
  40.7 0.0 copy-start.2
  40.7 13.2 %all_to_all.17.in_ref = f32[16,8,1024]{2,1,0:T(8,128)S(1)} all-to-all(f32[16,8,1024]{2,1,0:T(8,128)S(1)} %propagate.1), channel_id=1, replica_groups=mesh['blk'=32,'shard'=16] {'shard'}, dimensions={0} | all-to-all | bytes 1048576 | tf_op jit(solution)/shard_map/all_to_all | solution.py:466
  54.0 0.0 copy-done.2
  54.0 2.1 %kerr.1 = f32[128,1024]{1,0:T(8,128)} custom-call(f32[136,1024]{1,0:T(8,128)S(1)} %collective-permute-done.modes_ref, f32[16,8,1024]{2,1,0:T(8,128)S(1)} %all_to_all.17.in_ref, bf16[128,384]{1,0:T(8,128)(2,1)S(1)} %copy-done.2, f32[5,8,128]{2,1,0:T(8,128)S(1)} %copy-done.5, bf16[2,256,256]{2,1,0:T(8,128)(2,1)S(1)} %copy-done.1, bf16[2,256,256]{2,1,0:T(8,128)(2,1)S(1)} %copy-done), custom_call_target="tpu_custom_call" | custom-call | tf_op jit(solution)/shard_map/kerr/pallas_call | solution.py:526
Async XLA Ops:
  2.3 17.8 %copy-start.4 = (bf16[128,384]{1,0:T(8,128)(2,1)S(1)}, bf16[128,384]{1,0:T(8,128)(2,1)}, u32[]{:S(2)}) copy-start(bf16[128,384]{1,0:T(8,128)(2,1)} %constant.18.clone.mat_ref) | copy-start | bytes 294916
  20.7 14.9 %collective-permute-start = (f32[136,1024]{1,0:T(8,128)S(1)}, f32[136,1024]{1,0:T(8,128)S(1)}, u32[]{:S(2)}, u32[]{:S(2)}) collective-permute-start(f32[136,1024]{1,0:T(8,128)S(1)} %get-tuple-element.8), channel_id=1, source_target_pairs={{0,16},{16,32},{32,48},{48,64},{64,80},{80,96},{96,112},{112,128},... | collective-permute-start | bytes 1671176 | tf_op jit(solution)/shard_map/ppermute | solution.py:471
  20.7 10.7 %copy-start.6 = (f32[16,128]{1,0:T(8,128)S(1)}, f32[16,128]{1,0:T(8,128)}, u32[]{:S(2)}) copy-start(f32[16,128]{1,0:T(8,128)} %constant.20.clone.lam_ref) | copy-start | bytes 24580
  31.4 4.2 %copy-start = (bf16[2,256,256]{2,1,0:T(8,128)(2,1)S(1)}, bf16[2,256,256]{2,1,0:T(8,128)(2,1)}, u32[]{:S(2)}) copy-start(bf16[2,256,256]{2,1,0:T(8,128)(2,1)} %constant.22.clone.bwd_ref) | copy-start | bytes 786436
  31.4 4.2 %copy-start.1 = (bf16[2,256,256]{2,1,0:T(8,128)(2,1)S(1)}, bf16[2,256,256]{2,1,0:T(8,128)(2,1)}, u32[]{:S(2)}) copy-start(bf16[2,256,256]{2,1,0:T(8,128)(2,1)} %constant.21.clone.fwd_ref) | copy-start | bytes 786436
  31.4 4.2 %copy-start.5 = (f32[5,8,128]{2,1,0:T(8,128)S(1)}, f32[5,8,128]{2,1,0:T(8,128)}, u32[]{:S(2)}) copy-start(f32[5,8,128]{2,1,0:T(8,128)} %constant.23.clone.tw_ref) | copy-start | bytes 61444
  32.6 7.7 %copy-start.3 = (bf16[128,384]{1,0:T(8,128)(2,1)S(1)}, bf16[128,384]{1,0:T(8,128)(2,1)}, u32[]{:S(2)}) copy-start(bf16[128,384]{1,0:T(8,128)(2,1)} %constant.19.clone.mat_ref) | copy-start | bytes 294916
  32.6 7.7 %collective-permute-start.1 = (f32[8,128]{1,0:T(8,128)S(1)}, f32[8,128]{1,0:T(8,128)S(1)}, u32[]{:S(2)}, u32[]{:S(2)}) collective-permute-start(f32[8,128]{1,0:T(8,128)S(1)} %lanczos.1), channel_id=1, source_target_pairs={{0,16},{16,32},{32,48},{48,64},{64,80},{80,96},{96,112},{112,128},... | collective-permute-start | bytes 12296 | tf_op jit(solution)/shard_map/ppermute | solution.py:471
  40.7 13.2 %copy-start.2 = (bf16[128,384]{1,0:T(8,128)(2,1)S(1)}, bf16[128,384]{1,0:T(8,128)(2,1)}, u32[]{:S(2)}) copy-start(bf16[128,384]{1,0:T(8,128)(2,1)} %constant.17.clone.mat_ref) | copy-start | bytes 294916

commit v13 on v12

--- a/solution.py
+++ b/solution.py
@@ -410,34 +410,39 @@
     kerr = modes_ref[128:129, 68:69]
     field[...] = mm_wide(mat_ref[...], in_ref[...].reshape(128, NT))
 
-    def load(side, r0, a):
-        lanes = slice(a * NB, (a + 1) * NB)
-        re = field[32 * side + r0 : 32 * side + r0 + 8, lanes]
-        im = field[64 + 32 * side + r0 : 64 + 32 * side + r0 + 8, lanes]
-        return re * re + im * im
-
-    outer_forward(load, 32, tw_ref, one)
-    two[...] = mm_split(one[...], fwd_ref)
-    filter_spectrum(two, 32, tw_ref[3], tw_ref[4])
-    one[...] = mm_split(two[...], bwd_ref)
-
-    def store(r0, a, re, im):
-        lanes = slice(a * NB, (a + 1) * NB)
-        delayed[r0 : r0 + 8, lanes] = re
-        delayed[32 + r0 : 32 + r0 + 8, lanes] = im
-
-    outer_backward(one, 32, tw_ref, store)
-
     copies = []
-    for r0 in range(0, 64, 8):
-        re, im = field[r0 : r0 + 8, :], field[64 + r0 : 64 + r0 + 8, :]
-        late = delayed[r0 : r0 + 8, :]
-        rotation = kerr * ((1.0 - raman_share) * (re * re + im * im) + raman_share * late)
-        c, s = turn(rotation)
-        done[r0 : r0 + 8, :] = re * c - im * s
-        done[64 + r0 : 64 + r0 + 8, :] = re * s + im * c
-        if r0 % 16 == 8:
-            for lo in (r0 - 8, 64 + r0 - 8):
+    for half in range(2):
+        base = 16 * half
+        mine, other = one.at[half], two.at[half]
+
+        def load(side, r0, a):
+            lanes = slice(a * NB, (a + 1) * NB)
+            lo = 32 * side + base + r0
+            re, im = field[lo : lo + 8, lanes], field[64 + lo : 64 + lo + 8, lanes]
+            return re * re + im * im
+
+        outer_forward(load, 16, tw_ref, mine)
+        other[...] = mm_split(mine[...], fwd_ref)
+        filter_spectrum(other, 16, tw_ref[3], tw_ref[4])
+        mine[...] = mm_split(other[...], bwd_ref)
+
+        def store(r0, a, re, im):
+            lanes = slice(a * NB, (a + 1) * NB)
+            delayed[base + r0 : base + r0 + 8, lanes] = re
+            delayed[32 + base + r0 : 32 + base + r0 + 8, lanes] = im
+
+        outer_backward(mine, 16, tw_ref, store)
+
+        for side in range(2):
+            first = 32 * side + base
+            for r0 in (first, first + 8):
+                re, im = field[r0 : r0 + 8, :], field[64 + r0 : 64 + r0 + 8, :]
+                late = delayed[r0 : r0 + 8, :]
+                rotation = kerr * ((1.0 - raman_share) * (re * re + im * im) + raman_share * late)
+                c, s = turn(rotation)
+                done[r0 : r0 + 8, :] = re * c - im * s
+                done[64 + r0 : 64 + r0 + 8, :] = re * s + im * c
+            for lo in (first, 64 + first):
                 rows = pl.ds(lo, 16)
                 copy = pltpu.make_async_copy(done.at[rows], out_ref.at[rows], sems.at[lo // 16])
                 copy.start()
@@ -529,7 +534,7 @@
         in_specs=[VMEM] * 6,
         out_specs=HBM,
         scratch_shapes=[pltpu.VMEM((128, NT), F32), pltpu.VMEM((64, NT), F32)]
-        + [pltpu.VMEM((256, 256), F32)] * 2
+        + [pltpu.VMEM((2, 128, 256), F32)] * 2
         + [pltpu.VMEM((128, NT), F32), pltpu.SemaphoreType.DMA((8,))],
         name="kerr",
     )(

time: 56.4 us -> 56.2 us (level)
  no operation moved by 1% of the time
where the time goes in v13:
time: 56.2 us; the launch traced here: 55.9 us
  blocking collectives  41.6 us (74%)
  Pallas kernels  6.87 us (12%)
  waiting for transfers between devices  5.91 us (11%)
  starting transfers between devices  0.78 us (1%)
  between operations  0.74 us (1%)
    all_to_all x3, blocking collectives, exchange(): lax.all_to_all(value, 'shard', split_axis=0, concat_axis=0, tiled=True)  41.6 us
    ppermute x2, waiting for transfers between devices, pass_on(): lax.ppermute(value, 'blk', [(b, (b + 1) % count) for b in range(count)])  5.91 us
    pallas_call x1, Pallas kernels, per_device(): pl.pallas_call(kerr_kernel, out_shape=jax.ShapeDtypeStruct((128, NT), F32...  1.99 us
    pallas_call x1, Pallas kernels, per_device(): pl.pallas_call(ymode_kernel, out_shape=near(NS, 65, 1, 128), in_specs=[VM...  1.64 us
    pallas_call x1, Pallas kernels, per_device(): pl.pallas_call(lanczos_kernel, out_shape=near(8, 128), in_specs=[VMEM] *...  1.2 us
  transfers between devices with their start and end apart: 2, of which 2 were waited for; matrix products, arithmetic and copies ran while one was open for 0% of the time, Pallas kernels for 4%

profile of v13, /device:TPU:8, one launch (start us, length us, event | category | flops | bytes accessed | tf_op | source)
XLA Modules:
  0.0 55.9 jit_solution(1621974471319088844)
XLA Ops:
  0.7 1.6 %ymode.1 = f32[16,65,1,128]{3,2,1,0:T(1,128)S(1)} custom-call(f32[128,1024]{1,0:T(8,128)} %bitcast.8, bf16[128,384]{1,0:T(8,128)(2,1)} %constant.16.clone.mat_ref, f32[16,128]{1,0:T(8,128)} %constant.20.clone.lam_ref, s32[1,1]{1,0:T(1,128)} %bitcast.7.kind_ref, f32[1,32]{1,0:T(1,128)} %bitcast.9, f32[1,32]{1,0:T(1,128)} %bitcast.10, f32[1,32]{1,0:T(1,128)} %bitcast.11, ...), custom_call_target="tpu_custom_call" | custom-call | tf_op jit(solution)/shard_map/ymode/pallas_call | solution.py:484
  2.3 0.0 copy-start.4
  2.3 17.8 %all_to_all.15.in_ref = f32[16,65,1,128]{3,2,1,0:T(1,128)S(1)} all-to-all(f32[16,65,1,128]{3,2,1,0:T(1,128)S(1)} %ymode.1), channel_id=1, replica_groups=mesh['blk'=32,'shard'=16] {'shard'}, dimensions={0} | all-to-all | bytes 1064960 | tf_op jit(solution)/shard_map/all_to_all | solution.py:471
  20.1 0.0 copy-done.4
  20.1 0.6 %xmode.1 = (f32[136,1024]{1,0:T(8,128)S(1)}, f32[8,128]{1,0:T(8,128)S(1)}, f32[16,1,128]{2,1,0:T(1,128)S(1)}) custom-call(f32[16,65,1,128]{3,2,1,0:T(1,128)S(1)} %all_to_all.15.in_ref, bf16[128,384]{1,0:T(8,128)(2,1)S(1)} %copy-done.4), custom_call_target="tpu_custom_call" | custom-call | tf_op jit(solution)/shard_map/xmode/pallas_call | solution.py:495
  20.7 0.0 collective-permute-start
  20.7 0.0 copy-start.6
  20.7 10.6 %all_to_all.16.weight_ref = f32[16,1,128]{2,1,0:T(1,128)S(1)} all-to-all(f32[16,1,128]{2,1,0:T(1,128)S(1)} %get-tuple-element.10), channel_id=1, replica_groups=mesh['blk'=32,'shard'=16] {'shard'}, dimensions={0} | all-to-all | bytes 16384 | tf_op jit(solution)/shard_map/all_to_all | solution.py:471
  31.4 0.0 copy-done.6
  31.4 0.0 copy-start
  31.4 0.0 copy-start.1
  31.4 0.0 copy-start.5
  31.4 1.2 %lanczos.1 = f32[8,128]{1,0:T(8,128)S(1)} custom-call(f32[8,128]{1,0:T(8,128)S(1)} %get-tuple-element.9.side_ref, f32[16,1,128]{2,1,0:T(1,128)S(1)} %all_to_all.16.weight_ref, f32[16,128]{1,0:T(8,128)S(1)} %copy-done.6), custom_call_target="tpu_custom_call" | custom-call | flops 402653184 | bytes 1048576 | tf_op jit(solution)/shard_map/lanczos/pallas_call | solution.py:504
  32.6 0.0 copy-start.3
  32.6 0.8 %collective-permute-start.1 = (f32[8,128]{1,0:T(8,128)S(1)}, f32[8,128]{1,0:T(8,128)S(1)}, u32[]{:S(2)}, u32[]{:S(2)}) collective-permute-start(f32[8,128]{1,0:T(8,128)S(1)} %lanczos.1), channel_id=1, source_target_pairs={{0,16},{16,32},{32,48},{48,64},{64,80},{80,96},{96,112},{112,128},... | collective-permute-start | bytes 12296 | tf_op jit(solution)/shard_map/ppermute | solution.py:476
  33.4 2.2 %collective-permute-done.modes_ref = f32[136,1024]{1,0:T(8,128)S(1)} collective-permute-done((f32[136,1024]{1,0:T(8,128)S(1)}, f32[136,1024]{1,0:T(8,128)S(1)}, u32[]{:S(2)}, u32[]{:S(2)}) %collective-permute-start) | collective-permute-done | bytes 557088 | tf_op jit(solution)/shard_map/ppermute | solution.py:476
  35.6 0.0 copy-done
  35.6 0.0 copy-done.1
  35.6 0.0 copy-done.5
  35.6 1.0 %disperse.1.modes_ref = f32[128,1024]{1,0:T(8,128)S(1)} custom-call(f32[136,1024]{1,0:T(8,128)S(1)} %collective-permute-done.modes_ref, f32[5,8,128]{2,1,0:T(8,128)S(1)} %copy-done.5, bf16[2,256,256]{2,1,0:T(8,128)(2,1)S(1)} %copy-done.1, bf16[2,256,256]{2,1,0:T(8,128)(2,1)S(1)} %copy-done), custom_call_target="tpu_custom_call" | custom-call | flops 805306368 | bytes 1048576 | tf_op jit(solution)/shard_map/disperse/pallas_call | solution.py:513
  36.6 3.7 %collective-permute-done.1.factor_ref = f32[8,128]{1,0:T(8,128)S(1)} collective-permute-done((f32[8,128]{1,0:T(8,128)S(1)}, f32[8,128]{1,0:T(8,128)S(1)}, u32[]{:S(2)}, u32[]{:S(2)}) %collective-permute-start.1) | collective-permute-done | bytes 4128 | tf_op jit(solution)/shard_map/ppermute | solution.py:476
  40.3 0.0 copy-done.3
  40.3 0.4 propagate.1
  40.7 0.0 copy-start.2
  40.7 13.2 %all_to_all.17.in_ref = f32[16,8,1024]{2,1,0:T(8,128)S(1)} all-to-all(f32[16,8,1024]{2,1,0:T(8,128)S(1)} %propagate.1), channel_id=1, replica_groups=mesh['blk'=32,'shard'=16] {'shard'}, dimensions={0} | all-to-all | bytes 1048576 | tf_op jit(solution)/shard_map/all_to_all | solution.py:471
  54.0 0.0 copy-done.2
  54.0 2.0 %kerr.1 = f32[128,1024]{1,0:T(8,128)} custom-call(f32[136,1024]{1,0:T(8,128)S(1)} %collective-permute-done.modes_ref, f32[16,8,1024]{2,1,0:T(8,128)S(1)} %all_to_all.17.in_ref, bf16[128,384]{1,0:T(8,128)(2,1)S(1)} %copy-done.2, f32[5,8,128]{2,1,0:T(8,128)S(1)} %copy-done.5, bf16[2,256,256]{2,1,0:T(8,128)(2,1)S(1)} %copy-done.1, bf16[2,256,256]{2,1,0:T(8,128)(2,1)S(1)} %copy-done), custom_call_target="tpu_custom_call" | custom-call | tf_op jit(solution)/shard_map/kerr/pallas_call | solution.py:531
Async XLA Ops:
  2.3 17.8 %copy-start.4 = (bf16[128,384]{1,0:T(8,128)(2,1)S(1)}, bf16[128,384]{1,0:T(8,128)(2,1)}, u32[]{:S(2)}) copy-start(bf16[128,384]{1,0:T(8,128)(2,1)} %constant.18.clone.mat_ref) | copy-start | bytes 294916
  20.7 14.9 %collective-permute-start = (f32[136,1024]{1,0:T(8,128)S(1)}, f32[136,1024]{1,0:T(8,128)S(1)}, u32[]{:S(2)}, u32[]{:S(2)}) collective-permute-start(f32[136,1024]{1,0:T(8,128)S(1)} %get-tuple-element.8), channel_id=1, source_target_pairs={{0,16},{16,32},{32,48},{48,64},{64,80},{80,96},{96,112},{112,128},... | collective-permute-start | bytes 1671176 | tf_op jit(solution)/shard_map/ppermute | solution.py:476
  20.7 10.7 %copy-start.6 = (f32[16,128]{1,0:T(8,128)S(1)}, f32[16,128]{1,0:T(8,128)}, u32[]{:S(2)}) copy-start(f32[16,128]{1,0:T(8,128)} %constant.20.clone.lam_ref) | copy-start | bytes 24580
  31.4 4.2 %copy-start = (bf16[2,256,256]{2,1,0:T(8,128)(2,1)S(1)}, bf16[2,256,256]{2,1,0:T(8,128)(2,1)}, u32[]{:S(2)}) copy-start(bf16[2,256,256]{2,1,0:T(8,128)(2,1)} %constant.22.clone.bwd_ref) | copy-start | bytes 786436
  31.4 4.2 %copy-start.1 = (bf16[2,256,256]{2,1,0:T(8,128)(2,1)S(1)}, bf16[2,256,256]{2,1,0:T(8,128)(2,1)}, u32[]{:S(2)}) copy-start(bf16[2,256,256]{2,1,0:T(8,128)(2,1)} %constant.21.clone.fwd_ref) | copy-start | bytes 786436
  31.4 4.2 %copy-start.5 = (f32[5,8,128]{2,1,0:T(8,128)S(1)}, f32[5,8,128]{2,1,0:T(8,128)}, u32[]{:S(2)}) copy-start(f32[5,8,128]{2,1,0:T(8,128)} %constant.23.clone.tw_ref) | copy-start | bytes 61444
  32.6 7.7 %copy-start.3 = (bf16[128,384]{1,0:T(8,128)(2,1)S(1)}, bf16[128,384]{1,0:T(8,128)(2,1)}, u32[]{:S(2)}) copy-start(bf16[128,384]{1,0:T(8,128)(2,1)} %constant.19.clone.mat_ref) | copy-start | bytes 294916
  32.6 7.7 %collective-permute-start.1 = (f32[8,128]{1,0:T(8,128)S(1)}, f32[8,128]{1,0:T(8,128)S(1)}, u32[]{:S(2)}, u32[]{:S(2)}) collective-permute-start(f32[8,128]{1,0:T(8,128)S(1)} %lanczos.1), channel_id=1, source_target_pairs={{0,16},{16,32},{32,48},{48,64},{64,80},{80,96},{96,112},{112,128},... | collective-permute-start | bytes 12296 | tf_op jit(solution)/shard_map/ppermute | solution.py:476
  40.7 13.2 %copy-start.2 = (bf16[128,384]{1,0:T(8,128)(2,1)S(1)}, bf16[128,384]{1,0:T(8,128)(2,1)}, u32[]{:S(2)}) copy-start(bf16[128,384]{1,0:T(8,128)(2,1)} %constant.17.clone.mat_ref) | copy-start | bytes 294916

commit v14 on v13

--- a/solution.py
+++ b/solution.py
@@ -197,11 +197,12 @@
 
 
 def ymode_kernel(
-    seed_ref, mat_ref, lam_ref, kind_ref, disp_ref, gain_ref, sat_ref, kerr_ref, out_ref
+    upper_ref, lower_ref, mat_ref, lam_ref, kind_ref, disp_ref, gain_ref, sat_ref, kerr_ref, out_ref
 ):
     total = jnp.zeros((8, 128), F32)
     for c0 in range(0, NK, WIDE):
-        block = seed_ref[:, c0 * 128 : (c0 + WIDE) * 128]
+        lanes = slice(c0 * 128, (c0 + WIDE) * 128)
+        block = jnp.concatenate([upper_ref[:, lanes], lower_ref[:, lanes]], axis=0)
         square = block * block
         modes = mm_wide(mat_ref[...], block)
         for c in range(WIDE):
@@ -484,11 +485,13 @@
     ymodes = pl.pallas_call(
         ymode_kernel,
         out_shape=near(NS, 65, 1, 128),
-        in_specs=[VMEM] * 8,
+        grid=(1,),
+        in_specs=[pl.BlockSpec((64, NT), lambda i: (0, 0)), pl.BlockSpec((64, NT), lambda i: (1, 0))]
+        + [VMEM] * 7,
         out_specs=VMEM,
         name="ymode",
     )(
-        seed, t["to_ymode"], t["lam_all"], segment_order.reshape(1, 1),
+        seed, seed, t["to_ymode"], t["lam_all"], segment_order.reshape(1, 1),
         *(each.reshape(1, 32) for each in (seg_disp, seg_gain, seg_sat, seg_kerr)),
     )
     gathered = exchange(ymodes)

time: 56.2 us -> 56.2 us (level)
  no operation moved by 1% of the time
where the time goes in v14:
time: 56.2 us; the launch traced here: 55.9 us
  blocking collectives  41.6 us (74%)
  Pallas kernels  6.81 us (12%)
  waiting for transfers between devices  5.9 us (10%)
  starting transfers between devices  0.77 us (1%)
  between operations  0.74 us (1%)
    all_to_all x3, blocking collectives, exchange(): lax.all_to_all(value, 'shard', split_axis=0, concat_axis=0, tiled=True)  41.6 us
    ppermute x2, waiting for transfers between devices, pass_on(): lax.ppermute(value, 'blk', [(b, (b + 1) % count) for b in range(count)])  5.9 us
    pallas_call x1, Pallas kernels, per_device(): pl.pallas_call(kerr_kernel, out_shape=jax.ShapeDtypeStruct((128, NT), F32...  1.99 us
    pallas_call x1, Pallas kernels, per_device(): pl.pallas_call(ymode_kernel, out_shape=near(NS, 65, 1, 128), grid=(1,), i...  1.59 us
    pallas_call x1, Pallas kernels, per_device(): pl.pallas_call(lanczos_kernel, out_shape=near(8, 128), in_specs=[VMEM] *...  1.2 us
  transfers between devices with their start and end apart: 2, of which 2 were waited for; matrix products, arithmetic and copies ran while one was open for 0% of the time, Pallas kernels for 4%

profile of v14, /device:TPU:8, one launch (start us, length us, event | category | flops | bytes accessed | tf_op | source)
XLA Modules:
  0.0 55.9 jit_solution(15051361042092488965)
XLA Ops:
  0.7 1.6 %ymode.1 = f32[16,65,1,128]{3,2,1,0:T(1,128)S(1)} custom-call(f32[128,1024]{1,0:T(8,128)} %bitcast.8, f32[128,1024]{1,0:T(8,128)} %bitcast.9, bf16[128,384]{1,0:T(8,128)(2,1)} %constant.16.clone.mat_ref, f32[16,128]{1,0:T(8,128)} %constant.20.clone.lam_ref, s32[1,1]{1,0:T(1,128)} %bitcast.7.kind_ref, f32[1,32]{1,0:T(1,128)} %bitcast.10, f32[1,32]{1,0:T(1,128)} %bitcast.11, ...), custom_call_target="tpu_custom_call" | custom-call | tf_op jit(solution)/shard_map/ymode/pallas_call | solution.py:485
  2.2 0.0 copy-start.4
  2.3 17.8 %all_to_all.15.in_ref = f32[16,65,1,128]{3,2,1,0:T(1,128)S(1)} all-to-all(f32[16,65,1,128]{3,2,1,0:T(1,128)S(1)} %ymode.1), channel_id=1, replica_groups=mesh['blk'=32,'shard'=16] {'shard'}, dimensions={0} | all-to-all | bytes 1064960 | tf_op jit(solution)/shard_map/all_to_all | solution.py:472
  20.0 0.0 copy-done.4
  20.0 0.6 %xmode.1 = (f32[136,1024]{1,0:T(8,128)S(1)}, f32[8,128]{1,0:T(8,128)S(1)}, f32[16,1,128]{2,1,0:T(1,128)S(1)}) custom-call(f32[16,65,1,128]{3,2,1,0:T(1,128)S(1)} %all_to_all.15.in_ref, bf16[128,384]{1,0:T(8,128)(2,1)S(1)} %copy-done.4), custom_call_target="tpu_custom_call" | custom-call | tf_op jit(solution)/shard_map/xmode/pallas_call | solution.py:498
  20.6 0.0 collective-permute-start
  20.7 0.0 copy-start.6
  20.7 10.6 %all_to_all.16.weight_ref = f32[16,1,128]{2,1,0:T(1,128)S(1)} all-to-all(f32[16,1,128]{2,1,0:T(1,128)S(1)} %get-tuple-element.10), channel_id=1, replica_groups=mesh['blk'=32,'shard'=16] {'shard'}, dimensions={0} | all-to-all | bytes 16384 | tf_op jit(solution)/shard_map/all_to_all | solution.py:472
  31.3 0.0 copy-done.6
  31.3 0.0 copy-start
  31.3 0.0 copy-start.1
  31.3 0.0 copy-start.5
  31.3 1.2 %lanczos.1 = f32[8,128]{1,0:T(8,128)S(1)} custom-call(f32[8,128]{1,0:T(8,128)S(1)} %get-tuple-element.9.side_ref, f32[16,1,128]{2,1,0:T(1,128)S(1)} %all_to_all.16.weight_ref, f32[16,128]{1,0:T(8,128)S(1)} %copy-done.6), custom_call_target="tpu_custom_call" | custom-call | flops 402653184 | bytes 1048576 | tf_op jit(solution)/shard_map/lanczos/pallas_call | solution.py:507
  32.5 0.0 copy-start.3
  32.6 0.8 %collective-permute-start.1 = (f32[8,128]{1,0:T(8,128)S(1)}, f32[8,128]{1,0:T(8,128)S(1)}, u32[]{:S(2)}, u32[]{:S(2)}) collective-permute-start(f32[8,128]{1,0:T(8,128)S(1)} %lanczos.1), channel_id=1, source_target_pairs={{0,16},{16,32},{32,48},{48,64},{64,80},{80,96},{96,112},{112,128},... | collective-permute-start | bytes 12296 | tf_op jit(solution)/shard_map/ppermute | solution.py:477
  33.3 2.2 %collective-permute-done.modes_ref = f32[136,1024]{1,0:T(8,128)S(1)} collective-permute-done((f32[136,1024]{1,0:T(8,128)S(1)}, f32[136,1024]{1,0:T(8,128)S(1)}, u32[]{:S(2)}, u32[]{:S(2)}) %collective-permute-start) | collective-permute-done | bytes 557088 | tf_op jit(solution)/shard_map/ppermute | solution.py:477
  35.5 0.0 copy-done
  35.5 0.0 copy-done.1
  35.5 0.0 copy-done.5
  35.5 1.0 %disperse.1.modes_ref = f32[128,1024]{1,0:T(8,128)S(1)} custom-call(f32[136,1024]{1,0:T(8,128)S(1)} %collective-permute-done.modes_ref, f32[5,8,128]{2,1,0:T(8,128)S(1)} %copy-done.5, bf16[2,256,256]{2,1,0:T(8,128)(2,1)S(1)} %copy-done.1, bf16[2,256,256]{2,1,0:T(8,128)(2,1)S(1)} %copy-done), custom_call_target="tpu_custom_call" | custom-call | flops 805306368 | bytes 1048576 | tf_op jit(solution)/shard_map/disperse/pallas_call | solution.py:516
  36.6 3.7 %collective-permute-done.1.factor_ref = f32[8,128]{1,0:T(8,128)S(1)} collective-permute-done((f32[8,128]{1,0:T(8,128)S(1)}, f32[8,128]{1,0:T(8,128)S(1)}, u32[]{:S(2)}, u32[]{:S(2)}) %collective-permute-start.1) | collective-permute-done | bytes 4128 | tf_op jit(solution)/shard_map/ppermute | solution.py:477
  40.3 0.0 copy-done.3
  40.3 0.4 propagate.1
  40.7 0.0 copy-start.2
  40.7 13.2 %all_to_all.17.in_ref = f32[16,8,1024]{2,1,0:T(8,128)S(1)} all-to-all(f32[16,8,1024]{2,1,0:T(8,128)S(1)} %propagate.1), channel_id=1, replica_groups=mesh['blk'=32,'shard'=16] {'shard'}, dimensions={0} | all-to-all | bytes 1048576 | tf_op jit(solution)/shard_map/all_to_all | solution.py:472
  53.9 0.0 copy-done.2
  53.9 2.0 %kerr.1 = f32[128,1024]{1,0:T(8,128)} custom-call(f32[136,1024]{1,0:T(8,128)S(1)} %collective-permute-done.modes_ref, f32[16,8,1024]{2,1,0:T(8,128)S(1)} %all_to_all.17.in_ref, bf16[128,384]{1,0:T(8,128)(2,1)S(1)} %copy-done.2, f32[5,8,128]{2,1,0:T(8,128)S(1)} %copy-done.5, bf16[2,256,256]{2,1,0:T(8,128)(2,1)S(1)} %copy-done.1, bf16[2,256,256]{2,1,0:T(8,128)(2,1)S(1)} %copy-done), custom_call_target="tpu_custom_call" | custom-call | tf_op jit(solution)/shard_map/kerr/pallas_call | solution.py:534
Async XLA Ops:
  2.2 17.8 %copy-start.4 = (bf16[128,384]{1,0:T(8,128)(2,1)S(1)}, bf16[128,384]{1,0:T(8,128)(2,1)}, u32[]{:S(2)}) copy-start(bf16[128,384]{1,0:T(8,128)(2,1)} %constant.18.clone.mat_ref) | copy-start | bytes 294916
  20.6 14.9 %collective-permute-start = (f32[136,1024]{1,0:T(8,128)S(1)}, f32[136,1024]{1,0:T(8,128)S(1)}, u32[]{:S(2)}, u32[]{:S(2)}) collective-permute-start(f32[136,1024]{1,0:T(8,128)S(1)} %get-tuple-element.8), channel_id=1, source_target_pairs={{0,16},{16,32},{32,48},{48,64},{64,80},{80,96},{96,112},{112,128},... | collective-permute-start | bytes 1671176 | tf_op jit(solution)/shard_map/ppermute | solution.py:477
  20.7 10.7 %copy-start.6 = (f32[16,128]{1,0:T(8,128)S(1)}, f32[16,128]{1,0:T(8,128)}, u32[]{:S(2)}) copy-start(f32[16,128]{1,0:T(8,128)} %constant.20.clone.lam_ref) | copy-start | bytes 24580
  31.3 4.2 %copy-start = (bf16[2,256,256]{2,1,0:T(8,128)(2,1)S(1)}, bf16[2,256,256]{2,1,0:T(8,128)(2,1)}, u32[]{:S(2)}) copy-start(bf16[2,256,256]{2,1,0:T(8,128)(2,1)} %constant.22.clone.bwd_ref) | copy-start | bytes 786436
  31.3 4.2 %copy-start.1 = (bf16[2,256,256]{2,1,0:T(8,128)(2,1)S(1)}, bf16[2,256,256]{2,1,0:T(8,128)(2,1)}, u32[]{:S(2)}) copy-start(bf16[2,256,256]{2,1,0:T(8,128)(2,1)} %constant.21.clone.fwd_ref) | copy-start | bytes 786436
  31.3 4.2 %copy-start.5 = (f32[5,8,128]{2,1,0:T(8,128)S(1)}, f32[5,8,128]{2,1,0:T(8,128)}, u32[]{:S(2)}) copy-start(f32[5,8,128]{2,1,0:T(8,128)} %constant.23.clone.tw_ref) | copy-start | bytes 61444
  32.5 7.7 %copy-start.3 = (bf16[128,384]{1,0:T(8,128)(2,1)S(1)}, bf16[128,384]{1,0:T(8,128)(2,1)}, u32[]{:S(2)}) copy-start(bf16[128,384]{1,0:T(8,128)(2,1)} %constant.19.clone.mat_ref) | copy-start | bytes 294916
  32.6 7.7 %collective-permute-start.1 = (f32[8,128]{1,0:T(8,128)S(1)}, f32[8,128]{1,0:T(8,128)S(1)}, u32[]{:S(2)}, u32[]{:S(2)}) collective-permute-start(f32[8,128]{1,0:T(8,128)S(1)} %lanczos.1), channel_id=1, source_target_pairs={{0,16},{16,32},{32,48},{48,64},{64,80},{80,96},{96,112},{112,128},... | collective-permute-start | bytes 12296 | tf_op jit(solution)/shard_map/ppermute | solution.py:477
  40.7 13.2 %copy-start.2 = (bf16[128,384]{1,0:T(8,128)(2,1)S(1)}, bf16[128,384]{1,0:T(8,128)(2,1)}, u32[]{:S(2)}) copy-start(bf16[128,384]{1,0:T(8,128)(2,1)} %constant.17.clone.mat_ref) | copy-start | bytes 294916
